TPU v7x, 768 devices: a whole 4x8x12 slice. The times are simulated.
768 devices in a mesh: seq: 12 (over z), head: 64 (over y, x, core).
Axes of the slice: x: 4, y: 8, z: 12, core: 2. Of those that a mesh axis runs over, the one named last changes fastest.
Arguments:
- tokens: bfloat16 [6144, 4096], P('seq', 'head'), may hold values from -24 to 24
- query_weight: bfloat16 [4096, 4096], P('head'), may hold values from -3 to 3
- key_weight: bfloat16 [1024, 4096], P('head'), may hold values from -3 to 3
- value_weight: bfloat16 [1024, 4096], P('head'), may hold values from -0.09375 to 0.09375
- output_weight: bfloat16 [4096, 4096], P('head'), may hold values from -1 to 1
- segments: int32 [6144], replicated, may hold values from 0 to 23, never falling along the last dimension, each value on 1 to 4608 neighbouring positions
Outputs:
- attention_out: bfloat16 [6144, 4096], P('seq', 'head')
All inputs are finite; a program needn't handle non-finite values.
Results may differ from a plain program's by a relative error of at most 0.011.
Values may be sent and summed in bfloat16 or wider, within the bound.
No kernel may reach another device: no remote copies, remote signals or barrier semaphores. Data moves between devices by JAX's collectives and lax.ppermute only.
A program may use at most 32 MiB of HBM per device.

v0:
```python
import math

import jax
import jax.numpy as jnp
from jax import lax
from jax.sharding import PartitionSpec as P

HEADS = 32
KV_HEADS = 8
HEAD_DIM = 128
BLOCK = 128


def swapped(block, axis, apart):
    count = lax.axis_size(axis)
    route = []
    for low in range(count):
        high = low | 1 << apart
        if high != low and high < count:
            route += [(low, high), (high, low)]
    return lax.ppermute(block, axis, route)


def trade_partner(block, bit):
    return swapped(block, "head", bit)


def collect(block, place, bit_list, dim):
    for bit in bit_list:
        flag = place >> bit & 1
        other = trade_partner(block, bit)
        block = jnp.where(
            flag == 0, jnp.concatenate([block, other], dim), jnp.concatenate([other, block], dim)
        )
    return block


def local(tokens, query_weight, key_weight, value_weight, output_weight, segments):
    n_head = lax.axis_size("head")
    split = max(1, 2 * n_head // HEADS)
    groups = n_head // split
    pair_span = n_head // KV_HEADS
    place = lax.axis_index("head")
    seq_place = lax.axis_index("seq")
    local_rows = tokens.shape[0]
    local_cols = tokens.shape[1]
    section = local_rows // split
    piece = section // groups
    split_bits = list(range(split.bit_length() - 1))
    group_bits = list(range(split.bit_length() - 1, n_head.bit_length() - 1))
    span_bits = list(range(pair_span.bit_length() - 1))
    ordered = (
        tokens.reshape(split, groups, piece, local_cols)
        .transpose(1, 0, 2, 3)
        .reshape(n_head * piece, local_cols)
    )
    arrived = lax.all_to_all(ordered, "head", split_axis=0, concat_axis=1, tiled=True)
    rows_here = collect(arrived, place, group_bits, 0)
    head_rows = collect(jnp.stack([query_weight, output_weight]), place, split_bits, 1)
    pair_rows = collect(jnp.stack([key_weight, value_weight]), place, span_bits, 1)
    queries = lax.dot_general(
        rows_here, head_rows[0], (((1,), (1,)), ((), ())), preferred_element_type=jnp.float32
    ).astype(jnp.bfloat16)
    memory_local = jnp.einsum(
        "khd,rd->khr", pair_rows, rows_here, preferred_element_type=jnp.float32
    ).astype(jnp.bfloat16)
    spread = lax.all_gather(memory_local[:, :, None, :], "seq", axis=2, tiled=True)
    memory_all = collect(spread, place, split_bits, 3).reshape(2, HEAD_DIM, -1)
    head_dim = HEAD_DIM
    heads_here = queries.shape[1] // head_dim
    first_row = seq_place * local_rows + place % split * section
    query_position = first_row + lax.iota(jnp.int32, section)
    query_segment = lax.dynamic_slice_in_dim(segments, first_row, section, 0)
    doc_start = jnp.sum((segments < query_segment[0]).astype(jnp.int32))
    first_tile = doc_start // BLOCK
    last_tile = (first_row + section - 1) // BLOCK
    grouped = queries.reshape(section, 1, heads_here, head_dim)
    scale = 1.0 / math.sqrt(head_dim)
    key_rows = memory_all[0]
    value_rows = memory_all[1]

    def visit_tile(tile, carry):
        highest, totals, accum = carry
        begin = tile * BLOCK
        key_tile = lax.dynamic_slice_in_dim(key_rows, begin, BLOCK, 1).reshape(1, head_dim, BLOCK)
        value_tile = lax.dynamic_slice_in_dim(value_rows, begin, BLOCK, 1).reshape(
            1, head_dim, BLOCK
        )
        key_segment = lax.dynamic_slice_in_dim(segments, begin, BLOCK, 0)
        key_position = begin + lax.iota(jnp.int32, BLOCK)
        allowed = (query_segment[:, None] == key_segment[None, :]) & (
            key_position[None, :] <= query_position[:, None]
        )
        scores = (
            jnp.einsum("rkgd,kdb->kgrb", grouped, key_tile, preferred_element_type=jnp.float32)
            * scale
        )
        scores = jnp.where(allowed, scores, -1e30)
        new_highest = jnp.maximum(highest, jnp.max(scores, axis=3))
        shrink = jnp.exp(highest - new_highest)
        powers = jnp.where(allowed, jnp.exp(scores - new_highest[..., None]), 0.0)
        totals = totals * shrink + jnp.sum(powers, axis=3)
        update = jnp.einsum(
            "kgrb,kdb->kgrd",
            powers.astype(jnp.bfloat16),
            value_tile,
            preferred_element_type=jnp.float32,
        )
        accum = accum * shrink[..., None] + update
        return (new_highest, totals, accum)

    start_high = jnp.full((1, heads_here, section), -1e30, jnp.float32)
    start_total = jnp.zeros((1, heads_here, section), jnp.float32)
    start_accum = jnp.zeros((1, heads_here, section, head_dim), jnp.float32)
    highest, totals, accum = lax.fori_loop(
        first_tile, last_tile + 1, visit_tile, (start_high, start_total, start_accum)
    )
    attended = (
        (accum / totals[..., None])
        .transpose(2, 0, 1, 3)
        .reshape(section, heads_here * head_dim)
        .astype(jnp.bfloat16)
    )
    pairs_here = heads_here // 2
    partial_value = jnp.einsum(
        "rpk,pkd->prd",
        attended.reshape(section, pairs_here, 2 * head_dim),
        head_rows[1].reshape(pairs_here, 2 * head_dim, -1),
        preferred_element_type=jnp.float32,
    ).astype(jnp.bfloat16)
    returned = lax.all_to_all(partial_value, "head", split_axis=2, concat_axis=0, tiled=True)
    summed = (
        returned.astype(jnp.float32)
        .reshape(groups, split, pairs_here, section, -1)
        .sum(axis=(0, 2))
    )
    return summed.reshape(split * section, -1).astype(jnp.bfloat16)


def solution(mesh):
    placed = (
        P("seq", "head"),
        P("head", None),
        P("head", None),
        P("head", None),
        P("head", None),
        P(),
    )
    return jax.shard_map(
        local, mesh=mesh, in_specs=placed, out_specs=P("seq", "head"), check_vma=False
    )
```

profile of v0, /device:TPU:704, one launch (start us, length us, event | category | flops | bytes accessed | tf_op | source)
XLA Modules:
  0.0 256.7 jit_solution(2213398118976903453)
XLA Ops:
  1.3 20.4 %all_to_all.28 = bf16[64,2,256]{2,1,0:T(2,128)(2,1)S(1)} all-to-all(bf16[64,2,256]{2,1,0:T(2,128)(2,1)S(1)} %reshape.88), channel_id=1, replica_groups=mesh['seq'=12,'head'=64] {'head'}, dimensions={0} | all-to-all | bytes 131072 | tf_op jit(solution)/shard_map/all_to_all | solution.py:57
  22.0 3.1 %collective-permute-start.3 = (bf16[8,4096]{1,0:T(8,128)(2,1)S(1)}, bf16[8,4096]{1,0:T(8,128)(2,1)S(1)}, u32[]{:S(2)}, u32[]{:S(2)}) collective-permute-start(bf16[8,4096]{1,0:T(8,128)(2,1)S(1)} %all_to_all.24), channel_id=1, source_target_pairs={{0,4},{4,0},{1,5},{5,1},{2,6},{6,2},{3,7},{7,3},{8,12},{12,8},{9,1... | collective-permute-start | bytes 196616 | tf_op jit(solution)/shard_map/ppermute | solution.py:21
  26.2 1.9 collective-permute-start
  28.1 1.6 collective-permute-done.3
  29.7 2.5 collective-permute-start.4
  32.4 2.5 collective-permute-start.1
  35.1 1.9 collective-permute-start.9
  37.1 2.6 %collective-permute-start.5 = (bf16[32,4096]{1,0:T(8,128)(2,1)S(1)}, bf16[32,4096]{1,0:T(8,128)(2,1)S(1)}, u32[]{:S(2)}, u32[]{:S(2)}) collective-permute-start(bf16[32,4096]{1,0:T(8,128)(2,1)S(1)} %maximum_select_fusion.12), channel_id=1, source_target_pairs={{0,16},{16,0},{1,17},{17,1},{2,18},{18,2},{3,19},{19,3},{4,20},{20... | collective-permute-start | bytes 786440 | tf_op jit(solution)/shard_map/ppermute | solution.py:21
  39.7 7.3 %collective-permute-done.1 = bf16[2,32,4096]{2,1,0:T(8,128)(2,1)} collective-permute-done((bf16[2,32,4096]{2,1,0:T(8,128)(2,1)S(1)}, bf16[2,32,4096]{2,1,0:T(8,128)(2,1)}, u32[]{:S(2)}, u32[]{:S(2)}) %collective-permute-start.1) | collective-permute-done | bytes 524320 | tf_op jit(solution)/shard_map/ppermute | solution.py:21
  47.0 2.4 maximum_select_fusion.8
  49.4 4.1 %collective-permute-start.2 = (bf16[2,64,4096]{2,1,0:T(8,128)(2,1)}, bf16[2,64,4096]{2,1,0:T(8,128)(2,1)}, u32[]{:S(2)}, u32[]{:S(2)}) collective-permute-start(bf16[2,64,4096]{2,1,0:T(8,128)(2,1)} %maximum_select_fusion.8), channel_id=1, source_target_pairs={{0,4},{4,0},{1,5},{5,1},{2,6},{6,2},{3,7},{7,3},{8,12},{12,8},{9,1... | collective-permute-start | bytes 3145736 | tf_op jit(solution)/shard_map/ppermute | solution.py:21
  55.1 3.2 %collective-permute-start.6 = (bf16[64,4096]{1,0:T(8,128)(2,1)}, bf16[64,4096]{1,0:T(8,128)(2,1)}, u32[]{:S(2)}, u32[]{:S(2)}) collective-permute-start(bf16[64,4096]{1,0:T(8,128)(2,1)} %maximum_select_fusion.11), channel_id=1, source_target_pairs={{0,32},{32,0},{1,33},{33,1},{2,34},{34,2},{3,35},{35,3},{4,36},{36... | collective-permute-start | bytes 1572872 | tf_op jit(solution)/shard_map/ppermute | solution.py:21
  58.3 2.1 maximum_select_fusion.4
  60.4 3.4 %collective-permute-start.10 = (bf16[2,128,4096]{2,1,0:T(8,128)(2,1)S(1)}, bf16[2,128,4096]{2,1,0:T(8,128)(2,1)}, u32[]{:S(2)}, u32[]{:S(2)}) collective-permute-start(bf16[2,128,4096]{2,1,0:T(8,128)(2,1)S(1)} %maximum_select_fusion.4), channel_id=1, source_target_pairs={{0,2},{2,0},{1,3},{3,1},{4,6},{6,4},{5,7},{7,5},{8,10},{10,8},{9,1... | collective-permute-start | bytes 6291464 | tf_op jit(solution)/shard_map/ppermute | solution.py:21
  63.8 21.2 %collective-permute-done.6 = bf16[64,4096]{1,0:T(8,128)(2,1)} collective-permute-done((bf16[64,4096]{1,0:T(8,128)(2,1)}, bf16[64,4096]{1,0:T(8,128)(2,1)}, u32[]{:S(2)}, u32[]{:S(2)}) %collective-permute-start.6) | collective-permute-done | bytes 524320 | tf_op jit(solution)/shard_map/ppermute | solution.py:21
  85.1 3.7 %fusion.31 = bf16[2,128,128]{2,1,0:T(8,128)(2,1)S(1)} fusion(bf16[2,64,4096]{2,1,0:T(8,128)(2,1)} %collective-permute-done.2, bf16[2,64,4096]{2,1,0:T(8,128)(2,1)} %maximum_select_fusion.8, pred[]{:T(512)S(6)} %eq.40, bf16[64,4096]{1,0:T(8,128)(2,1)} %collective-permute-done.6, bf16[64,4096]{1,0:T(8,128)(2,1)} %maximum_select_fusion.11, pred[]{:T(512)S(6)} %eq.41), kind=kOutput, calls=%fused_computation.46 | convolution fusion | flops 282624000 | bytes 3211266 | tf_op jit(solution)/shard_map/khd,rd->khr/dot_general | solution.py:64
  88.8 24.1 %all-gather = bf16[2,128,1536]{2,1,0:T(8,128)(2,1)S(1)} all-gather(bf16[2,128,128]{2,1,0:T(8,128)(2,1)S(1)} %fusion.31), channel_id=2, replica_groups=mesh['seq'=12,'head'=64] {'seq'}, dimensions={2}, use_global_device_ids=true | all-gather | bytes 851968 | tf_op jit(solution)/shard_map/all_gather | solution.py:67
  112.9 1.1 copy.40
  114.1 1.9 collective-permute-start.7
  116.0 2.5 collective-permute-done.7
  118.4 3.0 %maximum_select_fusion.5 = bf16[2,128,12,256]{1,3,2,0:T(8,128)(2,1)} fusion(bf16[2,128,12,128]{1,3,2,0:T(8,128)(2,1)S(1)} %collective-permute-done.7, bf16[2,128,12,128]{1,3,2,0:T(8,128)(2,1)} %bitcast.99, pred[]{:T(512)S(6)} %eq.39), kind=kLoop, calls=%fused_computation.44 | loop fusion | flops 7077888 | bytes 3145729 | tf_op jit(solution)/shard_map/jit(_where)/select_n | solution.py:32
  121.5 2.6 %collective-permute-start.8 = (bf16[2,128,12,256]{1,3,2,0:T(8,128)(2,1)}, bf16[2,128,12,256]{1,3,2,0:T(8,128)(2,1)}, u32[]{:S(2)}, u32[]{:S(2)}) collective-permute-start(bf16[2,128,12,256]{1,3,2,0:T(8,128)(2,1)} %maximum_select_fusion.5), channel_id=1, source_target_pairs={{0,2},{2,0},{1,3},{3,1},{4,6},{6,4},{5,7},{7,5},{8,10},{10,8},{9,1... | collective-permute-start | bytes 4718600 | tf_op jit(solution)/shard_map/ppermute | solution.py:21
  127.8 3.8 %maximum_select_fusion = bf16[2,256,4096]{2,1,0:T(8,128)(2,1)S(1)} fusion(bf16[2,128,4096]{2,1,0:T(8,128)(2,1)} %collective-permute-done.10, bf16[2,128,4096]{2,1,0:T(8,128)(2,1)S(1)} %maximum_select_fusion.4, pred[]{:T(512)S(6)} %eq.38), kind=kLoop, calls=%fused_computation.30 | loop fusion | flops 18874368 | bytes 8388609 | tf_op jit(solution)/shard_map/jit(_where)/select_n | solution.py:32
  131.6 1.9 copy-done
  133.5 2.5 fusion.30
  136.0 24.1 %collective-permute-done.8 = bf16[2,128,12,256]{1,3,2,0:T(8,128)(2,1)} collective-permute-done((bf16[2,128,12,256]{1,3,2,0:T(8,128)(2,1)}, bf16[2,128,12,256]{1,3,2,0:T(8,128)(2,1)}, u32[]{:S(2)}, u32[]{:S(2)}) %collective-permute-start.8) | collective-permute-done | bytes 1572896 | tf_op jit(solution)/shard_map/ppermute | solution.py:21
  160.1 3.9 %maximum_select_fusion.1 = bf16[2,128,12,512]{1,3,2,0:T(8,128)(2,1)S(1)} fusion(bf16[2,128,12,256]{1,3,2,0:T(8,128)(2,1)} %collective-permute-done.8, bf16[2,128,12,256]{1,3,2,0:T(8,128)(2,1)} %maximum_select_fusion.5, pred[]{:T(512)S(6)} %eq.38), kind=kLoop, calls=%fused_computation.31 | loop fusion | flops 14155776 | bytes 6291457 | tf_op jit(solution)/shard_map/jit(_where)/select_n | solution.py:32
  164.3 26.1 %while.15 = (s32[]{:T(128)}, f32[1,2,128]{2,1,0:T(2,128)S(1)}, f32[1,2,128]{2,1,0:T(2,128)S(1)}, f32[1,2,128,128]{3,2,1,0:T(8,128)S(1)}, s32[]{:T(128)}, /*index...) while((s32[]{:T(128)}, f32[1,2,128]{2,1,0:T(2,128)S(1)}, ...), condition=%wide.region_4.5_spmd.clone, body=%wide.region_1.4_spmd.clone.sunk | while | flops 17187844 | bytes 872655 | solution.py:115
  190.6 2.1 fusion.21
  192.7 2.8 %copy.44 = bf16[1,128,4096]{1,0,2:T(2,128)(2,1)S(1)} copy(bf16[1,128,4096]{2,1,0:T(8,128)(2,1)S(1)} %fusion.21) | data formatting | bytes 2097152 | tf_op jit(solution)/shard_map/convert_element_type | solution.py:130
  196.0 22.4 %reduce.4 = bf16[4096,128]{1,0:T(8,128)(2,1)S(1)} reduce(bf16[4096,1,128]{2,1,0:T(2,128)(2,1)S(1)} %bitcast.96, bf16[]{:T(256)} %broadcast.22), dimensions={1}, to_apply=%bitcast.68.reduce_sub_computation | reduce | bytes 2097154
  218.7 35.9 %all_to_all.29 = bf16[64,2,4096]{2,1,0:T(2,128)(2,1)S(1)} all-to-all(bf16[64,2,4096]{2,1,0:T(2,128)(2,1)S(1)} %reshape.90), channel_id=1, replica_groups=mesh['seq'=12,'head'=64] {'head'}, dimensions={0} | all-to-all | bytes 2097152 | tf_op jit(solution)/shard_map/all_to_all | solution.py:131
  (360 shorter events, 32.4 us)
Async XLA Ops:
  0.0 32.3 %copy-start.4 = (bf16[16,4096]{1,0:T(8,128)(2,1)S(1)}, bf16[16,4096]{1,0:T(8,128)(2,1)}, u32[]{:S(2)}) copy-start(bf16[16,4096]{1,0:T(8,128)(2,1)} %param.10) | copy-start | bytes 393220
  0.0 32.3 %copy-start.3 = (bf16[16,4096]{1,0:T(8,128)(2,1)S(1)}, bf16[16,4096]{1,0:T(8,128)(2,1)}, u32[]{:S(2)}) copy-start(bf16[16,4096]{1,0:T(8,128)(2,1)} %param.11) | copy-start | bytes 393220
  0.0 34.9 %copy-start.2 = (bf16[64,4096]{1,0:T(8,128)(2,1)S(1)}, bf16[64,4096]{1,0:T(8,128)(2,1)}, u32[]{:S(2)}) copy-start(bf16[64,4096]{1,0:T(8,128)(2,1)} %param.9) | copy-start | bytes 1572868
  0.0 34.9 %copy-start.1 = (bf16[64,4096]{1,0:T(8,128)(2,1)S(1)}, bf16[64,4096]{1,0:T(8,128)(2,1)}, u32[]{:S(2)}) copy-start(bf16[64,4096]{1,0:T(8,128)(2,1)} %param.12) | copy-start | bytes 1572868
  22.0 7.7 %collective-permute-start.3 = (bf16[8,4096]{1,0:T(8,128)(2,1)S(1)}, bf16[8,4096]{1,0:T(8,128)(2,1)S(1)}, u32[]{:S(2)}, u32[]{:S(2)}) collective-permute-start(bf16[8,4096]{1,0:T(8,128)(2,1)S(1)} %all_to_all.24), channel_id=1, source_target_pairs={{0,4},{4,0},{1,5},{5,1},{2,6},{6,2},{3,7},{7,3},{8,12},{12,8},{9,1... | collective-permute-start | bytes 196616 | tf_op jit(solution)/shard_map/ppermute | solution.py:21
  26.2 6.1 %collective-permute-start = (bf16[2,16,4096]{2,1,0:T(8,128)(2,1)S(1)}, bf16[2,16,4096]{2,1,0:T(8,128)(2,1)S(1)}, u32[]{:S(2)}, u32[]{:S(2)}) collective-permute-start(bf16[2,16,4096]{2,1,0:T(8,128)(2,1)S(1)} %pad_maximum_fusion.1), channel_id=1, source_target_pairs={{0,1},{1,0},{2,3},{3,2},{4,5},{5,4},{6,7},{7,6},{8,9},{9,8},{10,11... | collective-permute-start | bytes 786440 | tf_op jit(solution)/shard_map/ppermute | solution.py:21
  29.7 7.3 %collective-permute-start.4 = (bf16[16,4096]{1,0:T(8,128)(2,1)S(1)}, bf16[16,4096]{1,0:T(8,128)(2,1)S(1)}, u32[]{:S(2)}, u32[]{:S(2)}) collective-permute-start(bf16[16,4096]{1,0:T(8,128)(2,1)S(1)} %maximum_select_fusion.15), channel_id=1, source_target_pairs={{0,8},{8,0},{1,9},{9,1},{2,10},{10,2},{3,11},{11,3},{4,12},{12,4},... | collective-permute-start | bytes 393224 | tf_op jit(solution)/shard_map/ppermute | solution.py:21
  32.4 14.5 %collective-permute-start.1 = (bf16[2,32,4096]{2,1,0:T(8,128)(2,1)S(1)}, bf16[2,32,4096]{2,1,0:T(8,128)(2,1)}, u32[]{:S(2)}, u32[]{:S(2)}) collective-permute-start(bf16[2,32,4096]{2,1,0:T(8,128)(2,1)S(1)} %maximum_select_fusion.10), channel_id=1, source_target_pairs={{0,2},{2,0},{1,3},{3,1},{4,6},{6,4},{5,7},{7,5},{8,10},{10,8},{9,1... | collective-permute-start | bytes 1572872 | tf_op jit(solution)/shard_map/ppermute | solution.py:21
  35.1 23.2 %collective-permute-start.9 = (bf16[2,64,4096]{2,1,0:T(8,128)(2,1)S(1)}, bf16[2,64,4096]{2,1,0:T(8,128)(2,1)}, u32[]{:S(2)}, u32[]{:S(2)}) collective-permute-start(bf16[2,64,4096]{2,1,0:T(8,128)(2,1)S(1)} %pad_maximum_fusion), channel_id=1, source_target_pairs={{0,1},{1,0},{2,3},{3,2},{4,5},{5,4},{6,7},{7,6},{8,9},{9,8},{10,11... | collective-permute-start | bytes 3145736 | tf_op jit(solution)/shard_map/ppermute | solution.py:21
  37.1 17.1 %collective-permute-start.5 = (bf16[32,4096]{1,0:T(8,128)(2,1)S(1)}, bf16[32,4096]{1,0:T(8,128)(2,1)S(1)}, u32[]{:S(2)}, u32[]{:S(2)}) collective-permute-start(bf16[32,4096]{1,0:T(8,128)(2,1)S(1)} %maximum_select_fusion.12), channel_id=1, source_target_pairs={{0,16},{16,0},{1,17},{17,1},{2,18},{18,2},{3,19},{19,3},{4,20},{20... | collective-permute-start | bytes 786440 | tf_op jit(solution)/shard_map/ppermute | solution.py:21
  49.4 35.7 %collective-permute-start.2 = (bf16[2,64,4096]{2,1,0:T(8,128)(2,1)}, bf16[2,64,4096]{2,1,0:T(8,128)(2,1)}, u32[]{:S(2)}, u32[]{:S(2)}) collective-permute-start(bf16[2,64,4096]{2,1,0:T(8,128)(2,1)} %maximum_select_fusion.8), channel_id=1, source_target_pairs={{0,4},{4,0},{1,5},{5,1},{2,6},{6,2},{3,7},{7,3},{8,12},{12,8},{9,1... | collective-permute-start | bytes 3145736 | tf_op jit(solution)/shard_map/ppermute | solution.py:21
  55.1 30.0 %collective-permute-start.6 = (bf16[64,4096]{1,0:T(8,128)(2,1)}, bf16[64,4096]{1,0:T(8,128)(2,1)}, u32[]{:S(2)}, u32[]{:S(2)}) collective-permute-start(bf16[64,4096]{1,0:T(8,128)(2,1)} %maximum_select_fusion.11), channel_id=1, source_target_pairs={{0,32},{32,0},{1,33},{33,1},{2,34},{34,2},{3,35},{35,3},{4,36},{36... | collective-permute-start | bytes 1572872 | tf_op jit(solution)/shard_map/ppermute | solution.py:21
  60.4 67.4 %collective-permute-start.10 = (bf16[2,128,4096]{2,1,0:T(8,128)(2,1)S(1)}, bf16[2,128,4096]{2,1,0:T(8,128)(2,1)}, u32[]{:S(2)}, u32[]{:S(2)}) collective-permute-start(bf16[2,128,4096]{2,1,0:T(8,128)(2,1)S(1)} %maximum_select_fusion.4), channel_id=1, source_target_pairs={{0,2},{2,0},{1,3},{3,1},{4,6},{6,4},{5,7},{7,5},{8,10},{10,8},{9,1... | collective-permute-start | bytes 6291464 | tf_op jit(solution)/shard_map/ppermute | solution.py:21
  112.9 11.2 %copy-start.5 = (s32[6144]{0:T(1024)S(1)}, s32[6144]{0:T(1024)}, u32[]{:S(2)}) copy-start(s32[6144]{0:T(1024)} %param.13) | copy-start | bytes 73732
  114.1 4.4 %collective-permute-start.7 = (bf16[2,128,12,128]{1,3,2,0:T(8,128)(2,1)}, bf16[2,128,12,128]{1,3,2,0:T(8,128)(2,1)S(1)}, u32[]{:S(2)}, u32[]{:S(2)}) collective-permute-start(bf16[2,128,12,128]{1,3,2,0:T(8,128)(2,1)} %bitcast.98), channel_id=1, source_target_pairs={{0,1},{1,0},{2,3},{3,2},{4,5},{5,4},{6,7},{7,6},{8,9},{9,8},{10,11... | collective-permute-start | bytes 2359304 | tf_op jit(solution)/shard_map/ppermute | solution.py:21
  121.5 38.6 %collective-permute-start.8 = (bf16[2,128,12,256]{1,3,2,0:T(8,128)(2,1)}, bf16[2,128,12,256]{1,3,2,0:T(8,128)(2,1)}, u32[]{:S(2)}, u32[]{:S(2)}) collective-permute-start(bf16[2,128,12,256]{1,3,2,0:T(8,128)(2,1)} %maximum_select_fusion.5), channel_id=1, source_target_pairs={{0,2},{2,0},{1,3},{3,1},{4,6},{6,4},{5,7},{7,5},{8,10},{10,8},{9,1... | collective-permute-start | bytes 4718600 | tf_op jit(solution)/shard_map/ppermute | solution.py:21
  131.5 1.9 copy-start
where the time goes:
time: 257 us
  blocking collectives  80.4 us (31%)
  waiting for transfers between devices  57.4 us (22%)
  other arithmetic  47 us (18%)
  starting transfers between devices  30 us (12%)
  matrix products  23.2 us (9%)
  local copies, waits for them, and re-layouts  13.4 us (5%)
  between operations  3.23 us (1%)
    ppermute x11, waiting for transfers between devices, swapped(): return lax.ppermute(block, axis, route)  57.4 us
    all_to_all x1, blocking collectives, local(): lax.all_to_all(partial_value, 'head', split_axis=2, concat_axis=0, tiled=...  35.9 us
    ppermute x11, starting transfers between devices, swapped(): return lax.ppermute(block, axis, route)  30 us
    all_gather x1, blocking collectives, local(): lax.all_gather(memory_local[:, :, None, :], 'seq', axis=2, tiled=True)  24.1 us
    unnamed x1, other arithmetic  22.4 us
    all_to_all x1, blocking collectives, local(): lax.all_to_all(ordered, 'head', split_axis=0, concat_axis=1, tiled=True)  20.4 us
    select_n x9, other arithmetic, collect(): jnp.where(flag == 0, jnp.concatenate([block, other], dim), jnp.concatenat...  16.3 us
    dot_general x35, matrix products, visit_tile(): jnp.einsum('kgrb,kdb->kgrd', powers.astype(jnp.bfloat16), value_tile, pre...  8.27 us
  transfers between devices with their start and end apart: 11, of which 6 were waited for; matrix products, arithmetic and copies ran while one was open for 8% of the time, Pallas kernels for 0%

commit v1 on v0

v1 whole, which is shorter than its diff:
```python
import functools
import math

import jax
import jax.numpy as jnp
from jax import lax
from jax.experimental import pallas as pl
from jax.experimental.pallas import tpu as pltpu
from jax.sharding import Mesh, PartitionSpec as P

DIM = 128
F32 = jnp.float32
BF16 = jnp.bfloat16
NEG = -1e30
FLOOR = -1e28


def call(body, outs, *args, smem=(), scratch=()):
    specs = [
        pl.BlockSpec(memory_space=pltpu.SMEM if i in smem else pltpu.VMEM)
        for i in range(len(args))
    ]
    single = not isinstance(outs, (list, tuple))
    many = [outs] if single else list(outs)
    out = pl.pallas_call(
        body,
        out_shape=many,
        in_specs=specs,
        out_specs=[pl.BlockSpec(memory_space=pltpu.VMEM)] * len(many),
        scratch_shapes=list(scratch),
    )(*args)
    return out[0] if single else out


def shape(*dims, dtype=BF16):
    return jax.ShapeDtypeStruct(dims, dtype)


def pack_weights(q_ref, k_ref, v_ref, out_ref):
    for x in range(4):
        for y in range(8):
            src = slice((y * 4 + x) * 128, (y * 4 + x + 1) * 128)
            dst = slice(y * 128, (y + 1) * 128)
            out_ref[x, 0:64, dst] = q_ref[:, src]
            out_ref[x, 64:80, dst] = k_ref[:, src]
            out_ref[x, 80:96, dst] = v_ref[:, src]


def pack_output_weight(o_ref, out_ref):
    for y in range(8):
        out_ref[y] = o_ref[:, y * 512 : (y + 1) * 512]


def project(meta_ref, own_ref, other_ref, x_ref, out_ref, y_ref):
    c = meta_ref[2]
    xs = x_ref[...].reshape(1024, 256)
    y_ref[c] = jnp.dot(own_ref[...].reshape(384, 1024), xs, preferred_element_type=F32)
    y_ref[1 - c] = jnp.dot(other_ref[...].reshape(384, 1024), xs, preferred_element_type=F32)
    low = lax.broadcasted_iota(jnp.int32, (16, 128), 1) < 64
    for x in range(4):
        for half in range(2):
            rows = y_ref[half, x * 96 : x * 96 + 64, :]
            for t in range(2):
                at = t * 128 + half * 64
                out_ref[x, at : at + 64, :] = rows[:, t * 128 : (t + 1) * 128].astype(BF16)
    for src in range(4):
        for half in range(2):
            at = 256 + (src * 2 + half) * 16
            for t in range(2):
                lanes = slice(t * 128, (t + 1) * 128)
                key = y_ref[half, src * 96 + 64 : src * 96 + 80, lanes]
                val = y_ref[half, src * 96 + 80 : src * 96 + 96, lanes]
                even = jnp.where(low, key, pltpu.roll(val, 64, 1))
                odd = jnp.where(low, pltpu.roll(key, 64, 1), val)
                out_ref[2 * t, at : at + 16, :] = even.astype(BF16)
                out_ref[2 * t + 1, at : at + 16, :] = odd.astype(BF16)


def sum_projection(in_ref, q_ref, kv_ref):
    total = in_ref[0].astype(F32)
    for j in range(1, 4):
        total = total + in_ref[j].astype(F32)
    total = total.astype(BF16)
    for j in range(4):
        q_ref[j] = total[0:256]
    kv_ref[...] = total[256:384]


def split3(value):
    high = value.astype(BF16)
    rest = value - high.astype(F32)
    mid = rest.astype(BF16)
    low = (rest - mid.astype(F32)).astype(BF16)
    return high, mid, low


def attend(meta_ref, start_ref, q_ref, own_ref, other_ref, out_ref, qs_ref, s_ref, m_ref, o_ref):
    z, x, c, first = meta_ref[0], meta_ref[1], meta_ref[2], meta_ref[3]
    for h in range(4):
        for t in range(2):
            at = (h * 2 + t) * 128
            qs_ref[:, at : at + 128] = q_ref[h, t * 128 : (t + 1) * 128, :]
    begin = jnp.concatenate([start_ref[...]] * 4, axis=1)
    lane = lax.broadcasted_iota(jnp.int32, (1, 1024), 1)
    query = z * 512 + c * 256 + (lane & 255)
    row = lax.broadcasted_iota(jnp.int32, (128, 1), 0)
    offset = (row >> 6) * 256 + x * 64 + (row & 63)
    low = lax.broadcasted_iota(jnp.int32, (128, 128), 1) < 64
    factor = math.log2(math.e) / math.sqrt(DIM)
    m_ref[...] = jnp.full((8, 1024), FLOOR, F32)
    o_ref[...] = jnp.zeros((128, 1024), F32)

    def tiles(j):
        own = own_ref[j].astype(F32)
        other = other_ref[j].astype(F32)
        first_half = jnp.where(c == 0, own, other)
        second_half = jnp.where(c == 0, other, own)
        return first_half, second_half

    def score(j, unused):
        a, b = tiles(j)
        key = jnp.where(low, a, pltpu.roll(b, 64, 1)).T.astype(BF16)
        s = jnp.dot(key, qs_ref[...], preferred_element_type=F32) * factor
        place = j * 512 + offset
        s = jnp.where((place >= begin) & (place <= query), s, NEG)
        s_ref[j] = s
        m_ref[...] = jnp.maximum(m_ref[...], jnp.max(s.reshape(16, 8, 1024), axis=0))
        return unused

    lax.fori_loop(first, z + 1, score, 0)
    top = jnp.max(m_ref[...], axis=0, keepdims=True)

    def mix(j, total):
        a, b = tiles(j)
        val = jnp.where(low, pltpu.roll(a, 64, 1), b).astype(BF16)
        p = jnp.exp2(s_ref[j] - top)
        o_ref[...] += jnp.dot(val, p.astype(BF16), preferred_element_type=F32)
        return total + jnp.sum(p.reshape(16, 8, 1024), axis=0)

    total = lax.fori_loop(first, z + 1, mix, jnp.zeros((8, 1024), F32))
    total = jnp.sum(total, axis=0, keepdims=True)
    stats = [v.astype(F32) for v in split3(top) + split3(total)]
    stats = jnp.concatenate(stats + [jnp.zeros((2, 1024), F32)], axis=0)
    for h in range(4):
        lanes = slice(h * 256, (h + 1) * 256)
        out_ref[h, 0:128, :] = o_ref[:, lanes].astype(BF16)
        out_ref[h, 128:136, :] = stats[:, lanes].astype(BF16)


def combine(in_ref, out_ref):
    tops, totals = [], []
    for j in range(4):
        st = in_ref[j, 128:136, :].astype(F32)
        tops.append(st[0:1] + st[1:2] + st[2:3])
        totals.append(st[3:4] + st[4:5] + st[5:6])
    top = jnp.maximum(jnp.maximum(tops[0], tops[1]), jnp.maximum(tops[2], tops[3]))
    shares = [jnp.exp2(t - top) for t in tops]
    total = sum(w * t for w, t in zip(shares, totals))
    mixed = sum(in_ref[j, 0:128, :].astype(F32) * (shares[j] / total) for j in range(4))
    mixed = mixed.astype(BF16)
    for j in range(8):
        out_ref[j] = mixed


def output_project(meta_ref, own_ref, other_ref, a_ref, out_ref, one_ref, two_ref):
    c = meta_ref[2]
    for y in range(8):
        one_ref[y * 64 : (y + 1) * 64, :] = a_ref[y, pl.ds(pl.multiple_of(c * 64, 64), 64), :]
        two_ref[y * 64 : (y + 1) * 64, :] = a_ref[y, pl.ds(pl.multiple_of(64 - c * 64, 64), 64), :]
    dims = (((0,), (0,)), ((), ()))
    r = lax.dot_general(own_ref[...].reshape(512, 512), one_ref[...], dims, preferred_element_type=F32)
    r = r + lax.dot_general(other_ref[...].reshape(512, 512), two_ref[...], dims, preferred_element_type=F32)
    out_ref[...] = r.astype(BF16).reshape(4, 128, 256)


def sum_output(in_ref, out_ref):
    total = in_ref[0].astype(F32)
    for j in range(1, 4):
        total = total + in_ref[j].astype(F32)
    out_ref[...] = total.astype(BF16).reshape(2, 64, 256)


def trade(block, axis):
    return lax.all_to_all(block, axis, split_axis=0, concat_axis=0, tiled=True)


def partner(block):
    return lax.ppermute(block, "c", [(0, 1), (1, 0)])


def local(tokens, query_weight, key_weight, value_weight, output_weight, segments):
    z, x, c = lax.axis_index("z"), lax.axis_index("x"), lax.axis_index("c")
    first_query = z * 512 + c * 256
    segment = lax.dynamic_slice_in_dim(segments, first_query, 256, 0)
    starts = jnp.sum((segments[:, None] < segment[None, :]).astype(jnp.int32), axis=0)
    place = lax.iota(jnp.int32, 8)
    meta = jnp.where(
        place == 0, z, jnp.where(place == 1, x, jnp.where(place == 2, c, starts[0] // 512))
    )

    halves = tokens.T.reshape(64, 2, 256).transpose(1, 0, 2)
    columns = trade(halves, "c").reshape(1, 128, 256)
    columns = trade(jnp.broadcast_to(columns, (8, 128, 256)), "y")

    packed = call(pack_weights, shape(4, 96, 1024), query_weight, key_weight, value_weight)
    own = trade(packed, "x")
    other = partner(own)

    out_own = trade(call(pack_output_weight, shape(8, 64, 512), output_weight), "y")
    out_other = partner(out_own)

    partial = call(
        project, shape(4, 384, 128), meta, own, other, columns, smem=(0,),
        scratch=[pltpu.VMEM((2, 384, 256), F32)],
    )
    spread, kv = call(sum_projection, [shape(4, 256, 128), shape(128, 128)], trade(partial, "x"))
    queries = trade(spread, "x")
    kv_own = lax.all_gather(kv, "z", axis=0, tiled=False)
    kv_other = partner(kv_own)
    mixed = call(
        attend, shape(4, 136, 256), meta, starts.reshape(1, 256), queries, kv_own, kv_other,
        smem=(0,),
        scratch=[
            pltpu.VMEM((128, 1024), BF16),
            pltpu.VMEM((12, 128, 1024), F32),
            pltpu.VMEM((8, 1024), F32),
            pltpu.VMEM((128, 1024), F32),
        ],
    )
    attended = trade(call(combine, shape(8, 128, 256), trade(mixed, "x")), "y")
    result = call(
        output_project, shape(4, 128, 256), meta, out_own, out_other, attended, smem=(0,),
        scratch=[pltpu.VMEM((512, 256), BF16), pltpu.VMEM((512, 256), BF16)],
    )
    summed = call(sum_output, shape(2, 64, 256), trade(result, "x"))
    final = trade(summed, "c")
    return final.transpose(1, 0, 2).reshape(64, 512).T


def solution(mesh):
    grid = Mesh(mesh.devices.reshape(12, 8, 4, 2), ("z", "y", "x", "c"))
    head = ("y", "x", "c")
    placed = (P("z", head), P(head, None), P(head, None), P(head, None), P(head, None), P())
    return jax.shard_map(
        local, mesh=grid, in_specs=placed, out_specs=P("z", head), check_vma=False
    )
```

time: 257 us -> 191 us (0.74)
  the two profiles are of different devices: /device:TPU:704 before, /device:TPU:1 now
where the time goes in v1:
time: 191 us; the launch traced here: 190 us
  blocking collectives  78.9 us (41%)
  starting transfers between devices  45.9 us (24%)
  waiting for transfers between devices  34.8 us (18%)
  Pallas kernels  17.5 us (9%)
  local copies, waits for them, and re-layouts  6.9 us (4%)
  other arithmetic  3.31 us (2%)
  between operations  2.74 us (1%)
    all_to_all x5, blocking collectives, trade(): return lax.all_to_all(block, axis, split_axis=0, concat_axis=0, tiled=True)  56.6 us
    all_to_all x5, waiting for transfers between devices, trade(): return lax.all_to_all(block, axis, split_axis=0, concat_axis=0, tiled=True)  33.2 us
    all_to_all x5, starting transfers between devices, trade(): return lax.all_to_all(block, axis, split_axis=0, concat_axis=0, tiled=True)  27.7 us
    all_gather x1, blocking collectives, local(): kv_own = lax.all_gather(kv, 'z', axis=0, tiled=False)  22.2 us
    ppermute x3, starting transfers between devices, partner(): return lax.ppermute(block, 'c', [(0, 1), (1, 0)])  18.2 us
    pallas_call x8, Pallas kernels, call(): pl.pallas_call(body, out_shape=many, in_specs=specs, out_specs=[pl.BlockS...  17.5 us
  transfers between devices with their start and end apart: 8, of which 5 were waited for; matrix products, arithmetic and copies ran while one was open for 2% of the time, Pallas kernels for 3%

profile of v1, /device:TPU:1, one launch (start us, length us, event | category | flops | bytes accessed | tf_op | source)
XLA Modules:
  0.0 189.9 jit_solution(4412893965718684431)
XLA Ops:
  0.0 0.9 reshape.14
  1.5 13.8 %all-to-all-start.2 = ((bf16[2,64,256]{2,1,0:T(8,128)(2,1)}), bf16[2,64,256]{2,1,0:T(8,128)(2,1)S(1)}, u32[]{:S(2)}, u32[]{:S(2)}) async-start(bf16[2,64,256]{2,1,0:T(8,128)(2,1)} %copy.13), calls=%async_computation.2 | async-start | bytes 131072 | tf_op jit(solution)/shard_map/all_to_all | solution.py:184
  15.3 2.2 %shard_map.65 = bf16[4,96,1024]{2,1,0:T(8,128)(2,1)} custom-call(bf16[64,4096]{1,0:T(8,128)(2,1)} %q_ref.1, bf16[16,4096]{1,0:T(8,128)(2,1)} %k_ref.1, bf16[16,4096]{1,0:T(8,128)(2,1)} %v_ref.1), custom_call_target="tpu_custom_call" | custom-call | tf_op jit(solution)/shard_map/pallas_call | solution.py:25
  17.4 15.5 %all_to_all.50.own_ref = bf16[4,96,1024]{2,1,0:T(8,128)(2,1)S(1)} all-to-all(bf16[4,96,1024]{2,1,0:T(8,128)(2,1)} %shard_map.65), channel_id=1, replica_groups=mesh['z'=12,'y'=8,'x'=4,'c'=2] {'x'}, dimensions={0} | all-to-all | bytes 1572864 | tf_op jit(solution)/shard_map/all_to_all | solution.py:184
  33.0 0.9 broadcast_in_dim.29
  33.9 3.5 %all-to-all-start.3 = ((bf16[8,128,256]{2,1,0:T(8,128)(2,1)}), bf16[8,128,256]{2,1,0:T(8,128)(2,1)S(1)}, u32[]{:S(2)}, u32[]{:S(2)}) async-start(bf16[8,128,256]{2,1,0:T(8,128)(2,1)} %broadcast_in_dim.29), calls=%async_computation.3 | async-start | bytes 1048576 | tf_op jit(solution)/shard_map/all_to_all | solution.py:184
  37.4 3.1 %collective-permute-start.1 = (bf16[4,96,1024]{2,1,0:T(8,128)(2,1)S(1)}, bf16[4,96,1024]{2,1,0:T(8,128)(2,1)S(1)}, u32[]{:S(2)}, u32[]{:S(2)}) collective-permute-start(bf16[4,96,1024]{2,1,0:T(8,128)(2,1)S(1)} %all_to_all.50.own_ref), channel_id=1, source_target_pairs={{0,1},{1,0},{2,3},{3,2},{4,5},{5,4},{6,7},{7,6},{8,9},{9,8},{10,11... | collective-permute-start | bytes 2359304 | tf_op jit(solution)/shard_map/ppermute | solution.py:188
  40.6 2.7 %convert_reduce_fusion = s32[256]{0:T(256)S(1)} fusion(s32[256]{0:T(256)S(1)} %dynamic_slice.3, s32[6144]{0:T(1024)S(1)} %copy-done.9), kind=kLoop, calls=%fused_computation | loop fusion | flops 4718336 | bytes 26624 | tf_op jit(solution)/shard_map/reduce_sum | solution.py:195
  47.0 8.1 %all-to-all-done.3.x_ref = bf16[8,128,256]{2,1,0:T(8,128)(2,1)S(1)} async-done(((bf16[8,128,256]{2,1,0:T(8,128)(2,1)}), bf16[8,128,256]{2,1,0:T(8,128)(2,1)S(1)}, u32[]{:S(2)}, u32[]{:S(2)}) %all-to-all-start.3) | async-done | bytes 524320 | tf_op jit(solution)/shard_map/all_to_all | solution.py:184
  55.1 0.8 copy-done.1
  55.9 0.9 copy-done.6
  56.8 3.0 %shard_map.66 = bf16[4,384,128]{2,1,0:T(8,128)(2,1)} custom-call(s32[8]{0:T(128)} %compare_select_fusion.2.meta_ref, bf16[4,96,1024]{2,1,0:T(8,128)(2,1)} %copy-done, bf16[4,96,1024]{2,1,0:T(8,128)(2,1)} %copy-done.6, bf16[8,128,256]{2,1,0:T(8,128)(2,1)} %copy-done.1), custom_call_target="tpu_custom_call" | custom-call | tf_op jit(solution)/shard_map/pallas_call | solution.py:25
  59.8 11.5 %all_to_all.51.in_ref = bf16[4,384,128]{2,1,0:T(8,128)(2,1)} all-to-all(bf16[4,384,128]{2,1,0:T(8,128)(2,1)} %shard_map.66), channel_id=1, replica_groups=mesh['z'=12,'y'=8,'x'=4,'c'=2] {'x'}, dimensions={0} | all-to-all | bytes 786432 | tf_op jit(solution)/shard_map/all_to_all | solution.py:184
  71.3 1.7 shard_map.67
  73.0 22.2 %all-gather = bf16[1536,128]{1,0:T(8,128)(2,1)S(1)} all-gather(bf16[128,128]{1,0:T(8,128)(2,1)} %get-tuple-element.8), channel_id=2, replica_groups=mesh['z'=12,'y'=8,'x'=4,'c'=2] {'z'}, dimensions={0}, use_global_device_ids=true | all-gather | bytes 425984 | tf_op jit(solution)/shard_map/all_gather | solution.py:218
  95.2 10.2 %collective-permute-start.2 = (bf16[12,128,128]{2,1,0:T(8,128)(2,1)S(1)}, bf16[12,128,128]{2,1,0:T(8,128)(2,1)S(1)}, u32[]{:S(2)}, u32[]{:S(2)}) collective-permute-start(bf16[12,128,128]{2,1,0:T(8,128)(2,1)S(1)} %bitcast.11), channel_id=1, source_target_pairs={{0,1},{1,0},{2,3},{3,2},{4,5},{5,4},{6,7},{7,6},{8,9},{9,8},{10,11... | collective-permute-start | bytes 1179656 | tf_op jit(solution)/shard_map/ppermute | solution.py:188
  105.4 10.6 %all_to_all.52.q_ref = bf16[4,256,128]{2,1,0:T(8,128)(2,1)} all-to-all(bf16[4,256,128]{2,1,0:T(8,128)(2,1)} %get-tuple-element.7), channel_id=1, replica_groups=mesh['z'=12,'y'=8,'x'=4,'c'=2] {'x'}, dimensions={0} | all-to-all | bytes 524288 | tf_op jit(solution)/shard_map/all_to_all | solution.py:184
  116.7 2.7 %shard_map.68 = bf16[4,136,256]{2,1,0:T(8,128)(2,1)} custom-call(s32[8]{0:T(128)} %compare_select_fusion.2.meta_ref, s32[1,256]{1,0:T(1,128)} %bitcast.17, bf16[4,256,128]{2,1,0:T(8,128)(2,1)} %all_to_all.52.q_ref, bf16[12,128,128]{2,1,0:T(8,128)(2,1)} %bitcast.12, bf16[12,128,128]{2,1,0:T(8,128)(2,1)} %copy-done.8), custom_call_target="tpu_custom_call" | custom-call | tf_op jit(solution)/shard_map/pallas_call | solution.py:25
  119.5 3.4 %all-to-all-start.6 = ((bf16[4,136,256]{2,1,0:T(8,128)(2,1)}), bf16[4,136,256]{2,1,0:T(8,128)(2,1)S(1)}, u32[]{:S(2)}, u32[]{:S(2)}) async-start(bf16[4,136,256]{2,1,0:T(8,128)(2,1)} %shard_map.68), calls=%async_computation.6 | async-start | bytes 557056 | tf_op jit(solution)/shard_map/all_to_all | solution.py:184
  122.9 1.9 shard_map.64
  124.8 3.7 %all-to-all-done.6.in_ref = bf16[4,136,256]{2,1,0:T(8,128)(2,1)S(1)} async-done(((bf16[4,136,256]{2,1,0:T(8,128)(2,1)}), bf16[4,136,256]{2,1,0:T(8,128)(2,1)S(1)}, u32[]{:S(2)}, u32[]{:S(2)}) %all-to-all-start.6) | async-done | bytes 278560 | tf_op jit(solution)/shard_map/all_to_all | solution.py:184
  128.5 3.5 %all-to-all-start = ((bf16[8,64,512]{2,1,0:T(8,128)(2,1)}), bf16[8,64,512]{2,1,0:T(8,128)(2,1)S(1)}, u32[]{:S(2)}, u32[]{:S(2)}) async-start(bf16[8,64,512]{2,1,0:T(8,128)(2,1)} %shard_map.64), calls=%async_computation | async-start | bytes 1048576 | tf_op jit(solution)/shard_map/all_to_all | solution.py:184
  132.0 1.8 shard_map.69
  133.9 13.5 %all-to-all-done.own_ref = bf16[8,64,512]{2,1,0:T(8,128)(2,1)S(1)} async-done(((bf16[8,64,512]{2,1,0:T(8,128)(2,1)}), bf16[8,64,512]{2,1,0:T(8,128)(2,1)S(1)}, u32[]{:S(2)}, u32[]{:S(2)}) %all-to-all-start) | async-done | bytes 524320 | tf_op jit(solution)/shard_map/all_to_all | solution.py:184
  147.3 3.5 %all-to-all-start.7 = ((bf16[8,128,256]{2,1,0:T(8,128)(2,1)}), bf16[8,128,256]{2,1,0:T(8,128)(2,1)S(1)}, u32[]{:S(2)}, u32[]{:S(2)}) async-start(bf16[8,128,256]{2,1,0:T(8,128)(2,1)} %shard_map.69), calls=%async_computation.7 | async-start | bytes 1048576 | tf_op jit(solution)/shard_map/all_to_all | solution.py:184
  150.8 5.0 %collective-permute-start = (bf16[8,64,512]{2,1,0:T(8,128)(2,1)S(1)}, bf16[8,64,512]{2,1,0:T(8,128)(2,1)S(1)}, u32[]{:S(2)}, u32[]{:S(2)}) collective-permute-start(bf16[8,64,512]{2,1,0:T(8,128)(2,1)S(1)} %all-to-all-done.own_ref), channel_id=1, source_target_pairs={{0,1},{1,0},{2,3},{3,2},{4,5},{5,4},{6,7},{7,6},{8,9},{9,8},{10,11... | collective-permute-start | bytes 1572872 | tf_op jit(solution)/shard_map/ppermute | solution.py:188
  155.8 1.5 collective-permute-done.other_ref
  157.3 7.9 %all-to-all-done.7.a_ref = bf16[8,128,256]{2,1,0:T(8,128)(2,1)S(1)} async-done(((bf16[8,128,256]{2,1,0:T(8,128)(2,1)}), bf16[8,128,256]{2,1,0:T(8,128)(2,1)S(1)}, u32[]{:S(2)}, u32[]{:S(2)}) %all-to-all-start.7) | async-done | bytes 524320 | tf_op jit(solution)/shard_map/all_to_all | solution.py:184
  166.0 2.6 %shard_map.70 = bf16[4,128,256]{2,1,0:T(8,128)(2,1)} custom-call(s32[8]{0:T(128)} %compare_select_fusion.2.meta_ref, bf16[8,64,512]{2,1,0:T(8,128)(2,1)} %copy-done.2, bf16[8,64,512]{2,1,0:T(8,128)(2,1)} %copy-done.7, bf16[8,128,256]{2,1,0:T(8,128)(2,1)} %copy-done.3), custom_call_target="tpu_custom_call" | custom-call | tf_op jit(solution)/shard_map/pallas_call | solution.py:25
  168.6 9.6 %all_to_all.53.in_ref = bf16[4,128,256]{2,1,0:T(8,128)(2,1)} all-to-all(bf16[4,128,256]{2,1,0:T(8,128)(2,1)} %shard_map.70), channel_id=1, replica_groups=mesh['z'=12,'y'=8,'x'=4,'c'=2] {'x'}, dimensions={0} | all-to-all | bytes 524288 | tf_op jit(solution)/shard_map/all_to_all | solution.py:184
  178.2 1.6 shard_map.71
  179.8 9.4 %all_to_all.54 = bf16[2,64,256]{2,1,0:T(8,128)(2,1)S(1)} all-to-all(bf16[2,64,256]{2,1,0:T(8,128)(2,1)} %shard_map.71), channel_id=1, replica_groups=mesh['z'=12,'y'=8,'x'=4,'c'=2] {'c'}, dimensions={0} | all-to-all | bytes 131072 | tf_op jit(solution)/shard_map/all_to_all | solution.py:184
  (28 shorter events, 4.0 us)
Async XLA Ops:
  1.5 15.9 %all-to-all-start.2 = ((bf16[2,64,256]{2,1,0:T(8,128)(2,1)}), bf16[2,64,256]{2,1,0:T(8,128)(2,1)S(1)}, u32[]{:S(2)}, u32[]{:S(2)}) async-start(bf16[2,64,256]{2,1,0:T(8,128)(2,1)} %copy.13), calls=%async_computation.2 | async-start | bytes 131072 | tf_op jit(solution)/shard_map/all_to_all | solution.py:184
  33.0 4.4 %copy-start = (bf16[4,96,1024]{2,1,0:T(8,128)(2,1)}, bf16[4,96,1024]{2,1,0:T(8,128)(2,1)S(1)}, u32[]{:S(2)}) copy-start(bf16[4,96,1024]{2,1,0:T(8,128)(2,1)S(1)} %all_to_all.50.own_ref) | copy-start | bytes 2359300
  33.0 7.5 %copy-start.9 = (s32[6144]{0:T(1024)S(1)}, s32[6144]{0:T(1024)}, u32[]{:S(2)}) copy-start(s32[6144]{0:T(1024)} %param.11) | copy-start | bytes 73732
  33.9 21.3 %all-to-all-start.3 = ((bf16[8,128,256]{2,1,0:T(8,128)(2,1)}), bf16[8,128,256]{2,1,0:T(8,128)(2,1)S(1)}, u32[]{:S(2)}, u32[]{:S(2)}) async-start(bf16[8,128,256]{2,1,0:T(8,128)(2,1)} %broadcast_in_dim.29), calls=%async_computation.3 | async-start | bytes 1048576 | tf_op jit(solution)/shard_map/all_to_all | solution.py:184
  37.4 17.8 %collective-permute-start.1 = (bf16[4,96,1024]{2,1,0:T(8,128)(2,1)S(1)}, bf16[4,96,1024]{2,1,0:T(8,128)(2,1)S(1)}, u32[]{:S(2)}, u32[]{:S(2)}) collective-permute-start(bf16[4,96,1024]{2,1,0:T(8,128)(2,1)S(1)} %all_to_all.50.own_ref), channel_id=1, source_target_pairs={{0,1},{1,0},{2,3},{3,2},{4,5},{5,4},{6,7},{7,6},{8,9},{9,8},{10,11... | collective-permute-start | bytes 2359304 | tf_op jit(solution)/shard_map/ppermute | solution.py:188
  43.3 16.5 %copy-start.10 = (s32[256]{0:T(256)}, s32[256]{0:T(256)S(1)}, u32[]{:S(2)}) copy-start(s32[256]{0:T(256)S(1)} %convert_reduce_fusion) | copy-start | bytes 3076
  55.1 0.8 copy-start.1
  55.9 0.9 copy-start.6
  95.2 20.8 %copy-start.4 = (bf16[1536,128]{1,0:T(8,128)(2,1)}, bf16[1536,128]{1,0:T(8,128)(2,1)S(1)}, u32[]{:S(2)}) copy-start(bf16[1536,128]{1,0:T(8,128)(2,1)S(1)} %all-gather) | copy-start | bytes 1179652
  95.2 20.8 %collective-permute-start.2 = (bf16[12,128,128]{2,1,0:T(8,128)(2,1)S(1)}, bf16[12,128,128]{2,1,0:T(8,128)(2,1)S(1)}, u32[]{:S(2)}, u32[]{:S(2)}) collective-permute-start(bf16[12,128,128]{2,1,0:T(8,128)(2,1)S(1)} %bitcast.11), channel_id=1, source_target_pairs={{0,1},{1,0},{2,3},{3,2},{4,5},{5,4},{6,7},{7,6},{8,9},{9,8},{10,11... | collective-permute-start | bytes 1179656 | tf_op jit(solution)/shard_map/ppermute | solution.py:188
  116.0 0.8 copy-start.8
  119.5 9.0 %all-to-all-start.6 = ((bf16[4,136,256]{2,1,0:T(8,128)(2,1)}), bf16[4,136,256]{2,1,0:T(8,128)(2,1)S(1)}, u32[]{:S(2)}, u32[]{:S(2)}) async-start(bf16[4,136,256]{2,1,0:T(8,128)(2,1)} %shard_map.68), calls=%async_computation.6 | async-start | bytes 557056 | tf_op jit(solution)/shard_map/all_to_all | solution.py:184
  128.5 3.5 %copy-start.5 = (bf16[4,136,256]{2,1,0:T(8,128)(2,1)}, bf16[4,136,256]{2,1,0:T(8,128)(2,1)S(1)}, u32[]{:S(2)}) copy-start(bf16[4,136,256]{2,1,0:T(8,128)(2,1)S(1)} %all-to-all-done.6.in_ref) | copy-start | bytes 835588
  128.5 18.8 %all-to-all-start = ((bf16[8,64,512]{2,1,0:T(8,128)(2,1)}), bf16[8,64,512]{2,1,0:T(8,128)(2,1)S(1)}, u32[]{:S(2)}, u32[]{:S(2)}) async-start(bf16[8,64,512]{2,1,0:T(8,128)(2,1)} %shard_map.64), calls=%async_computation | async-start | bytes 1048576 | tf_op jit(solution)/shard_map/all_to_all | solution.py:184
  147.3 17.9 %copy-start.2 = (bf16[8,64,512]{2,1,0:T(8,128)(2,1)}, bf16[8,64,512]{2,1,0:T(8,128)(2,1)S(1)}, u32[]{:S(2)}) copy-start(bf16[8,64,512]{2,1,0:T(8,128)(2,1)S(1)} %all-to-all-done.own_ref) | copy-start | bytes 1572868
  147.3 17.9 %all-to-all-start.7 = ((bf16[8,128,256]{2,1,0:T(8,128)(2,1)}), bf16[8,128,256]{2,1,0:T(8,128)(2,1)S(1)}, u32[]{:S(2)}, u32[]{:S(2)}) async-start(bf16[8,128,256]{2,1,0:T(8,128)(2,1)} %shard_map.69), calls=%async_computation.7 | async-start | bytes 1048576 | tf_op jit(solution)/shard_map/all_to_all | solution.py:184
  150.8 6.5 %collective-permute-start = (bf16[8,64,512]{2,1,0:T(8,128)(2,1)S(1)}, bf16[8,64,512]{2,1,0:T(8,128)(2,1)S(1)}, u32[]{:S(2)}, u32[]{:S(2)}) collective-permute-start(bf16[8,64,512]{2,1,0:T(8,128)(2,1)S(1)} %all-to-all-done.own_ref), channel_id=1, source_target_pairs={{0,1},{1,0},{2,3},{3,2},{4,5},{5,4},{6,7},{7,6},{8,9},{9,8},{10,11... | collective-permute-start | bytes 1572872 | tf_op jit(solution)/shard_map/ppermute | solution.py:188
  157.3 7.9 %copy-start.7 = (bf16[8,64,512]{2,1,0:T(8,128)(2,1)}, bf16[8,64,512]{2,1,0:T(8,128)(2,1)S(1)}, u32[]{:S(2)}) copy-start(bf16[8,64,512]{2,1,0:T(8,128)(2,1)S(1)} %collective-permute-done.other_ref) | copy-start | bytes 1572868
  165.2 0.8 copy-start.3

commit v2 on v1

v2 whole, which is shorter than its diff:
```python
import math

import jax
import jax.numpy as jnp
from jax import lax
from jax.experimental import pallas as pl
from jax.experimental.pallas import tpu as pltpu
from jax.sharding import Mesh, PartitionSpec as P


DIM = 128
F32 = jnp.float32
BF16 = jnp.bfloat16
NEG = -1e30
FLOOR = -1e28


def call(body, outs, *args, smem=(), scratch=(), limit=8):
    specs = [
        pl.BlockSpec(memory_space=pltpu.SMEM if i in smem else pltpu.VMEM)
        for i in range(len(args))
    ]
    single = not isinstance(outs, (list, tuple))
    many = [outs] if single else list(outs)
    out = pl.pallas_call(
        body,
        out_shape=many,
        in_specs=specs,
        out_specs=[pl.BlockSpec(memory_space=pltpu.VMEM)] * len(many),
        scratch_shapes=list(scratch),
        compiler_params=pltpu.CompilerParams(vmem_limit_bytes=limit << 20),
    )(*args)
    return out[0] if single else out


def shape(*dims, dtype=BF16):
    return jax.ShapeDtypeStruct(dims, dtype)


def find_starts(meta_ref, seg_ref, start_ref, first_ref):
    at = meta_ref[0] * 2 + meta_ref[2]
    window = seg_ref[pl.ds(at, 1), :]
    lane = lax.broadcasted_iota(jnp.int32, (1, 256), 1)
    head = jnp.min(window)
    begin = jnp.sum((seg_ref[...] < head).astype(jnp.int32))
    changed = (lane > 0) & (window != pltpu.roll(window, 1, 1))
    starts = jnp.where(changed, at * 256 + lane, begin)
    for bit in range(8):
        moved = pltpu.roll(starts, 1 << bit, 1)
        starts = jnp.maximum(starts, jnp.where(lane >= 1 << bit, moved, 0))
    start_ref[...] = starts
    first_ref[0] = begin


def away(x, step):
    return (x + step) & 3


def pack_weights(meta_ref, q_ref, k_ref, v_ref, o_ref, *outs):
    for step in range(4):
        x = away(meta_ref[1], step)
        w_ref, out_ref = outs[step], outs[4 + step]
        for y in range(8):
            src = pl.ds(pl.multiple_of((y * 4 + x) * 128, 128), 128)
            dst = slice(y * 128, (y + 1) * 128)
            w_ref[0:64, dst] = q_ref[:, src]
            w_ref[64:80, dst] = k_ref[:, src]
            w_ref[80:96, dst] = v_ref[:, src]
            out_ref[:, dst] = o_ref[:, src]


def take_columns(meta_ref, in_ref, out_ref):
    c = meta_ref[2]
    for half in range(2):
        block = jnp.where(c == 0, in_ref[half, 0:64, :], in_ref[half, 64:128, :])
        out_ref[:, half * 256 : (half + 1) * 256] = block


def rows_of(start, size):
    return pl.ds(pl.multiple_of(start, size), size)


def project(meta_ref, w0, w1, w2, w3, own_ref, other_ref, *rest):
    outs, (x_ref, all_ref, y_ref) = rest[:4], rest[4:]
    x, c = meta_ref[1], meta_ref[2]
    for y in range(8):
        x_ref[rows_of(y * 128 + c * 64, 64), :] = own_ref[y * 64 : (y + 1) * 64, :]
        x_ref[rows_of(y * 128 + 64 - c * 64, 64), :] = other_ref[y * 64 : (y + 1) * 64, :]
    for step, w in enumerate((w0, w1, w2, w3)):
        all_ref[pl.ds(pl.multiple_of(away(x, -step) * 96, 32), 96), :] = w[...]
    y_ref[...] = jnp.dot(all_ref[...], x_ref[...], preferred_element_type=F32)
    for step, out_ref in enumerate(outs):
        to = away(x, step)
        rows = y_ref[pl.ds(pl.multiple_of(to * 96, 32), 64), :].astype(BF16)
        for t in range(4):
            out_ref[t * 64 : (t + 1) * 64, :] = rows[:, t * 128 : (t + 1) * 128]
        lanes = pl.ds(pl.multiple_of(to * 128, 128), 128)
        for j in range(4):
            at = 256 + j * 16
            out_ref[at : at + 16, :] = y_ref[j * 96 + 64 : j * 96 + 80, lanes].astype(BF16)
            at = 320 + j * 16
            out_ref[at : at + 16, :] = y_ref[j * 96 + 80 : j * 96 + 96, lanes].astype(BF16)


def sum_projection(a_ref, b_ref, c_ref, d_ref, q_ref, kv_ref):
    total = a_ref[...].astype(F32) + b_ref[...].astype(F32)
    total = (total + c_ref[...].astype(F32) + d_ref[...].astype(F32)).astype(BF16)
    q_ref[...] = total[0:256]
    for j in range(12):
        kv_ref[j] = total[256:384]


def split3(value):
    high = value.astype(BF16)
    rest = value - high.astype(F32)
    mid = rest.astype(BF16)
    low = (rest - mid.astype(F32)).astype(BF16)
    return high, mid, low


def attend(meta_ref, first_ref, start_ref, q_ref, kv_ref, out0, out1, out2, out3, qs_ref, s_ref, m_ref, o_ref, st_ref):
    z, x, c, first = meta_ref[0], meta_ref[1], meta_ref[2], first_ref[0] >> 9
    for h in range(4):
        for t in range(2):
            lanes = slice((h * 2 + t) * 128, (h * 2 + t + 1) * 128)
            for block in range(8):
                to = (block % 2) * 64 + (block // 2) * 16
                at = pl.ds(pl.multiple_of(c * 128 + t * 64 + (block % 4) * 16, 16), 16)
                qs_ref[to : to + 16, lanes] = q_ref[h * 2 + block // 4, at, :]
    begin = jnp.concatenate([start_ref[...]] * 4, axis=1)
    lane = lax.broadcasted_iota(jnp.int32, (1, 1024), 1)
    query = z * 512 + c * 256 + (lane & 255)
    offset = lax.broadcasted_iota(jnp.int32, (128, 1), 0) + x * 128
    factor = math.log2(math.e) / math.sqrt(DIM)
    m_ref[...] = jnp.full((8, 1024), FLOOR, F32)
    o_ref[...] = jnp.zeros((128, 1024), F32)

    def score(j, unused):
        key = jnp.concatenate([kv_ref[0, j, 0:64, :], kv_ref[1, j, 0:64, :]], axis=0)
        key = key.astype(F32).T.astype(BF16)
        s = jnp.dot(key, qs_ref[...], preferred_element_type=F32) * factor
        place = j * 512 + offset
        s = jnp.where((place >= begin) & (place <= query), s, NEG)
        s_ref[j] = s
        m_ref[...] = jnp.maximum(m_ref[...], jnp.max(s.reshape(16, 8, 1024), axis=0))
        return unused

    lax.fori_loop(first, z + 1, score, 0)
    top = jnp.max(m_ref[...], axis=0, keepdims=True)

    def mix(j, total):
        val = jnp.concatenate([kv_ref[0, j, 64:128, :], kv_ref[1, j, 64:128, :]], axis=0)
        p = jnp.exp2(s_ref[j] - top)
        o_ref[...] += jnp.dot(val, p.astype(BF16), preferred_element_type=F32)
        return total + jnp.sum(p.reshape(16, 8, 1024), axis=0)

    total = lax.fori_loop(first, z + 1, mix, jnp.zeros((8, 1024), F32))
    total = jnp.sum(total, axis=0, keepdims=True)
    stats = [v.astype(F32) for v in split3(top) + split3(total)]
    stats = jnp.concatenate(stats + [jnp.zeros((2, 1024), F32)], axis=0)
    st_ref[...] = stats
    for step, out_ref in enumerate((out0, out1, out2, out3)):
        lanes = pl.ds(pl.multiple_of(away(x, step) * 256, 256), 256)
        for block in range(8):
            at = (block % 2) * 64 + (block // 2) * 16
            out_ref[block * 16 : block * 16 + 16, :] = o_ref[at : at + 16, lanes].astype(BF16)
        out_ref[128:136, :] = st_ref[:, lanes].astype(BF16)


def combine(a_ref, b_ref, c_ref, d_ref, out_ref):
    parts = (a_ref, b_ref, c_ref, d_ref)
    tops, totals = [], []
    for part in parts:
        st = part[128:136, :].astype(F32)
        tops.append(st[0:1] + st[1:2] + st[2:3])
        totals.append(st[3:4] + st[4:5] + st[5:6])
    top = jnp.maximum(jnp.maximum(tops[0], tops[1]), jnp.maximum(tops[2], tops[3]))
    shares = [jnp.exp2(t - top) for t in tops]
    total = sum(w * t for w, t in zip(shares, totals))
    mixed = sum(p[0:128, :].astype(F32) * (w / total) for p, w in zip(parts, shares))
    out_ref[...] = mixed.astype(BF16)


def output_project(meta_ref, own_ref, other_ref, a0, a1, a2, a3, out_ref, o_ref, a_ref):
    x, c = meta_ref[1], meta_ref[2]
    for step, part in enumerate((a0, a1, a2, a3)):
        at = away(x, -step) * 128
        a_ref[rows_of(at, 128), :] = part[...]
        o_ref[rows_of(at + c * 64, 64), :] = own_ref[step]
        o_ref[rows_of(at + 64 - c * 64, 64), :] = other_ref[step]
    dims = (((0,), (0,)), ((), ()))
    r = lax.dot_general(o_ref[...], a_ref[...], dims, preferred_element_type=F32)
    out_ref[...] = r.astype(BF16).reshape(8, 128, 256)


def sum_output(in_ref, out_ref):
    total = in_ref[0].astype(F32)
    for j in range(1, 8):
        total = total + in_ref[j].astype(F32)
    out_ref[...] = total.astype(BF16)


def trade(block, axis):
    return lax.all_to_all(block, axis, split_axis=0, concat_axis=0, tiled=True)


def gather(block, axis):
    return lax.all_gather(block, axis, axis=0, tiled=False)


def send(block, step):
    if step == 0:
        return block
    return lax.ppermute(block, "x", [(i, (i + step) % 4) for i in range(4)])


def partner(block):
    return lax.ppermute(block, "c", [(0, 1), (1, 0)])


def layer(tokens, query_weight, key_weight, value_weight, output_weight, segments):
    z, x, c = lax.axis_index("z"), lax.axis_index("x"), lax.axis_index("c")
    place = lax.iota(jnp.int32, 4)
    meta = jnp.where(place == 0, z, jnp.where(place == 1, x, c))
    starts, first = pl.pallas_call(
        find_starts,
        out_shape=[shape(1, 256, dtype=jnp.int32), shape(1, dtype=jnp.int32)],
        in_specs=[pl.BlockSpec(memory_space=s) for s in (pltpu.SMEM, pltpu.VMEM)],
        out_specs=[pl.BlockSpec(memory_space=s) for s in (pltpu.VMEM, pltpu.SMEM)],
        scratch_shapes=[],
        compiler_params=pltpu.CompilerParams(vmem_limit_bytes=4 << 20),
    )(meta, segments.reshape(24, 256))
    own = trade(jnp.broadcast_to(tokens.T, (8, 64, 512)), "y").reshape(512, 512)
    packed = call(
        pack_weights, [shape(96, 1024)] * 4 + [shape(64, 1024)] * 4,
        meta, query_weight, key_weight, value_weight, output_weight, smem=(0,),
    )
    weights = [send(packed[i], i) for i in range(4)]
    o_own = jnp.stack([send(packed[4 + i], i) for i in range(4)])
    o_other = partner(o_own)
    other = partner(own)
    partial = call(
        project, [shape(384, 128)] * 4, meta, *weights, own, other, smem=(0,), limit=12,
        scratch=[
            pltpu.VMEM((1024, 512), BF16),
            pltpu.VMEM((384, 1024), BF16),
            pltpu.VMEM((384, 512), F32),
        ],
    )
    partial = [send(partial[i], i) for i in range(4)]
    queries, spread = call(sum_projection, [shape(256, 128), shape(12, 128, 128)], *partial)
    memory = trade(spread, "z")
    queries = gather(queries, ("x", "c"))
    memory = gather(memory, "c")
    mixed = call(
        attend, [shape(136, 256)] * 4, meta, first, starts, queries, memory,
        smem=(0, 1),
        limit=16,
        scratch=[
            pltpu.VMEM((128, 1024), BF16),
            pltpu.VMEM((12, 128, 1024), F32),
            pltpu.VMEM((8, 1024), F32),
            pltpu.VMEM((128, 1024), F32),
            pltpu.VMEM((8, 1024), F32),
        ],
    )
    mixed = [send(mixed[i], i) for i in range(4)]
    attended = call(combine, shape(128, 256), *mixed)
    attended = [send(attended, i) for i in range(4)]
    result = call(
        output_project, shape(8, 128, 256), meta, o_own, o_other, *attended, smem=(0,), limit=12,
        scratch=[pltpu.VMEM((512, 1024), BF16), pltpu.VMEM((512, 256), BF16)],
    )
    summed = call(sum_output, shape(128, 256), trade(result, "y"))
    final = call(take_columns, shape(64, 512), meta, gather(summed, "c"), smem=(0,))
    return final.T


def solution(mesh):
    grid = Mesh(mesh.devices.reshape(12, 8, 4, 2), ("z", "y", "x", "c"))
    head = ("y", "x", "c")
    placed = (P("z", head), P(head, None), P(head, None), P(head, None), P(head, None), P())
    return jax.shard_map(layer, mesh=grid, in_specs=placed, out_specs=P("z", head), check_vma=False)
```

time: 191 us -> 163 us (0.85)
  starting transfers between devices: 45.9 us -> 76.4 us
  blocking collectives: 78.9 us -> 57.5 us
  waiting for transfers between devices: 34.8 us -> 17.9 us
  Pallas kernels: 17.5 us -> 8.74 us
  local copies, waits for them, and re-layouts: 6.9 us -> 0.95 us
  other arithmetic: 3.31 us -> 0.07 us
  between operations: 2.74 us -> 0.35 us
    ppermute x0 -> x15, starting transfers between devices: none -> 47.6 us  [send(): return lax.ppermute(block, 'x', [(i, (i + step) % 4) for i in range(4)])]
    all_to_all x5 -> x1, waiting for transfers between devices: 33.2 us -> 0.01 us  [trade(): return lax.all_to_all(block, axis, split_axis=0, concat_axis=0, tiled=True)]
    all_to_all x5 -> x2, blocking collectives: 56.6 us -> 35.4 us  [trade(): return lax.all_to_all(block, axis, split_axis=0, concat_axis=0, tiled=True)]
    ppermute x0 -> x15, waiting for transfers between devices: none -> 17.9 us  [send(): return lax.ppermute(block, 'x', [(i, (i + step) % 4) for i in range(4)])]
    all_to_all x5 -> x1, starting transfers between devices: 27.7 us -> 14.9 us  [trade(): return lax.all_to_all(block, axis, split_axis=0, concat_axis=0, tiled=True)]
    pallas_call x8, Pallas kernels: 17.5 us -> 7.35 us  [call(): pl.pallas_call(body, out_shape=many, in_specs=specs, out_specs=[pl.BlockS...]
    ppermute x3 -> x2, starting transfers between devices: 18.2 us -> 13.9 us  [partner(): return lax.ppermute(block, 'c', [(0, 1), (1, 0)])]
    unnamed x22 -> x10, local copies, waits for them, and re-layouts: 3.28 us -> 0.02 us
  transfers between devices with their start and end apart: 8 -> 18, of which waited for: 5 -> 9; matrix products, arithmetic and copies ran while one was open for 2% -> 0% of each run, Pallas kernels for 3% -> 3%
where the time goes in v2:
time: 163 us; the launch traced here: 162 us
  starting transfers between devices  76.4 us (47%)
  blocking collectives  57.5 us (35%)
  waiting for transfers between devices  17.9 us (11%)
  Pallas kernels  8.74 us (5%)
    ppermute x15, starting transfers between devices, send(): return lax.ppermute(block, 'x', [(i, (i + step) % 4) for i in range(4)])  47.6 us
    all_to_all x2, blocking collectives, trade(): return lax.all_to_all(block, axis, split_axis=0, concat_axis=0, tiled=True)  35.4 us
    all_gather x3, blocking collectives, gather(): return lax.all_gather(block, axis, axis=0, tiled=False)  22.1 us
    ppermute x15, waiting for transfers between devices, send(): return lax.ppermute(block, 'x', [(i, (i + step) % 4) for i in range(4)])  17.9 us
    all_to_all x1, starting transfers between devices, trade(): return lax.all_to_all(block, axis, split_axis=0, concat_axis=0, tiled=True)  14.9 us
    ppermute x2, starting transfers between devices, partner(): return lax.ppermute(block, 'c', [(0, 1), (1, 0)])  13.9 us
    pallas_call x8, Pallas kernels, call(): pl.pallas_call(body, out_shape=many, in_specs=specs, out_specs=[pl.BlockS...  7.35 us
  transfers between devices with their start and end apart: 18, of which 9 were waited for; matrix products, arithmetic and copies ran while one was open for 0% of the time, Pallas kernels for 3%

profile of v2, /device:TPU:1, one launch (start us, length us, event | category | flops | bytes accessed | tf_op | source)
XLA Modules:
  0.0 161.9 jit_solution(4134944786460976409)
XLA Ops:
  1.0 19.8 %all_to_all.15 = bf16[8,64,512]{2,1,0:T(8,128)(2,1)S(1)} all-to-all(bf16[8,64,512]{2,1,0:T(8,128)(2,1)S(1)} %broadcast_in_dim.18), channel_id=1, replica_groups=mesh['z'=12,'y'=8,'x'=4,'c'=2] {'y'}, dimensions={0} | all-to-all | bytes 1048576 | tf_op jit(solution)/shard_map/all_to_all | solution.py:204
  20.7 8.4 %collective-permute-start.7 = (bf16[512,512]{1,0:T(8,128)(2,1)S(1)}, bf16[512,512]{1,0:T(8,128)(2,1)S(1)}, u32[]{:S(2)}, u32[]{:S(2)}) collective-permute-start(bf16[512,512]{1,0:T(8,128)(2,1)S(1)} %bitcast.12), channel_id=1, source_target_pairs={{0,1},{1,0},{2,3},{3,2},{4,5},{5,4},{6,7},{7,6},{8,9},{9,8},{10,11... | collective-permute-start | bytes 1572872 | tf_op jit(solution)/shard_map/ppermute | solution.py:218
  30.1 2.8 %collective-permute-start.4 = (bf16[96,1024]{1,0:T(8,128)(2,1)S(1)}, bf16[96,1024]{1,0:T(8,128)(2,1)S(1)}, u32[]{:S(2)}, u32[]{:S(2)}) collective-permute-start(bf16[96,1024]{1,0:T(8,128)(2,1)S(1)} %get-tuple-element.32), channel_id=1, source_target_pairs={{0,2},{2,4},{4,6},{6,0},{1,3},{3,5},{5,7},{7,1},{8,10},{10,12},{12... | collective-permute-start | bytes 589832 | tf_op jit(solution)/shard_map/ppermute | solution.py:214
  33.0 4.4 %collective-permute-start.5 = (bf16[96,1024]{1,0:T(8,128)(2,1)S(1)}, bf16[96,1024]{1,0:T(8,128)(2,1)S(1)}, u32[]{:S(2)}, u32[]{:S(2)}) collective-permute-start(bf16[96,1024]{1,0:T(8,128)(2,1)S(1)} %get-tuple-element.33), channel_id=1, source_target_pairs={{0,4},{2,6},{4,0},{6,2},{1,5},{3,7},{5,1},{7,3},{8,12},{10,14},{12... | collective-permute-start | bytes 589832 | tf_op jit(solution)/shard_map/ppermute | solution.py:214
  37.3 3.1 %collective-permute-start.6 = (bf16[96,1024]{1,0:T(8,128)(2,1)S(1)}, bf16[96,1024]{1,0:T(8,128)(2,1)S(1)}, u32[]{:S(2)}, u32[]{:S(2)}) collective-permute-start(bf16[96,1024]{1,0:T(8,128)(2,1)S(1)} %get-tuple-element.34), channel_id=1, source_target_pairs={{0,6},{2,0},{4,2},{6,4},{1,7},{3,1},{5,3},{7,5},{8,14},{10,8},{12,... | collective-permute-start | bytes 589832 | tf_op jit(solution)/shard_map/ppermute | solution.py:214
  40.4 4.2 %collective-permute-done.5.w2 = bf16[96,1024]{1,0:T(8,128)(2,1)S(1)} collective-permute-done((bf16[96,1024]{1,0:T(8,128)(2,1)S(1)}, bf16[96,1024]{1,0:T(8,128)(2,1)S(1)}, u32[]{:S(2)}, u32[]{:S(2)}) %collective-permute-start.5) | collective-permute-done | bytes 196640 | tf_op jit(solution)/shard_map/ppermute | solution.py:214
  44.6 1.6 collective-permute-done.6.w3
  46.1 1.3 shard_map.66
  47.4 4.5 %collective-permute-start.10 = (bf16[384,128]{1,0:T(8,128)(2,1)S(1)}, bf16[384,128]{1,0:T(8,128)(2,1)S(1)}, u32[]{:S(2)}, u32[]{:S(2)}) collective-permute-start(bf16[384,128]{1,0:T(8,128)(2,1)S(1)} %get-tuple-element.38), channel_id=1, source_target_pairs={{0,6},{2,0},{4,2},{6,4},{1,7},{3,1},{5,3},{7,5},{8,14},{10,8},{12,... | collective-permute-start | bytes 294920 | tf_op jit(solution)/shard_map/ppermute | solution.py:214
  52.0 1.9 %collective-permute-start.8 = (bf16[384,128]{1,0:T(8,128)(2,1)S(1)}, bf16[384,128]{1,0:T(8,128)(2,1)S(1)}, u32[]{:S(2)}, u32[]{:S(2)}) collective-permute-start(bf16[384,128]{1,0:T(8,128)(2,1)S(1)} %get-tuple-element.36), channel_id=1, source_target_pairs={{0,2},{2,4},{4,6},{6,0},{1,3},{3,5},{5,7},{7,1},{8,10},{10,12},{12... | collective-permute-start | bytes 294920 | tf_op jit(solution)/shard_map/ppermute | solution.py:214
  53.9 3.6 %collective-permute-start.9 = (bf16[384,128]{1,0:T(8,128)(2,1)S(1)}, bf16[384,128]{1,0:T(8,128)(2,1)S(1)}, u32[]{:S(2)}, u32[]{:S(2)}) collective-permute-start(bf16[384,128]{1,0:T(8,128)(2,1)S(1)} %get-tuple-element.37), channel_id=1, source_target_pairs={{0,4},{2,6},{4,0},{6,2},{1,5},{3,7},{5,1},{7,3},{8,12},{10,14},{12... | collective-permute-start | bytes 294920 | tf_op jit(solution)/shard_map/ppermute | solution.py:214
  58.5 2.3 %collective-permute-done.9.c_ref = bf16[384,128]{1,0:T(8,128)(2,1)S(1)} collective-permute-done((bf16[384,128]{1,0:T(8,128)(2,1)S(1)}, bf16[384,128]{1,0:T(8,128)(2,1)S(1)}, u32[]{:S(2)}, u32[]{:S(2)}) %collective-permute-start.9) | collective-permute-done | bytes 98336 | tf_op jit(solution)/shard_map/ppermute | solution.py:214
  61.7 14.9 %all-to-all-start.1 = ((bf16[12,128,128]{2,1,0:T(8,128)(2,1)}), bf16[12,128,128]{2,1,0:T(8,128)(2,1)S(1)}, u32[]{:S(2)}, u32[]{:S(2)}) async-start(bf16[12,128,128]{2,1,0:T(8,128)(2,1)} %get-tuple-element.40), calls=%async_computation.1 | async-start | bytes 786432 | tf_op jit(solution)/shard_map/all_to_all | solution.py:204
  76.5 3.3 %collective-permute-start = (bf16[64,1024]{1,0:T(8,128)(2,1)S(1)}, bf16[64,1024]{1,0:T(8,128)(2,1)S(1)}, u32[]{:S(2)}, u32[]{:S(2)}) collective-permute-start(bf16[64,1024]{1,0:T(8,128)(2,1)S(1)} %get-tuple-element.26), channel_id=1, source_target_pairs={{0,2},{2,4},{4,6},{6,0},{1,3},{3,5},{5,7},{7,1},{8,10},{10,12},{12... | collective-permute-start | bytes 393224 | tf_op jit(solution)/shard_map/ppermute | solution.py:214
  79.8 4.1 %collective-permute-start.1 = (bf16[64,1024]{1,0:T(8,128)(2,1)S(1)}, bf16[64,1024]{1,0:T(8,128)(2,1)S(1)}, u32[]{:S(2)}, u32[]{:S(2)}) collective-permute-start(bf16[64,1024]{1,0:T(8,128)(2,1)S(1)} %get-tuple-element.27), channel_id=1, source_target_pairs={{0,4},{2,6},{4,0},{6,2},{1,5},{3,7},{5,1},{7,3},{8,12},{10,14},{12... | collective-permute-start | bytes 393224 | tf_op jit(solution)/shard_map/ppermute | solution.py:214
  83.9 2.1 %collective-permute-start.2 = (bf16[64,1024]{1,0:T(8,128)(2,1)S(1)}, bf16[64,1024]{1,0:T(8,128)(2,1)S(1)}, u32[]{:S(2)}, u32[]{:S(2)}) collective-permute-start(bf16[64,1024]{1,0:T(8,128)(2,1)S(1)} %get-tuple-element.28), channel_id=1, source_target_pairs={{0,6},{2,0},{4,2},{6,4},{1,7},{3,1},{5,3},{7,5},{8,14},{10,8},{12,... | collective-permute-start | bytes 393224 | tf_op jit(solution)/shard_map/ppermute | solution.py:214
  86.1 1.4 shard_map.65
  88.0 2.7 %collective-permute-done.2 = bf16[64,1024]{1,0:T(8,128)(2,1)S(1)} collective-permute-done((bf16[64,1024]{1,0:T(8,128)(2,1)S(1)}, bf16[64,1024]{1,0:T(8,128)(2,1)S(1)}, u32[]{:S(2)}, u32[]{:S(2)}) %collective-permute-start.2) | collective-permute-done | bytes 131104 | tf_op jit(solution)/shard_map/ppermute | solution.py:214
  90.8 5.4 %collective-permute-start.3 = (bf16[4,64,1024]{2,1,0:T(8,128)(2,1)S(1)}, bf16[4,64,1024]{2,1,0:T(8,128)(2,1)S(1)}, u32[]{:S(2)}, u32[]{:S(2)}) collective-permute-start(bf16[4,64,1024]{2,1,0:T(8,128)(2,1)S(1)} %pad_maximum_fusion.own_ref), channel_id=1, source_target_pairs={{0,1},{1,0},{2,3},{3,2},{4,5},{5,4},{6,7},{7,6},{8,9},{9,8},{10,11... | collective-permute-start | bytes 1572872 | tf_op jit(solution)/shard_map/ppermute | solution.py:218
  96.3 13.0 %all-gather = bf16[2048,128]{1,0:T(8,128)(2,1)S(1)} all-gather(bf16[256,128]{1,0:T(8,128)(2,1)S(1)} %get-tuple-element.39), channel_id=2, replica_groups=mesh['z'=12,'y'=8,'x'=4,'c'=2] {'x','c'}, dimensions={0}, use_global_device_ids=true | all-gather | bytes 589824 | tf_op jit(solution)/shard_map/all_gather | solution.py:208
  109.2 2.4 %all-gather.1 = bf16[24,128,128]{2,1,0:T(8,128)(2,1)S(1)} all-gather(bf16[12,128,128]{2,1,0:T(8,128)(2,1)S(1)} %all-to-all-done.1), channel_id=3, replica_groups=mesh['z'=12,'y'=8,'x'=4,'c'=2] {'c'}, dimensions={0}, use_global_device_ids=true | all-gather | bytes 1179648 | tf_op jit(solution)/shard_map/all_gather | solution.py:208
  111.6 1.9 %shard_map.68 = (bf16[136,256]{1,0:T(8,128)(2,1)S(1)}, bf16[136,256]{1,0:T(8,128)(2,1)S(1)}, bf16[136,256]{1,0:T(8,128)(2,1)S(1)}, bf16[136,256]{1,0:T(8,128)(2,1)S(1)}) custom-call(s32[4]{0:T(128)S(1)} %compare_select_fusion.1.meta_ref, s32[1]{0:T(128)} %get-tuple-element.29.first_ref, s32[1,256]{1,0:T(1,128)S(1)} %get-tuple-element.30.start_ref, ...), custom_call_target="tpu_custom_call" | custom-call | tf_op jit(solution)/shard_map/pallas_call | solution.py:25
  113.5 2.0 %collective-permute-start.11 = (bf16[136,256]{1,0:T(8,128)(2,1)S(1)}, bf16[136,256]{1,0:T(8,128)(2,1)S(1)}, u32[]{:S(2)}, u32[]{:S(2)}) collective-permute-start(bf16[136,256]{1,0:T(8,128)(2,1)S(1)} %get-tuple-element.42), channel_id=1, source_target_pairs={{0,2},{2,4},{4,6},{6,0},{1,3},{3,5},{5,7},{7,1},{8,10},{10,12},{12... | collective-permute-start | bytes 208904 | tf_op jit(solution)/shard_map/ppermute | solution.py:214
  115.5 4.3 %collective-permute-start.12 = (bf16[136,256]{1,0:T(8,128)(2,1)S(1)}, bf16[136,256]{1,0:T(8,128)(2,1)S(1)}, u32[]{:S(2)}, u32[]{:S(2)}) collective-permute-start(bf16[136,256]{1,0:T(8,128)(2,1)S(1)} %get-tuple-element.43), channel_id=1, source_target_pairs={{0,4},{2,6},{4,0},{6,2},{1,5},{3,7},{5,1},{7,3},{8,12},{10,14},{12... | collective-permute-start | bytes 208904 | tf_op jit(solution)/shard_map/ppermute | solution.py:214
  119.8 2.7 %collective-permute-start.13 = (bf16[136,256]{1,0:T(8,128)(2,1)S(1)}, bf16[136,256]{1,0:T(8,128)(2,1)S(1)}, u32[]{:S(2)}, u32[]{:S(2)}) collective-permute-start(bf16[136,256]{1,0:T(8,128)(2,1)S(1)} %get-tuple-element.44), channel_id=1, source_target_pairs={{0,6},{2,0},{4,2},{6,4},{1,7},{3,1},{5,3},{7,5},{8,14},{10,8},{12,... | collective-permute-start | bytes 208904 | tf_op jit(solution)/shard_map/ppermute | solution.py:214
  122.5 2.3 %collective-permute-done.13.d_ref = bf16[136,256]{1,0:T(8,128)(2,1)S(1)} collective-permute-done((bf16[136,256]{1,0:T(8,128)(2,1)S(1)}, bf16[136,256]{1,0:T(8,128)(2,1)S(1)}, u32[]{:S(2)}, u32[]{:S(2)}) %collective-permute-start.13) | collective-permute-done | bytes 69664 | tf_op jit(solution)/shard_map/ppermute | solution.py:214
  124.9 2.7 %collective-permute-start.14 = (bf16[128,256]{1,0:T(8,128)(2,1)S(1)}, bf16[128,256]{1,0:T(8,128)(2,1)S(1)}, u32[]{:S(2)}, u32[]{:S(2)}) collective-permute-start(bf16[128,256]{1,0:T(8,128)(2,1)S(1)} %shard_map.69.a0), channel_id=1, source_target_pairs={{0,2},{2,4},{4,6},{6,0},{1,3},{3,5},{5,7},{7,1},{8,10},{10,12},{12... | collective-permute-start | bytes 196616 | tf_op jit(solution)/shard_map/ppermute | solution.py:214
  127.6 4.3 %collective-permute-start.15 = (bf16[128,256]{1,0:T(8,128)(2,1)S(1)}, bf16[128,256]{1,0:T(8,128)(2,1)S(1)}, u32[]{:S(2)}, u32[]{:S(2)}) collective-permute-start(bf16[128,256]{1,0:T(8,128)(2,1)S(1)} %shard_map.69.a0), channel_id=1, source_target_pairs={{0,4},{2,6},{4,0},{6,2},{1,5},{3,7},{5,1},{7,3},{8,12},{10,14},{12... | collective-permute-start | bytes 196616 | tf_op jit(solution)/shard_map/ppermute | solution.py:214
  132.0 1.9 %collective-permute-start.16 = (bf16[128,256]{1,0:T(8,128)(2,1)S(1)}, bf16[128,256]{1,0:T(8,128)(2,1)S(1)}, u32[]{:S(2)}, u32[]{:S(2)}) collective-permute-start(bf16[128,256]{1,0:T(8,128)(2,1)S(1)} %shard_map.69.a0), channel_id=1, source_target_pairs={{0,6},{2,0},{4,2},{6,4},{1,7},{3,1},{5,3},{7,5},{8,14},{10,8},{12,... | collective-permute-start | bytes 196616 | tf_op jit(solution)/shard_map/ppermute | solution.py:214
  134.7 2.4 %collective-permute-done.16.a3 = bf16[128,256]{1,0:T(8,128)(2,1)S(1)} collective-permute-done((bf16[128,256]{1,0:T(8,128)(2,1)S(1)}, bf16[128,256]{1,0:T(8,128)(2,1)S(1)}, u32[]{:S(2)}, u32[]{:S(2)}) %collective-permute-start.16) | collective-permute-done | bytes 65568 | tf_op jit(solution)/shard_map/ppermute | solution.py:214
  138.2 15.6 %all_to_all.16.in_ref = bf16[8,128,256]{2,1,0:T(8,128)(2,1)S(1)} all-to-all(bf16[8,128,256]{2,1,0:T(8,128)(2,1)S(1)} %shard_map.70), channel_id=1, replica_groups=mesh['z'=12,'y'=8,'x'=4,'c'=2] {'y'}, dimensions={0} | all-to-all | bytes 1048576 | tf_op jit(solution)/shard_map/all_to_all | solution.py:204
  153.9 6.8 %all-gather.2 = bf16[256,256]{1,0:T(8,128)(2,1)S(1)} all-gather(bf16[128,256]{1,0:T(8,128)(2,1)S(1)} %shard_map.71), channel_id=4, replica_groups=mesh['z'=12,'y'=8,'x'=4,'c'=2] {'c'}, dimensions={0}, use_global_device_ids=true | all-gather | bytes 196608 | tf_op jit(solution)/shard_map/all_gather | solution.py:208
  (32 shorter events, 7.6 us)
Async XLA Ops:
  0.0 29.2 %copy-start.2 = (bf16[16,4096]{1,0:T(8,128)(2,1)S(1)}, bf16[16,4096]{1,0:T(8,128)(2,1)}, u32[]{:S(2)}) copy-start(bf16[16,4096]{1,0:T(8,128)(2,1)} %k_ref.1) | copy-start | bytes 393220
  0.0 29.2 %copy-start.3 = (bf16[16,4096]{1,0:T(8,128)(2,1)S(1)}, bf16[16,4096]{1,0:T(8,128)(2,1)}, u32[]{:S(2)}) copy-start(bf16[16,4096]{1,0:T(8,128)(2,1)} %v_ref.1) | copy-start | bytes 393220
  0.9 28.3 %copy-start = (bf16[64,4096]{1,0:T(8,128)(2,1)S(1)}, bf16[64,4096]{1,0:T(8,128)(2,1)}, u32[]{:S(2)}) copy-start(bf16[64,4096]{1,0:T(8,128)(2,1)} %q_ref.1) | copy-start | bytes 1572868
  0.9 28.3 %copy-start.1 = (bf16[64,4096]{1,0:T(8,128)(2,1)S(1)}, bf16[64,4096]{1,0:T(8,128)(2,1)}, u32[]{:S(2)}) copy-start(bf16[64,4096]{1,0:T(8,128)(2,1)} %o_ref.1) | copy-start | bytes 1572868
  20.7 25.4 %collective-permute-start.7 = (bf16[512,512]{1,0:T(8,128)(2,1)S(1)}, bf16[512,512]{1,0:T(8,128)(2,1)S(1)}, u32[]{:S(2)}, u32[]{:S(2)}) collective-permute-start(bf16[512,512]{1,0:T(8,128)(2,1)S(1)} %bitcast.12), channel_id=1, source_target_pairs={{0,1},{1,0},{2,3},{3,2},{4,5},{5,4},{6,7},{7,6},{8,9},{9,8},{10,11... | collective-permute-start | bytes 1572872 | tf_op jit(solution)/shard_map/ppermute | solution.py:218
  30.1 10.3 %collective-permute-start.4 = (bf16[96,1024]{1,0:T(8,128)(2,1)S(1)}, bf16[96,1024]{1,0:T(8,128)(2,1)S(1)}, u32[]{:S(2)}, u32[]{:S(2)}) collective-permute-start(bf16[96,1024]{1,0:T(8,128)(2,1)S(1)} %get-tuple-element.32), channel_id=1, source_target_pairs={{0,2},{2,4},{4,6},{6,0},{1,3},{3,5},{5,7},{7,1},{8,10},{10,12},{12... | collective-permute-start | bytes 589832 | tf_op jit(solution)/shard_map/ppermute | solution.py:214
  33.0 11.6 %collective-permute-start.5 = (bf16[96,1024]{1,0:T(8,128)(2,1)S(1)}, bf16[96,1024]{1,0:T(8,128)(2,1)S(1)}, u32[]{:S(2)}, u32[]{:S(2)}) collective-permute-start(bf16[96,1024]{1,0:T(8,128)(2,1)S(1)} %get-tuple-element.33), channel_id=1, source_target_pairs={{0,4},{2,6},{4,0},{6,2},{1,5},{3,7},{5,1},{7,3},{8,12},{10,14},{12... | collective-permute-start | bytes 589832 | tf_op jit(solution)/shard_map/ppermute | solution.py:214
  37.3 8.8 %collective-permute-start.6 = (bf16[96,1024]{1,0:T(8,128)(2,1)S(1)}, bf16[96,1024]{1,0:T(8,128)(2,1)S(1)}, u32[]{:S(2)}, u32[]{:S(2)}) collective-permute-start(bf16[96,1024]{1,0:T(8,128)(2,1)S(1)} %get-tuple-element.34), channel_id=1, source_target_pairs={{0,6},{2,0},{4,2},{6,4},{1,7},{3,1},{5,3},{7,5},{8,14},{10,8},{12,... | collective-permute-start | bytes 589832 | tf_op jit(solution)/shard_map/ppermute | solution.py:214
  47.4 10.0 %collective-permute-start.10 = (bf16[384,128]{1,0:T(8,128)(2,1)S(1)}, bf16[384,128]{1,0:T(8,128)(2,1)S(1)}, u32[]{:S(2)}, u32[]{:S(2)}) collective-permute-start(bf16[384,128]{1,0:T(8,128)(2,1)S(1)} %get-tuple-element.38), channel_id=1, source_target_pairs={{0,6},{2,0},{4,2},{6,4},{1,7},{3,1},{5,3},{7,5},{8,14},{10,8},{12,... | collective-permute-start | bytes 294920 | tf_op jit(solution)/shard_map/ppermute | solution.py:214
  52.0 6.6 %collective-permute-start.8 = (bf16[384,128]{1,0:T(8,128)(2,1)S(1)}, bf16[384,128]{1,0:T(8,128)(2,1)S(1)}, u32[]{:S(2)}, u32[]{:S(2)}) collective-permute-start(bf16[384,128]{1,0:T(8,128)(2,1)S(1)} %get-tuple-element.36), channel_id=1, source_target_pairs={{0,2},{2,4},{4,6},{6,0},{1,3},{3,5},{5,7},{7,1},{8,10},{10,12},{12... | collective-permute-start | bytes 294920 | tf_op jit(solution)/shard_map/ppermute | solution.py:214
  53.9 7.0 %collective-permute-start.9 = (bf16[384,128]{1,0:T(8,128)(2,1)S(1)}, bf16[384,128]{1,0:T(8,128)(2,1)S(1)}, u32[]{:S(2)}, u32[]{:S(2)}) collective-permute-start(bf16[384,128]{1,0:T(8,128)(2,1)S(1)} %get-tuple-element.37), channel_id=1, source_target_pairs={{0,4},{2,6},{4,0},{6,2},{1,5},{3,7},{5,1},{7,3},{8,12},{10,14},{12... | collective-permute-start | bytes 294920 | tf_op jit(solution)/shard_map/ppermute | solution.py:214
  61.7 24.4 %copy-start.4 = (s32[6144]{0:T(1024)S(1)}, s32[6144]{0:T(1024)}, u32[]{:S(2)}) copy-start(s32[6144]{0:T(1024)} %param.11) | copy-start | bytes 73732
  61.7 47.6 %all-to-all-start.1 = ((bf16[12,128,128]{2,1,0:T(8,128)(2,1)}), bf16[12,128,128]{2,1,0:T(8,128)(2,1)S(1)}, u32[]{:S(2)}, u32[]{:S(2)}) async-start(bf16[12,128,128]{2,1,0:T(8,128)(2,1)} %get-tuple-element.40), calls=%async_computation.1 | async-start | bytes 786432 | tf_op jit(solution)/shard_map/all_to_all | solution.py:204
  76.5 10.9 %collective-permute-start = (bf16[64,1024]{1,0:T(8,128)(2,1)S(1)}, bf16[64,1024]{1,0:T(8,128)(2,1)S(1)}, u32[]{:S(2)}, u32[]{:S(2)}) collective-permute-start(bf16[64,1024]{1,0:T(8,128)(2,1)S(1)} %get-tuple-element.26), channel_id=1, source_target_pairs={{0,2},{2,4},{4,6},{6,0},{1,3},{3,5},{5,7},{7,1},{8,10},{10,12},{12... | collective-permute-start | bytes 393224 | tf_op jit(solution)/shard_map/ppermute | solution.py:214
  79.8 8.2 %collective-permute-start.1 = (bf16[64,1024]{1,0:T(8,128)(2,1)S(1)}, bf16[64,1024]{1,0:T(8,128)(2,1)S(1)}, u32[]{:S(2)}, u32[]{:S(2)}) collective-permute-start(bf16[64,1024]{1,0:T(8,128)(2,1)S(1)} %get-tuple-element.27), channel_id=1, source_target_pairs={{0,4},{2,6},{4,0},{6,2},{1,5},{3,7},{5,1},{7,3},{8,12},{10,14},{12... | collective-permute-start | bytes 393224 | tf_op jit(solution)/shard_map/ppermute | solution.py:214
  83.9 6.9 %collective-permute-start.2 = (bf16[64,1024]{1,0:T(8,128)(2,1)S(1)}, bf16[64,1024]{1,0:T(8,128)(2,1)S(1)}, u32[]{:S(2)}, u32[]{:S(2)}) collective-permute-start(bf16[64,1024]{1,0:T(8,128)(2,1)S(1)} %get-tuple-element.28), channel_id=1, source_target_pairs={{0,6},{2,0},{4,2},{6,4},{1,7},{3,1},{5,3},{7,5},{8,14},{10,8},{12,... | collective-permute-start | bytes 393224 | tf_op jit(solution)/shard_map/ppermute | solution.py:214
  90.8 43.1 %collective-permute-start.3 = (bf16[4,64,1024]{2,1,0:T(8,128)(2,1)S(1)}, bf16[4,64,1024]{2,1,0:T(8,128)(2,1)S(1)}, u32[]{:S(2)}, u32[]{:S(2)}) collective-permute-start(bf16[4,64,1024]{2,1,0:T(8,128)(2,1)S(1)} %pad_maximum_fusion.own_ref), channel_id=1, source_target_pairs={{0,1},{1,0},{2,3},{3,2},{4,5},{5,4},{6,7},{7,6},{8,9},{9,8},{10,11... | collective-permute-start | bytes 1572872 | tf_op jit(solution)/shard_map/ppermute | solution.py:218
  113.5 9.0 %collective-permute-start.11 = (bf16[136,256]{1,0:T(8,128)(2,1)S(1)}, bf16[136,256]{1,0:T(8,128)(2,1)S(1)}, u32[]{:S(2)}, u32[]{:S(2)}) collective-permute-start(bf16[136,256]{1,0:T(8,128)(2,1)S(1)} %get-tuple-element.42), channel_id=1, source_target_pairs={{0,2},{2,4},{4,6},{6,0},{1,3},{3,5},{5,7},{7,1},{8,10},{10,12},{12... | collective-permute-start | bytes 208904 | tf_op jit(solution)/shard_map/ppermute | solution.py:214
  115.5 7.0 %collective-permute-start.12 = (bf16[136,256]{1,0:T(8,128)(2,1)S(1)}, bf16[136,256]{1,0:T(8,128)(2,1)S(1)}, u32[]{:S(2)}, u32[]{:S(2)}) collective-permute-start(bf16[136,256]{1,0:T(8,128)(2,1)S(1)} %get-tuple-element.43), channel_id=1, source_target_pairs={{0,4},{2,6},{4,0},{6,2},{1,5},{3,7},{5,1},{7,3},{8,12},{10,14},{12... | collective-permute-start | bytes 208904 | tf_op jit(solution)/shard_map/ppermute | solution.py:214
  119.8 5.1 %collective-permute-start.13 = (bf16[136,256]{1,0:T(8,128)(2,1)S(1)}, bf16[136,256]{1,0:T(8,128)(2,1)S(1)}, u32[]{:S(2)}, u32[]{:S(2)}) collective-permute-start(bf16[136,256]{1,0:T(8,128)(2,1)S(1)} %get-tuple-element.44), channel_id=1, source_target_pairs={{0,6},{2,0},{4,2},{6,4},{1,7},{3,1},{5,3},{7,5},{8,14},{10,8},{12,... | collective-permute-start | bytes 208904 | tf_op jit(solution)/shard_map/ppermute | solution.py:214
  124.9 9.0 %collective-permute-start.14 = (bf16[128,256]{1,0:T(8,128)(2,1)S(1)}, bf16[128,256]{1,0:T(8,128)(2,1)S(1)}, u32[]{:S(2)}, u32[]{:S(2)}) collective-permute-start(bf16[128,256]{1,0:T(8,128)(2,1)S(1)} %shard_map.69.a0), channel_id=1, source_target_pairs={{0,2},{2,4},{4,6},{6,0},{1,3},{3,5},{5,7},{7,1},{8,10},{10,12},{12... | collective-permute-start | bytes 196616 | tf_op jit(solution)/shard_map/ppermute | solution.py:214
  127.6 7.1 %collective-permute-start.15 = (bf16[128,256]{1,0:T(8,128)(2,1)S(1)}, bf16[128,256]{1,0:T(8,128)(2,1)S(1)}, u32[]{:S(2)}, u32[]{:S(2)}) collective-permute-start(bf16[128,256]{1,0:T(8,128)(2,1)S(1)} %shard_map.69.a0), channel_id=1, source_target_pairs={{0,4},{2,6},{4,0},{6,2},{1,5},{3,7},{5,1},{7,3},{8,12},{10,14},{12... | collective-permute-start | bytes 196616 | tf_op jit(solution)/shard_map/ppermute | solution.py:214
  132.0 5.1 %collective-permute-start.16 = (bf16[128,256]{1,0:T(8,128)(2,1)S(1)}, bf16[128,256]{1,0:T(8,128)(2,1)S(1)}, u32[]{:S(2)}, u32[]{:S(2)}) collective-permute-start(bf16[128,256]{1,0:T(8,128)(2,1)S(1)} %shard_map.69.a0), channel_id=1, source_target_pairs={{0,6},{2,0},{4,2},{6,4},{1,7},{3,1},{5,3},{7,5},{8,14},{10,8},{12,... | collective-permute-start | bytes 196616 | tf_op jit(solution)/shard_map/ppermute | solution.py:214

commit v3 on v2

v3 whole, which is shorter than its diff:
```python
import math

import jax
import jax.numpy as jnp
from jax import lax
from jax.experimental import pallas as pl
from jax.experimental.pallas import tpu as pltpu
from jax.sharding import Mesh, PartitionSpec as P


DIM = 128
F32 = jnp.float32
BF16 = jnp.bfloat16
NEG = -1e30
FLOOR = -1e28


def call(body, outs, *args, smem=(), scratch=(), limit=8):
    specs = [
        pl.BlockSpec(memory_space=pltpu.SMEM if i in smem else pltpu.VMEM)
        for i in range(len(args))
    ]
    single = not isinstance(outs, (list, tuple))
    many = [outs] if single else list(outs)
    out = pl.pallas_call(
        body,
        out_shape=many,
        in_specs=specs,
        out_specs=[pl.BlockSpec(memory_space=pltpu.VMEM)] * len(many),
        scratch_shapes=list(scratch),
        compiler_params=pltpu.CompilerParams(vmem_limit_bytes=limit << 20),
    )(*args)
    return out[0] if single else out


def shape(*dims, dtype=BF16):
    return jax.ShapeDtypeStruct(dims, dtype)


def find_starts(meta_ref, seg_ref, start_ref, first_ref):
    at = meta_ref[0] * 2 + meta_ref[2]
    window = seg_ref[pl.ds(at, 1), :]
    lane = lax.broadcasted_iota(jnp.int32, (1, 256), 1)
    head = jnp.min(window)
    begin = jnp.sum((seg_ref[...] < head).astype(jnp.int32))
    changed = (lane > 0) & (window != pltpu.roll(window, 1, 1))
    starts = jnp.where(changed, at * 256 + lane, begin)
    for bit in range(8):
        moved = pltpu.roll(starts, 1 << bit, 1)
        starts = jnp.maximum(starts, jnp.where(lane >= 1 << bit, moved, 0))
    start_ref[...] = starts
    first_ref[0] = begin
    first_ref[1] = jnp.max(starts)


def away(x, step):
    return (x + step) & 3


def pack_weights(meta_ref, q_ref, k_ref, v_ref, o_ref, *outs):
    for step, out_ref in enumerate(outs):
        x = away(meta_ref[1], step)
        for y in range(8):
            src = pl.ds(pl.multiple_of((y * 4 + x) * 128, 128), 128)
            dst = slice(y * 128, (y + 1) * 128)
            out_ref[0:64, dst] = q_ref[:, src]
            out_ref[64:80, dst] = k_ref[:, src]
            out_ref[80:96, dst] = v_ref[:, src]
            out_ref[96:160, dst] = o_ref[:, src]


def rows_of(start, size):
    return pl.ds(pl.multiple_of(start, size), size)


def project(meta_ref, w0, w1, w2, w3, own_ref, other_ref, out_ref, o_ref, x_ref, all_ref, y_ref):
    x, c = meta_ref[1], meta_ref[2]
    for y in range(8):
        x_ref[rows_of(y * 128 + c * 64, 64), :] = own_ref[y * 64 : (y + 1) * 64, :]
        x_ref[rows_of(y * 128 + 64 - c * 64, 64), :] = other_ref[y * 64 : (y + 1) * 64, :]
    for step, w in enumerate((w0, w1, w2, w3)):
        all_ref[pl.ds(pl.multiple_of(away(x, -step) * 96, 32), 96), :] = w[0:96, :]
        o_ref[step] = w[96:160, :]
    y_ref[...] = jnp.dot(all_ref[...], x_ref[...], preferred_element_type=F32).astype(BF16)
    for j in range(4):
        for t in range(4):
            lanes = slice(t * 128, (t + 1) * 128)
            at = (t % 2) * 64
            out_ref[j * 2 + t // 2, at : at + 64, :] = y_ref[j * 96 : j * 96 + 64, lanes]
            at = 128 + j * 16
            out_ref[t * 2, at : at + 16, :] = y_ref[j * 96 + 64 : j * 96 + 80, lanes]
            out_ref[t * 2 + 1, at : at + 16, :] = y_ref[j * 96 + 80 : j * 96 + 96, lanes]


def sum_projection(in_ref, q_ref, kv_ref):
    for half in range(2):
        total = in_ref[half].astype(F32)
        for j in range(1, 4):
            total = total + in_ref[j * 2 + half].astype(F32)
        total = total.astype(BF16)
        rows = slice(half * 64, half * 64 + 64)
        for t in range(2):
            q_ref[t, rows, :] = total[t * 64 : t * 64 + 64]
        for j in range(12):
            kv_ref[j, rows, :] = total[128:192]


def split3(value):
    high = value.astype(BF16)
    rest = value - high.astype(F32)
    mid = rest.astype(BF16)
    low = (rest - mid.astype(F32)).astype(BF16)
    return high, mid, low


def attend(meta_ref, first_ref, start_ref, q_ref, kv_ref, out_ref, qs_ref, s_ref, m_ref, l_ref, o_ref):
    z, x, c = meta_ref[0], meta_ref[1], meta_ref[2]
    first, latest = first_ref[0] >> 9, first_ref[1]
    for block in range(8):
        to = (block % 2) * 64 + (block // 2) * 16
        for h in range(4):
            for t in range(2):
                lanes = slice((h * 2 + t) * 128, (h * 2 + t + 1) * 128)
                qs_ref[to : to + 16, lanes] = q_ref[h, t, block * 16 : block * 16 + 16, :]
    factor = math.log2(math.e) / math.sqrt(DIM)
    m_ref[...] = jnp.full((8, 1024), FLOOR, F32)
    l_ref[...] = jnp.zeros((8, 1024), F32)
    o_ref[...] = jnp.zeros((128, 1024), F32)
    heads = [slice(h * 256, (h + 1) * 256) for h in range(4)]
    pairs = (z - first + 2) >> 1

    def tile(which, i):
        j = first + 2 * i
        return jnp.concatenate([kv_ref[which, j], kv_ref[which, jnp.minimum(j + 1, 11)]], axis=1)

    def score(i, unused):
        j = first + 2 * i
        key = tile(0, i).astype(F32).T.astype(BF16)

        def note(s, lanes):
            s_ref[i, :, lanes] = s
            m_ref[:, lanes] = jnp.maximum(m_ref[:, lanes], jnp.max(s.reshape(32, 8, 256), axis=0))

        inside = (j * 512 >= latest) & (j + 1 < z)

        @pl.when(inside)
        def _():
            for lanes in heads:
                note(jnp.dot(key, qs_ref[:, lanes], preferred_element_type=F32) * factor, lanes)

        @pl.when(jnp.logical_not(inside))
        def _():
            row = lax.broadcasted_iota(jnp.int32, (256, 256), 0)
            place = j * 512 + (row >> 7) * 512 + x * 128 + (row & 127)
            query = z * 512 + c * 256 + lax.broadcasted_iota(jnp.int32, (256, 256), 1)
            allowed = (place >= start_ref[...]) & (place <= query)
            for lanes in heads:
                s = jnp.dot(key, qs_ref[:, lanes], preferred_element_type=F32) * factor
                note(jnp.where(allowed, s, NEG), lanes)

        return unused

    lax.fori_loop(0, pairs, score, 0)
    top = jnp.max(m_ref[...], axis=0, keepdims=True)

    def mix(i, unused):
        val = tile(1, i)
        for lanes in heads:
            p = jnp.exp2(s_ref[i, :, lanes] - top[:, lanes])
            l_ref[:, lanes] += jnp.sum(p.reshape(32, 8, 256), axis=0)
            o_ref[:, lanes] += jnp.dot(val, p.astype(BF16), preferred_element_type=F32)
        return unused

    lax.fori_loop(0, pairs, mix, 0)
    total = jnp.sum(l_ref[...], axis=0, keepdims=True)
    stats = [v.astype(F32) for v in split3(top) + split3(total)]
    stats = jnp.concatenate(stats + [jnp.zeros((2, 1024), F32)], axis=0)
    for h, lanes in enumerate(heads):
        for block in range(8):
            at = (block % 2) * 64 + (block // 2) * 16
            out_ref[h, block * 16 : block * 16 + 16, :] = o_ref[at : at + 16, lanes].astype(BF16)
        out_ref[h, 128:136, :] = stats[:, lanes].astype(BF16)


def combine(in_ref, out_ref):
    tops, totals = [], []
    for j in range(4):
        st = in_ref[j, 128:136, :].astype(F32)
        tops.append(st[0:1] + st[1:2] + st[2:3])
        totals.append(st[3:4] + st[4:5] + st[5:6])
    top = jnp.maximum(jnp.maximum(tops[0], tops[1]), jnp.maximum(tops[2], tops[3]))
    shares = [jnp.exp2(t - top) for t in tops]
    total = sum(w * t for w, t in zip(shares, totals))
    mixed = sum(in_ref[j, 0:128, :].astype(F32) * (shares[j] / total) for j in range(4))
    mixed = mixed.astype(BF16)
    for j in range(4):
        out_ref[j] = mixed


def output_project(meta_ref, own_ref, other_ref, a_ref, out_ref, o_ref):
    x, c = meta_ref[1], meta_ref[2]
    for step in range(4):
        at = away(x, -step) * 128
        o_ref[rows_of(at + c * 64, 64), :] = own_ref[step]
        o_ref[rows_of(at + 64 - c * 64, 64), :] = other_ref[step]
    dims = (((0,), (0,)), ((), ()))
    r = lax.dot_general(o_ref[...], a_ref[...].reshape(512, 256), dims, preferred_element_type=F32)
    out_ref[...] = r.astype(BF16).reshape(16, 64, 256)


def sum_output(in_ref, out_ref):
    for half in range(2):
        total = in_ref[half].astype(F32)
        for j in range(1, 8):
            total = total + in_ref[j * 2 + half].astype(F32)
        out_ref[:, half * 256 : (half + 1) * 256] = total.astype(BF16)


def trade(block, axis):
    return lax.all_to_all(block, axis, split_axis=0, concat_axis=0, tiled=True)


def gather(block, axis):
    return lax.all_gather(block, axis, axis=0, tiled=False)


def send(block, step):
    if step == 0:
        return block
    return lax.ppermute(block, "x", [(i, (i + step) % 4) for i in range(4)])


def partner(block):
    return lax.ppermute(block, "c", [(0, 1), (1, 0)])


def layer(tokens, query_weight, key_weight, value_weight, output_weight, segments):
    z, x, c = lax.axis_index("z"), lax.axis_index("x"), lax.axis_index("c")
    place = lax.iota(jnp.int32, 4)
    meta = jnp.where(place == 0, z, jnp.where(place == 1, x, c))
    starts, first = pl.pallas_call(
        find_starts,
        out_shape=[shape(1, 256, dtype=jnp.int32), shape(2, dtype=jnp.int32)],
        in_specs=[pl.BlockSpec(memory_space=s) for s in (pltpu.SMEM, pltpu.VMEM)],
        out_specs=[pl.BlockSpec(memory_space=s) for s in (pltpu.VMEM, pltpu.SMEM)],
        scratch_shapes=[],
        compiler_params=pltpu.CompilerParams(vmem_limit_bytes=4 << 20),
    )(meta, segments.reshape(24, 256))
    own = trade(jnp.broadcast_to(tokens.T, (8, 64, 512)), "y").reshape(512, 512)
    packed = call(
        pack_weights, [shape(160, 1024)] * 4,
        meta, query_weight, key_weight, value_weight, output_weight, smem=(0,),
    )
    weights = [send(packed[i], i) for i in range(4)]
    other = partner(own)
    partial, o_own = call(
        project, [shape(8, 192, 128), shape(4, 64, 1024)],
        meta, *weights, own, other, smem=(0,), limit=12,
        scratch=[
            pltpu.VMEM((1024, 512), BF16),
            pltpu.VMEM((384, 1024), BF16),
            pltpu.VMEM((384, 512), BF16),
        ],
    )
    o_other = partner(o_own)
    queries, spread = call(
        sum_projection,
        [shape(2, 128, 128), shape(12, 128, 128)],
        trade(partial, ("x", "c")),
    )
    memory = trade(spread, "z")
    queries = gather(queries, "x")
    memory = gather(memory, "c")
    mixed = call(
        attend, shape(4, 136, 256), meta, first, starts, queries, memory,
        smem=(0, 1),
        limit=16,
        scratch=[
            pltpu.VMEM((128, 1024), BF16),
            pltpu.VMEM((6, 256, 1024), F32),
            pltpu.VMEM((8, 1024), F32),
            pltpu.VMEM((8, 1024), F32),
            pltpu.VMEM((128, 1024), F32),
        ],
    )
    attended = trade(call(combine, shape(4, 128, 256), trade(mixed, "x")), "x")
    result = call(
        output_project, shape(16, 64, 256), meta, o_own, o_other, attended, smem=(0,), limit=12,
        scratch=[pltpu.VMEM((512, 1024), BF16)],
    )
    final = call(sum_output, shape(64, 512), trade(result, ("y", "c")))
    return final.T


def solution(mesh):
    grid = Mesh(mesh.devices.reshape(12, 8, 4, 2), ("z", "y", "x", "c"))
    head = ("y", "x", "c")
    placed = (P("z", head), P(head, None), P(head, None), P(head, None), P(head, None), P())
    return jax.shard_map(layer, mesh=grid, in_specs=placed, out_specs=P("z", head), check_vma=False)
```

time: 163 us -> 149 us (0.914)
  starting transfers between devices: 76.4 us -> 40.1 us
  blocking collectives: 57.5 us -> 77.8 us
  waiting for transfers between devices: 17.9 us -> 20.3 us
    ppermute x15 -> x3, starting transfers between devices: 47.6 us -> 10.2 us  [send(): return lax.ppermute(block, 'x', [(i, (i + step) % 4) for i in range(4)])]
    all_to_all x2 -> x4, blocking collectives: 35.4 us -> 63.8 us  [trade(): return lax.all_to_all(block, axis, split_axis=0, concat_axis=0, tiled=True)]
    all_to_all x1 -> x2, waiting for transfers between devices: 0.01 us -> 8.95 us  [trade(): return lax.all_to_all(block, axis, split_axis=0, concat_axis=0, tiled=True)]
    all_gather x3 -> x2, blocking collectives: 22.1 us -> 14 us  [gather(): return lax.all_gather(block, axis, axis=0, tiled=False)]
    ppermute x15 -> x3, waiting for transfers between devices: 17.9 us -> 11.4 us  [send(): return lax.ppermute(block, 'x', [(i, (i + step) % 4) for i in range(4)])]
    all_to_all x1 -> x2, starting transfers between devices: 14.9 us -> 18.4 us  [trade(): return lax.all_to_all(block, axis, split_axis=0, concat_axis=0, tiled=True)]
    ppermute x2, starting transfers between devices: 13.9 us -> 11.5 us  [partner(): return lax.ppermute(block, 'c', [(0, 1), (1, 0)])]
    pallas_call x8 -> x7, Pallas kernels: 7.35 us -> 6.99 us  [call(): pl.pallas_call(body, out_shape=many, in_specs=specs, out_specs=[pl.BlockS...]
  transfers between devices with their start and end apart: 18 -> 7, of which waited for: 9 -> 5; matrix products, arithmetic and copies ran while one was open for 0% -> 0% of each run, Pallas kernels for 3% -> 4%
where the time goes in v3:
time: 149 us
  blocking collectives  77.8 us (52%)
  starting transfers between devices  40.1 us (27%)
  waiting for transfers between devices  20.3 us (14%)
  Pallas kernels  9.14 us (6%)
    all_to_all x4, blocking collectives, trade(): return lax.all_to_all(block, axis, split_axis=0, concat_axis=0, tiled=True)  63.8 us
    all_to_all x2, starting transfers between devices, trade(): return lax.all_to_all(block, axis, split_axis=0, concat_axis=0, tiled=True)  18.4 us
    all_gather x2, blocking collectives, gather(): return lax.all_gather(block, axis, axis=0, tiled=False)  14 us
    ppermute x2, starting transfers between devices, partner(): return lax.ppermute(block, 'c', [(0, 1), (1, 0)])  11.5 us
    ppermute x3, waiting for transfers between devices, send(): return lax.ppermute(block, 'x', [(i, (i + step) % 4) for i in range(4)])  11.4 us
    ppermute x3, starting transfers between devices, send(): return lax.ppermute(block, 'x', [(i, (i + step) % 4) for i in range(4)])  10.2 us
    all_to_all x2, waiting for transfers between devices, trade(): return lax.all_to_all(block, axis, split_axis=0, concat_axis=0, tiled=True)  8.95 us
    pallas_call x7, Pallas kernels, call(): pl.pallas_call(body, out_shape=many, in_specs=specs, out_specs=[pl.BlockS...  6.99 us
  transfers between devices with their start and end apart: 7, of which 5 were waited for; matrix products, arithmetic and copies ran while one was open for 0% of the time, Pallas kernels for 4%

profile of v3, /device:TPU:1, one launch (start us, length us, event | category | flops | bytes accessed | tf_op | source)
XLA Modules:
  0.0 148.6 jit_solution(2720445495449274359)
XLA Ops:
  0.0 0.9 broadcast_in_dim.18
  0.9 0.0 copy-start
  0.9 0.0 copy-start.1
  1.0 19.8 %all_to_all.30 = bf16[8,64,512]{2,1,0:T(8,128)(2,1)S(1)} all-to-all(bf16[8,64,512]{2,1,0:T(8,128)(2,1)S(1)} %broadcast_in_dim.18), channel_id=1, replica_groups=mesh['z'=12,'y'=8,'x'=4,'c'=2] {'y'}, dimensions={0} | all-to-all | bytes 1048576 | tf_op jit(solution)/shard_map/all_to_all | solution.py:220
  20.7 8.4 %collective-permute-start.3 = (bf16[512,512]{1,0:T(8,128)(2,1)S(1)}, bf16[512,512]{1,0:T(8,128)(2,1)S(1)}, u32[]{:S(2)}, u32[]{:S(2)}) collective-permute-start(bf16[512,512]{1,0:T(8,128)(2,1)S(1)} %bitcast.6), channel_id=1, source_target_pairs={{0,1},{1,0},{2,3},{3,2},{4,5},{5,4},{6,7},{7,6},{8,9},{9,8},{10,11... | collective-permute-start | bytes 1572872 | tf_op jit(solution)/shard_map/ppermute | solution.py:234
  29.2 0.9 shard_map.64
  30.1 2.8 %collective-permute-start = (bf16[160,1024]{1,0:T(8,128)(2,1)S(1)}, bf16[160,1024]{1,0:T(8,128)(2,1)S(1)}, u32[]{:S(2)}, u32[]{:S(2)}) collective-permute-start(bf16[160,1024]{1,0:T(8,128)(2,1)S(1)} %get-tuple-element.16), channel_id=1, source_target_pairs={{0,2},{2,4},{4,6},{6,0},{1,3},{3,5},{5,7},{7,1},{8,10},{10,12},{12... | collective-permute-start | bytes 983048 | tf_op jit(solution)/shard_map/ppermute | solution.py:230
  33.0 4.4 %collective-permute-start.1 = (bf16[160,1024]{1,0:T(8,128)(2,1)S(1)}, bf16[160,1024]{1,0:T(8,128)(2,1)S(1)}, u32[]{:S(2)}, u32[]{:S(2)}) collective-permute-start(bf16[160,1024]{1,0:T(8,128)(2,1)S(1)} %get-tuple-element.17), channel_id=1, source_target_pairs={{0,4},{2,6},{4,0},{6,2},{1,5},{3,7},{5,1},{7,3},{8,12},{10,14},{12... | collective-permute-start | bytes 983048 | tf_op jit(solution)/shard_map/ppermute | solution.py:230
  37.3 3.1 %collective-permute-start.2 = (bf16[160,1024]{1,0:T(8,128)(2,1)S(1)}, bf16[160,1024]{1,0:T(8,128)(2,1)S(1)}, u32[]{:S(2)}, u32[]{:S(2)}) collective-permute-start(bf16[160,1024]{1,0:T(8,128)(2,1)S(1)} %get-tuple-element.18), channel_id=1, source_target_pairs={{0,6},{2,0},{4,2},{6,4},{1,7},{3,1},{5,3},{7,5},{8,14},{10,8},{12,... | collective-permute-start | bytes 983048 | tf_op jit(solution)/shard_map/ppermute | solution.py:230
  40.4 2.1 %collective-permute-done.w1 = bf16[160,1024]{1,0:T(8,128)(2,1)S(1)} collective-permute-done((bf16[160,1024]{1,0:T(8,128)(2,1)S(1)}, bf16[160,1024]{1,0:T(8,128)(2,1)S(1)}, u32[]{:S(2)}, u32[]{:S(2)}) %collective-permute-start) | collective-permute-done | bytes 327712 | tf_op jit(solution)/shard_map/ppermute | solution.py:230
  42.5 7.7 %collective-permute-done.1.w2 = bf16[160,1024]{1,0:T(8,128)(2,1)S(1)} collective-permute-done((bf16[160,1024]{1,0:T(8,128)(2,1)S(1)}, bf16[160,1024]{1,0:T(8,128)(2,1)S(1)}, u32[]{:S(2)}, u32[]{:S(2)}) %collective-permute-start.1) | collective-permute-done | bytes 327712 | tf_op jit(solution)/shard_map/ppermute | solution.py:230
  50.2 1.6 %collective-permute-done.2.w3 = bf16[160,1024]{1,0:T(8,128)(2,1)S(1)} collective-permute-done((bf16[160,1024]{1,0:T(8,128)(2,1)S(1)}, bf16[160,1024]{1,0:T(8,128)(2,1)S(1)}, u32[]{:S(2)}, u32[]{:S(2)}) %collective-permute-start.2) | collective-permute-done | bytes 327712 | tf_op jit(solution)/shard_map/ppermute | solution.py:230
  51.8 0.0 collective-permute-done.3.other_ref
  51.8 1.3 shard_map.65
  53.1 13.0 %all_to_all.31.in_ref = bf16[8,192,128]{2,1,0:T(8,128)(2,1)S(1)} all-to-all(bf16[8,192,128]{2,1,0:T(8,128)(2,1)S(1)} %get-tuple-element.22), channel_id=1, replica_groups=mesh['z'=12,'y'=8,'x'=4,'c'=2] {'x','c'}, dimensions={0} | all-to-all | bytes 786432 | tf_op jit(solution)/shard_map/all_to_all | solution.py:220
  66.1 0.8 shard_map.67
  66.9 15.0 %all-to-all-start.2 = ((bf16[12,128,128]{2,1,0:T(8,128)(2,1)}), bf16[12,128,128]{2,1,0:T(8,128)(2,1)S(1)}, u32[]{:S(2)}, u32[]{:S(2)}) async-start(bf16[12,128,128]{2,1,0:T(8,128)(2,1)} %get-tuple-element.24), calls=%async_computation.2 | async-start | bytes 786432 | tf_op jit(solution)/shard_map/all_to_all | solution.py:220
  81.9 0.0 copy-done.4
  81.9 2.1 %shard_map.66 = (s32[1,256]{1,0:T(1,128)S(1)}, s32[2]{0:T(128)S(1)}) custom-call(s32[4]{0:T(128)S(1)} %compare_select_fusion.1.meta_ref, s32[24,256]{1,0:T(8,128)S(1)} %reshape.7.seg_ref), custom_call_target="tpu_custom_call" | custom-call | tf_op jit(solution)/shard_map/pallas_call | solution.py:241
  84.1 3.1 %collective-permute-start.4 = (bf16[4,64,1024]{2,1,0:T(8,128)(2,1)S(1)}, bf16[4,64,1024]{2,1,0:T(8,128)(2,1)S(1)}, u32[]{:S(2)}, u32[]{:S(2)}) collective-permute-start(bf16[4,64,1024]{2,1,0:T(8,128)(2,1)S(1)} %get-tuple-element.19.own_ref), channel_id=1, source_target_pairs={{0,1},{1,0},{2,3},{3,2},{4,5},{5,4},{6,7},{7,6},{8,9},{9,8},{10,11... | collective-permute-start | bytes 1572872 | tf_op jit(solution)/shard_map/ppermute | solution.py:234
  87.1 10.0 %all-gather = bf16[8,128,128]{2,1,0:T(8,128)(2,1)S(1)} all-gather(bf16[2,128,128]{2,1,0:T(8,128)(2,1)S(1)} %get-tuple-element.23), channel_id=2, replica_groups=mesh['z'=12,'y'=8,'x'=4,'c'=2] {'x'}, dimensions={0}, use_global_device_ids=true | all-gather | bytes 327680 | tf_op jit(solution)/shard_map/all_gather | solution.py:224
  97.1 3.5 %all-to-all-done.2 = bf16[12,128,128]{2,1,0:T(8,128)(2,1)S(1)} async-done(((bf16[12,128,128]{2,1,0:T(8,128)(2,1)}), bf16[12,128,128]{2,1,0:T(8,128)(2,1)S(1)}, u32[]{:S(2)}, u32[]{:S(2)}) %all-to-all-start.2) | async-done | bytes 393248 | tf_op jit(solution)/shard_map/all_to_all | solution.py:220
  100.6 4.0 %all-gather.1 = bf16[24,128,128]{2,1,0:T(8,128)(2,1)S(1)} all-gather(bf16[12,128,128]{2,1,0:T(8,128)(2,1)S(1)} %all-to-all-done.2), channel_id=3, replica_groups=mesh['z'=12,'y'=8,'x'=4,'c'=2] {'c'}, dimensions={0}, use_global_device_ids=true | all-gather | bytes 1179648 | tf_op jit(solution)/shard_map/all_gather | solution.py:224
  104.6 1.4 shard_map.68
  106.0 8.9 %all_to_all.32.in_ref = bf16[4,136,256]{2,1,0:T(8,128)(2,1)S(1)} all-to-all(bf16[4,136,256]{2,1,0:T(8,128)(2,1)S(1)} %shard_map.68), channel_id=1, replica_groups=mesh['z'=12,'y'=8,'x'=4,'c'=2] {'x'}, dimensions={0} | all-to-all | bytes 557056 | tf_op jit(solution)/shard_map/all_to_all | solution.py:220
  114.9 0.8 shard_map.69
  115.7 3.4 %all-to-all-start.4 = ((bf16[4,128,256]{2,1,0:T(8,128)(2,1)}), bf16[4,128,256]{2,1,0:T(8,128)(2,1)S(1)}, u32[]{:S(2)}, u32[]{:S(2)}) async-start(bf16[4,128,256]{2,1,0:T(8,128)(2,1)} %shard_map.69), calls=%async_computation.4 | async-start | bytes 524288 | tf_op jit(solution)/shard_map/all_to_all | solution.py:220
  119.1 0.0 collective-permute-done.4.other_ref
  119.1 5.5 %all-to-all-done.4.a_ref = bf16[4,128,256]{2,1,0:T(8,128)(2,1)S(1)} async-done(((bf16[4,128,256]{2,1,0:T(8,128)(2,1)}), bf16[4,128,256]{2,1,0:T(8,128)(2,1)S(1)}, u32[]{:S(2)}, u32[]{:S(2)}) %all-to-all-start.4) | async-done | bytes 262176 | tf_op jit(solution)/shard_map/all_to_all | solution.py:220
  124.6 1.1 shard_map.70
  125.7 22.1 %all_to_all.33.in_ref = bf16[16,64,256]{2,1,0:T(8,128)(2,1)S(1)} all-to-all(bf16[16,64,256]{2,1,0:T(8,128)(2,1)S(1)} %shard_map.70), channel_id=1, replica_groups=mesh['z'=12,'y'=8,'x'=4,'c'=2] {'y','c'}, dimensions={0} | all-to-all | bytes 1048576 | tf_op jit(solution)/shard_map/all_to_all | solution.py:220
  147.9 0.7 shard_map.71
  (9 shorter events, 0.0 us)
Async XLA Ops:
  0.0 29.2 %copy-start.2 = (bf16[16,4096]{1,0:T(8,128)(2,1)S(1)}, bf16[16,4096]{1,0:T(8,128)(2,1)}, u32[]{:S(2)}) copy-start(bf16[16,4096]{1,0:T(8,128)(2,1)} %k_ref.1) | copy-start | bytes 393220
  0.0 29.2 %copy-start.3 = (bf16[16,4096]{1,0:T(8,128)(2,1)S(1)}, bf16[16,4096]{1,0:T(8,128)(2,1)}, u32[]{:S(2)}) copy-start(bf16[16,4096]{1,0:T(8,128)(2,1)} %v_ref.1) | copy-start | bytes 393220
  0.9 28.3 %copy-start = (bf16[64,4096]{1,0:T(8,128)(2,1)S(1)}, bf16[64,4096]{1,0:T(8,128)(2,1)}, u32[]{:S(2)}) copy-start(bf16[64,4096]{1,0:T(8,128)(2,1)} %q_ref.1) | copy-start | bytes 1572868
  0.9 28.3 %copy-start.1 = (bf16[64,4096]{1,0:T(8,128)(2,1)S(1)}, bf16[64,4096]{1,0:T(8,128)(2,1)}, u32[]{:S(2)}) copy-start(bf16[64,4096]{1,0:T(8,128)(2,1)} %o_ref.1) | copy-start | bytes 1572868
  20.7 31.0 %collective-permute-start.3 = (bf16[512,512]{1,0:T(8,128)(2,1)S(1)}, bf16[512,512]{1,0:T(8,128)(2,1)S(1)}, u32[]{:S(2)}, u32[]{:S(2)}) collective-permute-start(bf16[512,512]{1,0:T(8,128)(2,1)S(1)} %bitcast.6), channel_id=1, source_target_pairs={{0,1},{1,0},{2,3},{3,2},{4,5},{5,4},{6,7},{7,6},{8,9},{9,8},{10,11... | collective-permute-start | bytes 1572872 | tf_op jit(solution)/shard_map/ppermute | solution.py:234
  30.1 12.4 %collective-permute-start = (bf16[160,1024]{1,0:T(8,128)(2,1)S(1)}, bf16[160,1024]{1,0:T(8,128)(2,1)S(1)}, u32[]{:S(2)}, u32[]{:S(2)}) collective-permute-start(bf16[160,1024]{1,0:T(8,128)(2,1)S(1)} %get-tuple-element.16), channel_id=1, source_target_pairs={{0,2},{2,4},{4,6},{6,0},{1,3},{3,5},{5,7},{7,1},{8,10},{10,12},{12... | collective-permute-start | bytes 983048 | tf_op jit(solution)/shard_map/ppermute | solution.py:230
  33.0 17.2 %collective-permute-start.1 = (bf16[160,1024]{1,0:T(8,128)(2,1)S(1)}, bf16[160,1024]{1,0:T(8,128)(2,1)S(1)}, u32[]{:S(2)}, u32[]{:S(2)}) collective-permute-start(bf16[160,1024]{1,0:T(8,128)(2,1)S(1)} %get-tuple-element.17), channel_id=1, source_target_pairs={{0,4},{2,6},{4,0},{6,2},{1,5},{3,7},{5,1},{7,3},{8,12},{10,14},{12... | collective-permute-start | bytes 983048 | tf_op jit(solution)/shard_map/ppermute | solution.py:230
  37.3 14.4 %collective-permute-start.2 = (bf16[160,1024]{1,0:T(8,128)(2,1)S(1)}, bf16[160,1024]{1,0:T(8,128)(2,1)S(1)}, u32[]{:S(2)}, u32[]{:S(2)}) collective-permute-start(bf16[160,1024]{1,0:T(8,128)(2,1)S(1)} %get-tuple-element.18), channel_id=1, source_target_pairs={{0,6},{2,0},{4,2},{6,4},{1,7},{3,1},{5,3},{7,5},{8,14},{10,8},{12,... | collective-permute-start | bytes 983048 | tf_op jit(solution)/shard_map/ppermute | solution.py:230
  66.9 15.0 %copy-start.4 = (s32[6144]{0:T(1024)S(1)}, s32[6144]{0:T(1024)}, u32[]{:S(2)}) copy-start(s32[6144]{0:T(1024)} %param.11) | copy-start | bytes 73732
  66.9 33.7 %all-to-all-start.2 = ((bf16[12,128,128]{2,1,0:T(8,128)(2,1)}), bf16[12,128,128]{2,1,0:T(8,128)(2,1)S(1)}, u32[]{:S(2)}, u32[]{:S(2)}) async-start(bf16[12,128,128]{2,1,0:T(8,128)(2,1)} %get-tuple-element.24), calls=%async_computation.2 | async-start | bytes 786432 | tf_op jit(solution)/shard_map/all_to_all | solution.py:220
  84.1 35.1 %collective-permute-start.4 = (bf16[4,64,1024]{2,1,0:T(8,128)(2,1)S(1)}, bf16[4,64,1024]{2,1,0:T(8,128)(2,1)S(1)}, u32[]{:S(2)}, u32[]{:S(2)}) collective-permute-start(bf16[4,64,1024]{2,1,0:T(8,128)(2,1)S(1)} %get-tuple-element.19.own_ref), channel_id=1, source_target_pairs={{0,1},{1,0},{2,3},{3,2},{4,5},{5,4},{6,7},{7,6},{8,9},{9,8},{10,11... | collective-permute-start | bytes 1572872 | tf_op jit(solution)/shard_map/ppermute | solution.py:234
  115.7 8.9 %all-to-all-start.4 = ((bf16[4,128,256]{2,1,0:T(8,128)(2,1)}), bf16[4,128,256]{2,1,0:T(8,128)(2,1)S(1)}, u32[]{:S(2)}, u32[]{:S(2)}) async-start(bf16[4,128,256]{2,1,0:T(8,128)(2,1)} %shard_map.69), calls=%async_computation.4 | async-start | bytes 524288 | tf_op jit(solution)/shard_map/all_to_all | solution.py:220

commit v4 on v3

--- a/solution.py
+++ b/solution.py
@@ -85,24 +85,29 @@
     for j in range(4):
         for t in range(4):
             lanes = slice(t * 128, (t + 1) * 128)
-            at = (t % 2) * 64
-            out_ref[j * 2 + t // 2, at : at + 64, :] = y_ref[j * 96 : j * 96 + 64, lanes]
-            at = 128 + j * 16
-            out_ref[t * 2, at : at + 16, :] = y_ref[j * 96 + 64 : j * 96 + 80, lanes]
-            out_ref[t * 2 + 1, at : at + 16, :] = y_ref[j * 96 + 80 : j * 96 + 96, lanes]
+            out_ref[j, t * 64 : (t + 1) * 64, :] = y_ref[j * 96 : j * 96 + 64, lanes]
+            at = 256 + j * 16
+            out_ref[t, at : at + 16, :] = y_ref[j * 96 + 64 : j * 96 + 80, lanes]
+            at = 320 + j * 16
+            out_ref[t, at : at + 16, :] = y_ref[j * 96 + 80 : j * 96 + 96, lanes]
 
 
 def sum_projection(in_ref, q_ref, kv_ref):
-    for half in range(2):
-        total = in_ref[half].astype(F32)
-        for j in range(1, 4):
-            total = total + in_ref[j * 2 + half].astype(F32)
-        total = total.astype(BF16)
-        rows = slice(half * 64, half * 64 + 64)
-        for t in range(2):
-            q_ref[t, rows, :] = total[t * 64 : t * 64 + 64]
-        for j in range(12):
-            kv_ref[j, rows, :] = total[128:192]
+    total = in_ref[0].astype(F32)
+    for j in range(1, 4):
+        total = total + in_ref[j].astype(F32)
+    total = total.astype(BF16)
+    q_ref[...] = total[0:256]
+    for j in range(12):
+        kv_ref[j] = total[256:384]
+
+
+def spread_tokens(in_ref, out_ref, sems):
+    copies = [pltpu.make_async_copy(in_ref, out_ref.at[y], sems.at[y]) for y in range(8)]
+    for copy in copies:
+        copy.start()
+    for copy in copies:
+        copy.wait()
 
 
 def split3(value):
@@ -118,10 +123,11 @@
     first, latest = first_ref[0] >> 9, first_ref[1]
     for block in range(8):
         to = (block % 2) * 64 + (block // 2) * 16
-        for h in range(4):
-            for t in range(2):
+        for t in range(2):
+            at = pl.ds(pl.multiple_of(c * 128 + t * 64 + (block % 4) * 16, 16), 16)
+            for h in range(4):
                 lanes = slice((h * 2 + t) * 128, (h * 2 + t + 1) * 128)
-                qs_ref[to : to + 16, lanes] = q_ref[h, t, block * 16 : block * 16 + 16, :]
+                qs_ref[to : to + 16, lanes] = q_ref[h * 2 + block // 4, at, :]
     factor = math.log2(math.e) / math.sqrt(DIM)
     m_ref[...] = jnp.full((8, 1024), FLOOR, F32)
     l_ref[...] = jnp.zeros((8, 1024), F32)
@@ -130,8 +136,11 @@
     pairs = (z - first + 2) >> 1
 
     def tile(which, i):
-        j = first + 2 * i
-        return jnp.concatenate([kv_ref[which, j], kv_ref[which, jnp.minimum(j + 1, 11)]], axis=1)
+        rows = slice(which * 64, which * 64 + 64)
+        columns = []
+        for j in (first + 2 * i, jnp.minimum(first + 2 * i + 1, 11)):
+            columns.append(jnp.concatenate([kv_ref[0, j, rows, :], kv_ref[1, j, rows, :]], axis=0))
+        return jnp.concatenate(columns, axis=1)
 
     def score(i, unused):
         j = first + 2 * i
@@ -246,7 +255,15 @@
         scratch_shapes=[],
         compiler_params=pltpu.CompilerParams(vmem_limit_bytes=4 << 20),
     )(meta, segments.reshape(24, 256))
-    own = trade(jnp.broadcast_to(tokens.T, (8, 64, 512)), "y").reshape(512, 512)
+    copies = pl.pallas_call(
+        spread_tokens,
+        out_shape=shape(8, 64, 512),
+        in_specs=[pl.BlockSpec(memory_space=pl.ANY)],
+        out_specs=pl.BlockSpec(memory_space=pl.ANY),
+        scratch_shapes=[pltpu.SemaphoreType.DMA((8,))],
+        compiler_params=pltpu.CompilerParams(vmem_limit_bytes=4 << 20),
+    )(tokens.T)
+    own = trade(copies, "y").reshape(512, 512)
     packed = call(
         pack_weights, [shape(160, 1024)] * 4,
         meta, query_weight, key_weight, value_weight, output_weight, smem=(0,),
@@ -254,7 +271,7 @@
     weights = [send(packed[i], i) for i in range(4)]
     other = partner(own)
     partial, o_own = call(
-        project, [shape(8, 192, 128), shape(4, 64, 1024)],
+        project, [shape(4, 384, 128), shape(4, 64, 1024)],
         meta, *weights, own, other, smem=(0,), limit=12,
         scratch=[
             pltpu.VMEM((1024, 512), BF16),
@@ -265,11 +282,11 @@
     o_other = partner(o_own)
     queries, spread = call(
         sum_projection,
-        [shape(2, 128, 128), shape(12, 128, 128)],
-        trade(partial, ("x", "c")),
+        [shape(256, 128), shape(12, 128, 128)],
+        trade(partial, "x"),
     )
     memory = trade(spread, "z")
-    queries = gather(queries, "x")
+    queries = gather(queries, ("x", "c"))
     memory = gather(memory, "c")
     mixed = call(
         attend, shape(4, 136, 256), meta, first, starts, queries, memory,

time: 149 us -> 148 us (level)
  waiting for transfers between devices: 20.3 us -> 16.9 us
    all_to_all x2, waiting for transfers between devices: 8.95 us -> 5.49 us  [trade(): return lax.all_to_all(block, axis, split_axis=0, concat_axis=0, tiled=True)]
    all_gather x2, blocking collectives: 14 us -> 16.5 us  [gather(): return lax.all_gather(block, axis, axis=0, tiled=False)]
    all_to_all x4, blocking collectives: 63.8 us -> 62.1 us  [trade(): return lax.all_to_all(block, axis, split_axis=0, concat_axis=0, tiled=True)]
  transfers between devices with their start and end apart: 7 -> 7, of which waited for: 5 -> 4; matrix products, arithmetic and copies ran while one was open for 0% -> 0% of each run, Pallas kernels for 4% -> 4%
where the time goes in v4:
time: 148 us; the launch traced here: 147 us
  blocking collectives  78.5 us (53%)
  starting transfers between devices  40.8 us (28%)
  waiting for transfers between devices  16.9 us (11%)
  Pallas kernels  9.9 us (7%)
    all_to_all x4, blocking collectives, trade(): return lax.all_to_all(block, axis, split_axis=0, concat_axis=0, tiled=True)  62.1 us
    all_to_all x2, starting transfers between devices, trade(): return lax.all_to_all(block, axis, split_axis=0, concat_axis=0, tiled=True)  18 us
    all_gather x2, blocking collectives, gather(): return lax.all_gather(block, axis, axis=0, tiled=False)  16.5 us
    ppermute x2, starting transfers between devices, partner(): return lax.ppermute(block, 'c', [(0, 1), (1, 0)])  12.6 us
    ppermute x3, waiting for transfers between devices, send(): return lax.ppermute(block, 'x', [(i, (i + step) % 4) for i in range(4)])  11.4 us
    ppermute x3, starting transfers between devices, send(): return lax.ppermute(block, 'x', [(i, (i + step) % 4) for i in range(4)])  10.2 us
    pallas_call x7, Pallas kernels, call(): pl.pallas_call(body, out_shape=many, in_specs=specs, out_specs=[pl.BlockS...  7 us
    all_to_all x2, waiting for transfers between devices, trade(): return lax.all_to_all(block, axis, split_axis=0, concat_axis=0, tiled=True)  5.49 us
  transfers between devices with their start and end apart: 7, of which 4 were waited for; matrix products, arithmetic and copies ran while one was open for 0% of the time, Pallas kernels for 4%

profile of v4, /device:TPU:1, one launch (start us, length us, event | category | flops | bytes accessed | tf_op | source)
XLA Modules:
  0.0 147.2 jit_solution(9994934668420150761)
XLA Ops:
  0.0 0.8 copy-done.4
  0.8 0.7 shard_map.65
  1.6 0.0 copy-start
  1.6 0.0 copy-start.1
  1.6 19.8 %all_to_all.30 = bf16[8,64,512]{2,1,0:T(8,128)(2,1)S(1)} all-to-all(bf16[8,64,512]{2,1,0:T(8,128)(2,1)S(1)} %shard_map.65), channel_id=1, replica_groups=mesh['z'=12,'y'=8,'x'=4,'c'=2] {'y'}, dimensions={0} | all-to-all | bytes 1048576 | tf_op jit(solution)/shard_map/all_to_all | solution.py:229
  21.4 8.4 %collective-permute-start.3 = (bf16[512,512]{1,0:T(8,128)(2,1)S(1)}, bf16[512,512]{1,0:T(8,128)(2,1)S(1)}, u32[]{:S(2)}, u32[]{:S(2)}) collective-permute-start(bf16[512,512]{1,0:T(8,128)(2,1)S(1)} %bitcast.6), channel_id=1, source_target_pairs={{0,1},{1,0},{2,3},{3,2},{4,5},{5,4},{6,7},{7,6},{8,9},{9,8},{10,11... | collective-permute-start | bytes 1572872 | tf_op jit(solution)/shard_map/ppermute | solution.py:243
  29.9 0.9 shard_map.64
  30.8 2.8 %collective-permute-start = (bf16[160,1024]{1,0:T(8,128)(2,1)S(1)}, bf16[160,1024]{1,0:T(8,128)(2,1)S(1)}, u32[]{:S(2)}, u32[]{:S(2)}) collective-permute-start(bf16[160,1024]{1,0:T(8,128)(2,1)S(1)} %get-tuple-element.16), channel_id=1, source_target_pairs={{0,2},{2,4},{4,6},{6,0},{1,3},{3,5},{5,7},{7,1},{8,10},{10,12},{12... | collective-permute-start | bytes 983048 | tf_op jit(solution)/shard_map/ppermute | solution.py:239
  33.6 4.4 %collective-permute-start.1 = (bf16[160,1024]{1,0:T(8,128)(2,1)S(1)}, bf16[160,1024]{1,0:T(8,128)(2,1)S(1)}, u32[]{:S(2)}, u32[]{:S(2)}) collective-permute-start(bf16[160,1024]{1,0:T(8,128)(2,1)S(1)} %get-tuple-element.17), channel_id=1, source_target_pairs={{0,4},{2,6},{4,0},{6,2},{1,5},{3,7},{5,1},{7,3},{8,12},{10,14},{12... | collective-permute-start | bytes 983048 | tf_op jit(solution)/shard_map/ppermute | solution.py:239
  38.0 3.1 %collective-permute-start.2 = (bf16[160,1024]{1,0:T(8,128)(2,1)S(1)}, bf16[160,1024]{1,0:T(8,128)(2,1)S(1)}, u32[]{:S(2)}, u32[]{:S(2)}) collective-permute-start(bf16[160,1024]{1,0:T(8,128)(2,1)S(1)} %get-tuple-element.18), channel_id=1, source_target_pairs={{0,6},{2,0},{4,2},{6,4},{1,7},{3,1},{5,3},{7,5},{8,14},{10,8},{12,... | collective-permute-start | bytes 983048 | tf_op jit(solution)/shard_map/ppermute | solution.py:239
  41.1 2.1 %collective-permute-done.w1 = bf16[160,1024]{1,0:T(8,128)(2,1)S(1)} collective-permute-done((bf16[160,1024]{1,0:T(8,128)(2,1)S(1)}, bf16[160,1024]{1,0:T(8,128)(2,1)S(1)}, u32[]{:S(2)}, u32[]{:S(2)}) %collective-permute-start) | collective-permute-done | bytes 327712 | tf_op jit(solution)/shard_map/ppermute | solution.py:239
  43.2 7.7 %collective-permute-done.1.w2 = bf16[160,1024]{1,0:T(8,128)(2,1)S(1)} collective-permute-done((bf16[160,1024]{1,0:T(8,128)(2,1)S(1)}, bf16[160,1024]{1,0:T(8,128)(2,1)S(1)}, u32[]{:S(2)}, u32[]{:S(2)}) %collective-permute-start.1) | collective-permute-done | bytes 327712 | tf_op jit(solution)/shard_map/ppermute | solution.py:239
  50.9 1.6 %collective-permute-done.2.w3 = bf16[160,1024]{1,0:T(8,128)(2,1)S(1)} collective-permute-done((bf16[160,1024]{1,0:T(8,128)(2,1)S(1)}, bf16[160,1024]{1,0:T(8,128)(2,1)S(1)}, u32[]{:S(2)}, u32[]{:S(2)}) %collective-permute-start.2) | collective-permute-done | bytes 327712 | tf_op jit(solution)/shard_map/ppermute | solution.py:239
  52.4 0.0 collective-permute-done.3.other_ref
  52.4 1.3 shard_map.66
  53.7 11.2 %all_to_all.31.in_ref = bf16[4,384,128]{2,1,0:T(8,128)(2,1)S(1)} all-to-all(bf16[4,384,128]{2,1,0:T(8,128)(2,1)S(1)} %get-tuple-element.22), channel_id=1, replica_groups=mesh['z'=12,'y'=8,'x'=4,'c'=2] {'x'}, dimensions={0} | all-to-all | bytes 786432 | tf_op jit(solution)/shard_map/all_to_all | solution.py:229
  65.0 0.8 shard_map.68
  65.8 14.6 %all-to-all-start.2 = ((bf16[12,128,128]{2,1,0:T(8,128)(2,1)}), bf16[12,128,128]{2,1,0:T(8,128)(2,1)S(1)}, u32[]{:S(2)}, u32[]{:S(2)}) async-start(bf16[12,128,128]{2,1,0:T(8,128)(2,1)} %get-tuple-element.24), calls=%async_computation.2 | async-start | bytes 786432 | tf_op jit(solution)/shard_map/all_to_all | solution.py:229
  80.4 2.1 %shard_map.67 = (s32[1,256]{1,0:T(1,128)S(1)}, s32[2]{0:T(128)S(1)}) custom-call(s32[4]{0:T(128)S(1)} %compare_select_fusion.1.meta_ref, s32[24,256]{1,0:T(8,128)S(1)} %reshape.7.seg_ref), custom_call_target="tpu_custom_call" | custom-call | tf_op jit(solution)/shard_map/pallas_call | solution.py:250
  82.5 4.2 %collective-permute-start.4 = (bf16[4,64,1024]{2,1,0:T(8,128)(2,1)S(1)}, bf16[4,64,1024]{2,1,0:T(8,128)(2,1)S(1)}, u32[]{:S(2)}, u32[]{:S(2)}) collective-permute-start(bf16[4,64,1024]{2,1,0:T(8,128)(2,1)S(1)} %get-tuple-element.19.own_ref), channel_id=1, source_target_pairs={{0,1},{1,0},{2,3},{3,2},{4,5},{5,4},{6,7},{7,6},{8,9},{9,8},{10,11... | collective-permute-start | bytes 1572872 | tf_op jit(solution)/shard_map/ppermute | solution.py:243
  86.7 13.0 %all-gather = bf16[2048,128]{1,0:T(8,128)(2,1)S(1)} all-gather(bf16[256,128]{1,0:T(8,128)(2,1)S(1)} %get-tuple-element.23), channel_id=2, replica_groups=mesh['z'=12,'y'=8,'x'=4,'c'=2] {'x','c'}, dimensions={0}, use_global_device_ids=true | all-gather | bytes 589824 | tf_op jit(solution)/shard_map/all_gather | solution.py:233
  99.7 0.0 all-to-all-done.2
  99.7 3.5 %all-gather.1 = bf16[24,128,128]{2,1,0:T(8,128)(2,1)S(1)} all-gather(bf16[12,128,128]{2,1,0:T(8,128)(2,1)S(1)} %all-to-all-done.2), channel_id=3, replica_groups=mesh['z'=12,'y'=8,'x'=4,'c'=2] {'c'}, dimensions={0}, use_global_device_ids=true | all-gather | bytes 1179648 | tf_op jit(solution)/shard_map/all_gather | solution.py:233
  103.2 1.4 shard_map.69
  104.6 8.9 %all_to_all.32.in_ref = bf16[4,136,256]{2,1,0:T(8,128)(2,1)S(1)} all-to-all(bf16[4,136,256]{2,1,0:T(8,128)(2,1)S(1)} %shard_map.69), channel_id=1, replica_groups=mesh['z'=12,'y'=8,'x'=4,'c'=2] {'x'}, dimensions={0} | all-to-all | bytes 557056 | tf_op jit(solution)/shard_map/all_to_all | solution.py:229
  113.5 0.8 shard_map.70
  114.3 3.4 %all-to-all-start.4 = ((bf16[4,128,256]{2,1,0:T(8,128)(2,1)}), bf16[4,128,256]{2,1,0:T(8,128)(2,1)S(1)}, u32[]{:S(2)}, u32[]{:S(2)}) async-start(bf16[4,128,256]{2,1,0:T(8,128)(2,1)} %shard_map.70), calls=%async_computation.4 | async-start | bytes 524288 | tf_op jit(solution)/shard_map/all_to_all | solution.py:229
  117.7 0.0 collective-permute-done.4.other_ref
  117.8 5.5 %all-to-all-done.4.a_ref = bf16[4,128,256]{2,1,0:T(8,128)(2,1)S(1)} async-done(((bf16[4,128,256]{2,1,0:T(8,128)(2,1)}), bf16[4,128,256]{2,1,0:T(8,128)(2,1)S(1)}, u32[]{:S(2)}, u32[]{:S(2)}) %all-to-all-start.4) | async-done | bytes 262176 | tf_op jit(solution)/shard_map/all_to_all | solution.py:229
  123.2 1.1 shard_map.71
  124.4 22.1 %all_to_all.33.in_ref = bf16[16,64,256]{2,1,0:T(8,128)(2,1)S(1)} all-to-all(bf16[16,64,256]{2,1,0:T(8,128)(2,1)S(1)} %shard_map.71), channel_id=1, replica_groups=mesh['z'=12,'y'=8,'x'=4,'c'=2] {'y','c'}, dimensions={0} | all-to-all | bytes 1048576 | tf_op jit(solution)/shard_map/all_to_all | solution.py:229
  146.5 0.7 shard_map.72
  (11 shorter events, 0.0 us)
Async XLA Ops:
  0.0 0.8 copy-start.4
  0.8 29.0 %copy-start.2 = (bf16[16,4096]{1,0:T(8,128)(2,1)S(1)}, bf16[16,4096]{1,0:T(8,128)(2,1)}, u32[]{:S(2)}) copy-start(bf16[16,4096]{1,0:T(8,128)(2,1)} %k_ref.1) | copy-start | bytes 393220
  0.8 29.0 %copy-start.3 = (bf16[16,4096]{1,0:T(8,128)(2,1)S(1)}, bf16[16,4096]{1,0:T(8,128)(2,1)}, u32[]{:S(2)}) copy-start(bf16[16,4096]{1,0:T(8,128)(2,1)} %v_ref.1) | copy-start | bytes 393220
  1.6 28.3 %copy-start = (bf16[64,4096]{1,0:T(8,128)(2,1)S(1)}, bf16[64,4096]{1,0:T(8,128)(2,1)}, u32[]{:S(2)}) copy-start(bf16[64,4096]{1,0:T(8,128)(2,1)} %q_ref.1) | copy-start | bytes 1572868
  1.6 28.3 %copy-start.1 = (bf16[64,4096]{1,0:T(8,128)(2,1)S(1)}, bf16[64,4096]{1,0:T(8,128)(2,1)}, u32[]{:S(2)}) copy-start(bf16[64,4096]{1,0:T(8,128)(2,1)} %o_ref.1) | copy-start | bytes 1572868
  21.4 31.0 %collective-permute-start.3 = (bf16[512,512]{1,0:T(8,128)(2,1)S(1)}, bf16[512,512]{1,0:T(8,128)(2,1)S(1)}, u32[]{:S(2)}, u32[]{:S(2)}) collective-permute-start(bf16[512,512]{1,0:T(8,128)(2,1)S(1)} %bitcast.6), channel_id=1, source_target_pairs={{0,1},{1,0},{2,3},{3,2},{4,5},{5,4},{6,7},{7,6},{8,9},{9,8},{10,11... | collective-permute-start | bytes 1572872 | tf_op jit(solution)/shard_map/ppermute | solution.py:243
  30.8 12.4 %collective-permute-start = (bf16[160,1024]{1,0:T(8,128)(2,1)S(1)}, bf16[160,1024]{1,0:T(8,128)(2,1)S(1)}, u32[]{:S(2)}, u32[]{:S(2)}) collective-permute-start(bf16[160,1024]{1,0:T(8,128)(2,1)S(1)} %get-tuple-element.16), channel_id=1, source_target_pairs={{0,2},{2,4},{4,6},{6,0},{1,3},{3,5},{5,7},{7,1},{8,10},{10,12},{12... | collective-permute-start | bytes 983048 | tf_op jit(solution)/shard_map/ppermute | solution.py:239
  33.6 17.2 %collective-permute-start.1 = (bf16[160,1024]{1,0:T(8,128)(2,1)S(1)}, bf16[160,1024]{1,0:T(8,128)(2,1)S(1)}, u32[]{:S(2)}, u32[]{:S(2)}) collective-permute-start(bf16[160,1024]{1,0:T(8,128)(2,1)S(1)} %get-tuple-element.17), channel_id=1, source_target_pairs={{0,4},{2,6},{4,0},{6,2},{1,5},{3,7},{5,1},{7,3},{8,12},{10,14},{12... | collective-permute-start | bytes 983048 | tf_op jit(solution)/shard_map/ppermute | solution.py:239
  38.0 14.4 %collective-permute-start.2 = (bf16[160,1024]{1,0:T(8,128)(2,1)S(1)}, bf16[160,1024]{1,0:T(8,128)(2,1)S(1)}, u32[]{:S(2)}, u32[]{:S(2)}) collective-permute-start(bf16[160,1024]{1,0:T(8,128)(2,1)S(1)} %get-tuple-element.18), channel_id=1, source_target_pairs={{0,6},{2,0},{4,2},{6,4},{1,7},{3,1},{5,3},{7,5},{8,14},{10,8},{12,... | collective-permute-start | bytes 983048 | tf_op jit(solution)/shard_map/ppermute | solution.py:239
  65.8 14.6 %copy-start.5 = (s32[6144]{0:T(1024)S(1)}, s32[6144]{0:T(1024)}, u32[]{:S(2)}) copy-start(s32[6144]{0:T(1024)} %param.11) | copy-start | bytes 73732
  65.8 33.9 %all-to-all-start.2 = ((bf16[12,128,128]{2,1,0:T(8,128)(2,1)}), bf16[12,128,128]{2,1,0:T(8,128)(2,1)S(1)}, u32[]{:S(2)}, u32[]{:S(2)}) async-start(bf16[12,128,128]{2,1,0:T(8,128)(2,1)} %get-tuple-element.24), calls=%async_computation.2 | async-start | bytes 786432 | tf_op jit(solution)/shard_map/all_to_all | solution.py:229
  82.5 35.2 %collective-permute-start.4 = (bf16[4,64,1024]{2,1,0:T(8,128)(2,1)S(1)}, bf16[4,64,1024]{2,1,0:T(8,128)(2,1)S(1)}, u32[]{:S(2)}, u32[]{:S(2)}) collective-permute-start(bf16[4,64,1024]{2,1,0:T(8,128)(2,1)S(1)} %get-tuple-element.19.own_ref), channel_id=1, source_target_pairs={{0,1},{1,0},{2,3},{3,2},{4,5},{5,4},{6,7},{7,6},{8,9},{9,8},{10,11... | collective-permute-start | bytes 1572872 | tf_op jit(solution)/shard_map/ppermute | solution.py:243
  114.3 8.9 %all-to-all-start.4 = ((bf16[4,128,256]{2,1,0:T(8,128)(2,1)}), bf16[4,128,256]{2,1,0:T(8,128)(2,1)S(1)}, u32[]{:S(2)}, u32[]{:S(2)}) async-start(bf16[4,128,256]{2,1,0:T(8,128)(2,1)} %shard_map.70), calls=%async_computation.4 | async-start | bytes 524288 | tf_op jit(solution)/shard_map/all_to_all | solution.py:229

commit v5 on v4

--- a/solution.py
+++ b/solution.py
@@ -144,7 +144,7 @@
 
     def score(i, unused):
         j = first + 2 * i
-        key = tile(0, i).astype(F32).T.astype(BF16)
+        key = tile(0, i).T
 
         def note(s, lanes):
             s_ref[i, :, lanes] = s
@@ -202,27 +202,35 @@
     total = sum(w * t for w, t in zip(shares, totals))
     mixed = sum(in_ref[j, 0:128, :].astype(F32) * (shares[j] / total) for j in range(4))
     mixed = mixed.astype(BF16)
-    for j in range(4):
+    for j in range(8):
         out_ref[j] = mixed
 
 
-def output_project(meta_ref, own_ref, other_ref, a_ref, out_ref, o_ref):
+def turn_output_weight(meta_ref, own_ref, other_ref, out_ref, o_ref, turned_ref):
     x, c = meta_ref[1], meta_ref[2]
     for step in range(4):
         at = away(x, -step) * 128
         o_ref[rows_of(at + c * 64, 64), :] = own_ref[step]
         o_ref[rows_of(at + 64 - c * 64, 64), :] = other_ref[step]
-    dims = (((0,), (0,)), ((), ()))
-    r = lax.dot_general(o_ref[...], a_ref[...].reshape(512, 256), dims, preferred_element_type=F32)
-    out_ref[...] = r.astype(BF16).reshape(16, 64, 256)
+    turned_ref[...] = o_ref[...].T
+    for y in range(8):
+        out_ref[y * 64 : (y + 1) * 64, :] = turned_ref[rows_of(y * 128 + c * 64, 64), :]
+
+
+def output_project(o_ref, in_ref, out_ref, a_ref):
+    for j in range(4):
+        for half in range(2):
+            lanes = slice(half * 256, (half + 1) * 256)
+            a_ref[j * 128 : (j + 1) * 128, lanes] = in_ref[j * 2 + half]
+    r = jnp.dot(o_ref[...], a_ref[...], preferred_element_type=F32)
+    out_ref[...] = r.astype(BF16).reshape(8, 64, 512)
 
 
 def sum_output(in_ref, out_ref):
-    for half in range(2):
-        total = in_ref[half].astype(F32)
-        for j in range(1, 8):
-            total = total + in_ref[j * 2 + half].astype(F32)
-        out_ref[:, half * 256 : (half + 1) * 256] = total.astype(BF16)
+    total = in_ref[0].astype(F32)
+    for j in range(1, 8):
+        total = total + in_ref[j].astype(F32)
+    out_ref[...] = total.astype(BF16)
 
 
 def trade(block, axis):
@@ -258,8 +266,8 @@
     copies = pl.pallas_call(
         spread_tokens,
         out_shape=shape(8, 64, 512),
-        in_specs=[pl.BlockSpec(memory_space=pl.ANY)],
-        out_specs=pl.BlockSpec(memory_space=pl.ANY),
+        in_specs=[pl.BlockSpec(memory_space=pltpu.HBM)],
+        out_specs=pl.BlockSpec(memory_space=pltpu.HBM),
         scratch_shapes=[pltpu.SemaphoreType.DMA((8,))],
         compiler_params=pltpu.CompilerParams(vmem_limit_bytes=4 << 20),
     )(tokens.T)
@@ -300,12 +308,17 @@
             pltpu.VMEM((128, 1024), F32),
         ],
     )
-    attended = trade(call(combine, shape(4, 128, 256), trade(mixed, "x")), "x")
+    turned = call(
+        turn_output_weight, shape(512, 512), meta, o_own, o_other, smem=(0,), limit=12,
+        scratch=[pltpu.VMEM((512, 1024), BF16), pltpu.VMEM((1024, 512), BF16)],
+    )
+    attended = call(combine, shape(8, 128, 256), trade(mixed, "x"))
+    attended = trade(attended, ("x", "c"))
     result = call(
-        output_project, shape(16, 64, 256), meta, o_own, o_other, attended, smem=(0,), limit=12,
-        scratch=[pltpu.VMEM((512, 1024), BF16)],
-    )
-    final = call(sum_output, shape(64, 512), trade(result, ("y", "c")))
+        output_project, shape(8, 64, 512), turned, attended, limit=12,
+        scratch=[pltpu.VMEM((512, 512), BF16)],
+    )
+    final = call(sum_output, shape(64, 512), trade(result, "y"))
     return final.T
 
 

time: 148 us -> 151 us (1.020)
  the two profiles are of different devices: /device:TPU:1 before, /device:TPU:64 now
where the time goes in v5:
time: 151 us; the launch traced here: 150 us
  blocking collectives  71.8 us (48%)
  starting transfers between devices  37.2 us (25%)
  waiting for transfers between devices  29.2 us (19%)
  Pallas kernels  10.9 us (7%)
    all_to_all x3, blocking collectives, trade(): return lax.all_to_all(block, axis, split_axis=0, concat_axis=0, tiled=True)  56.4 us
    all_to_all x3, starting transfers between devices, trade(): return lax.all_to_all(block, axis, split_axis=0, concat_axis=0, tiled=True)  21.8 us
    all_to_all x3, waiting for transfers between devices, trade(): return lax.all_to_all(block, axis, split_axis=0, concat_axis=0, tiled=True)  17.8 us
    all_gather x2, blocking collectives, gather(): return lax.all_gather(block, axis, axis=0, tiled=False)  15.5 us
    ppermute x3, starting transfers between devices, send(): return lax.ppermute(block, 'x', [(i, (i + step) % 4) for i in range(4)])  11.4 us
    ppermute x3, waiting for transfers between devices, send(): return lax.ppermute(block, 'x', [(i, (i + step) % 4) for i in range(4)])  11.4 us
    pallas_call x8, Pallas kernels, call(): pl.pallas_call(body, out_shape=many, in_specs=specs, out_specs=[pl.BlockS...  8.06 us
    ppermute x2, starting transfers between devices, partner(): return lax.ppermute(block, 'c', [(0, 1), (1, 0)])  3.95 us
  transfers between devices with their start and end apart: 8, of which 6 were waited for; matrix products, arithmetic and copies ran while one was open for 0% of the time, Pallas kernels for 3%

profile of v5, /device:TPU:64, one launch (start us, length us, event | category | flops | bytes accessed | tf_op | source)
XLA Modules:
  0.0 150.2 jit_solution(543972146603824164)
XLA Ops:
  0.0 0.8 copy-done.4
  0.8 0.7 shard_map.65
  1.6 0.0 copy-start
  1.6 0.0 copy-start.1
  1.6 24.5 %all_to_all.30 = bf16[8,64,512]{2,1,0:T(8,128)(2,1)S(1)} all-to-all(bf16[8,64,512]{2,1,0:T(8,128)(2,1)S(1)} %shard_map.65), channel_id=1, replica_groups=mesh['z'=12,'y'=8,'x'=4,'c'=2] {'y'}, dimensions={0} | all-to-all | bytes 1048576 | tf_op jit(solution)/shard_map/all_to_all | solution.py:237
  26.1 1.9 %collective-permute-start.3 = (bf16[512,512]{1,0:T(8,128)(2,1)S(1)}, bf16[512,512]{1,0:T(8,128)(2,1)S(1)}, u32[]{:S(2)}, u32[]{:S(2)}) collective-permute-start(bf16[512,512]{1,0:T(8,128)(2,1)S(1)} %bitcast.6), channel_id=1, source_target_pairs={{0,1},{1,0},{2,3},{3,2},{4,5},{5,4},{6,7},{7,6},{8,9},{9,8},{10,11... | collective-permute-start | bytes 1572872 | tf_op jit(solution)/shard_map/ppermute | solution.py:251
  28.1 0.9 shard_map.64
  29.0 3.4 %collective-permute-start = (bf16[160,1024]{1,0:T(8,128)(2,1)S(1)}, bf16[160,1024]{1,0:T(8,128)(2,1)S(1)}, u32[]{:S(2)}, u32[]{:S(2)}) collective-permute-start(bf16[160,1024]{1,0:T(8,128)(2,1)S(1)} %get-tuple-element.16), channel_id=1, source_target_pairs={{0,2},{2,4},{4,6},{6,0},{1,3},{3,5},{5,7},{7,1},{8,10},{10,12},{12... | collective-permute-start | bytes 983048 | tf_op jit(solution)/shard_map/ppermute | solution.py:247
  32.4 4.6 %collective-permute-start.1 = (bf16[160,1024]{1,0:T(8,128)(2,1)S(1)}, bf16[160,1024]{1,0:T(8,128)(2,1)S(1)}, u32[]{:S(2)}, u32[]{:S(2)}) collective-permute-start(bf16[160,1024]{1,0:T(8,128)(2,1)S(1)} %get-tuple-element.17), channel_id=1, source_target_pairs={{0,4},{2,6},{4,0},{6,2},{1,5},{3,7},{5,1},{7,3},{8,12},{10,14},{12... | collective-permute-start | bytes 983048 | tf_op jit(solution)/shard_map/ppermute | solution.py:247
  37.1 3.3 %collective-permute-start.2 = (bf16[160,1024]{1,0:T(8,128)(2,1)S(1)}, bf16[160,1024]{1,0:T(8,128)(2,1)S(1)}, u32[]{:S(2)}, u32[]{:S(2)}) collective-permute-start(bf16[160,1024]{1,0:T(8,128)(2,1)S(1)} %get-tuple-element.18), channel_id=1, source_target_pairs={{0,6},{2,0},{4,2},{6,4},{1,7},{3,1},{5,3},{7,5},{8,14},{10,8},{12,... | collective-permute-start | bytes 983048 | tf_op jit(solution)/shard_map/ppermute | solution.py:247
  40.4 1.8 %collective-permute-done.w1 = bf16[160,1024]{1,0:T(8,128)(2,1)S(1)} collective-permute-done((bf16[160,1024]{1,0:T(8,128)(2,1)S(1)}, bf16[160,1024]{1,0:T(8,128)(2,1)S(1)}, u32[]{:S(2)}, u32[]{:S(2)}) %collective-permute-start) | collective-permute-done | bytes 327712 | tf_op jit(solution)/shard_map/ppermute | solution.py:247
  42.2 8.0 %collective-permute-done.1.w2 = bf16[160,1024]{1,0:T(8,128)(2,1)S(1)} collective-permute-done((bf16[160,1024]{1,0:T(8,128)(2,1)S(1)}, bf16[160,1024]{1,0:T(8,128)(2,1)S(1)}, u32[]{:S(2)}, u32[]{:S(2)}) %collective-permute-start.1) | collective-permute-done | bytes 327712 | tf_op jit(solution)/shard_map/ppermute | solution.py:247
  50.2 1.6 %collective-permute-done.2.w3 = bf16[160,1024]{1,0:T(8,128)(2,1)S(1)} collective-permute-done((bf16[160,1024]{1,0:T(8,128)(2,1)S(1)}, bf16[160,1024]{1,0:T(8,128)(2,1)S(1)}, u32[]{:S(2)}, u32[]{:S(2)}) %collective-permute-start.2) | collective-permute-done | bytes 327712 | tf_op jit(solution)/shard_map/ppermute | solution.py:247
  51.8 1.3 shard_map.66
  53.1 12.0 %all_to_all.31.in_ref = bf16[4,384,128]{2,1,0:T(8,128)(2,1)S(1)} all-to-all(bf16[4,384,128]{2,1,0:T(8,128)(2,1)S(1)} %get-tuple-element.22), channel_id=1, replica_groups=mesh['z'=12,'y'=8,'x'=4,'c'=2] {'x'}, dimensions={0} | all-to-all | bytes 786432 | tf_op jit(solution)/shard_map/all_to_all | solution.py:237
  65.1 0.8 shard_map.69
  65.9 14.9 %all-to-all-start.2 = ((bf16[12,128,128]{2,1,0:T(8,128)(2,1)}), bf16[12,128,128]{2,1,0:T(8,128)(2,1)S(1)}, u32[]{:S(2)}, u32[]{:S(2)}) async-start(bf16[12,128,128]{2,1,0:T(8,128)(2,1)} %get-tuple-element.24), calls=%async_computation.2 | async-start | bytes 786432 | tf_op jit(solution)/shard_map/all_to_all | solution.py:237
  80.8 2.1 %shard_map.68 = (s32[1,256]{1,0:T(1,128)S(1)}, s32[2]{0:T(128)S(1)}) custom-call(s32[4]{0:T(128)S(1)} %compare_select_fusion.1.meta_ref, s32[24,256]{1,0:T(8,128)S(1)} %reshape.7.seg_ref), custom_call_target="tpu_custom_call" | custom-call | tf_op jit(solution)/shard_map/pallas_call | solution.py:258
  82.9 13.1 %all-gather = bf16[2048,128]{1,0:T(8,128)(2,1)S(1)} all-gather(bf16[256,128]{1,0:T(8,128)(2,1)S(1)} %get-tuple-element.23), channel_id=2, replica_groups=mesh['z'=12,'y'=8,'x'=4,'c'=2] {'x','c'}, dimensions={0}, use_global_device_ids=true | all-gather | bytes 589824 | tf_op jit(solution)/shard_map/all_gather | solution.py:241
  96.1 3.2 %all-to-all-done.2 = bf16[12,128,128]{2,1,0:T(8,128)(2,1)S(1)} async-done(((bf16[12,128,128]{2,1,0:T(8,128)(2,1)}), bf16[12,128,128]{2,1,0:T(8,128)(2,1)S(1)}, u32[]{:S(2)}, u32[]{:S(2)}) %all-to-all-start.2) | async-done | bytes 393248 | tf_op jit(solution)/shard_map/all_to_all | solution.py:237
  99.3 2.4 %all-gather.1 = bf16[24,128,128]{2,1,0:T(8,128)(2,1)S(1)} all-gather(bf16[12,128,128]{2,1,0:T(8,128)(2,1)S(1)} %all-to-all-done.2), channel_id=3, replica_groups=mesh['z'=12,'y'=8,'x'=4,'c'=2] {'c'}, dimensions={0}, use_global_device_ids=true | all-gather | bytes 1179648 | tf_op jit(solution)/shard_map/all_gather | solution.py:241
  101.6 2.1 %shard_map.70 = bf16[4,136,256]{2,1,0:T(8,128)(2,1)} custom-call(s32[4]{0:T(128)S(1)} %compare_select_fusion.1.meta_ref, s32[2]{0:T(128)S(1)} %get-tuple-element.20.first_ref, s32[1,256]{1,0:T(1,128)S(1)} %get-tuple-element.21.start_ref, bf16[8,256,128]{2,1,0:T(8,128)(2,1)S(1)} %bitcast.8, bf16[2,12,128,128]{3,2,1,0:T(8,128)(2,1)S(1)} %bitcast.5), custom_call_target="tpu_custom_call" | custom-call | tf_op jit(solution)/shard_map/pallas_call | solution.py:25
  103.7 3.4 %all-to-all-start.3 = ((bf16[4,136,256]{2,1,0:T(8,128)(2,1)}), bf16[4,136,256]{2,1,0:T(8,128)(2,1)S(1)}, u32[]{:S(2)}, u32[]{:S(2)}) async-start(bf16[4,136,256]{2,1,0:T(8,128)(2,1)} %shard_map.70), calls=%async_computation.3 | async-start | bytes 557056 | tf_op jit(solution)/shard_map/all_to_all | solution.py:237
  107.2 2.0 %collective-permute-start.4 = (bf16[4,64,1024]{2,1,0:T(8,128)(2,1)S(1)}, bf16[4,64,1024]{2,1,0:T(8,128)(2,1)S(1)}, u32[]{:S(2)}, u32[]{:S(2)}) collective-permute-start(bf16[4,64,1024]{2,1,0:T(8,128)(2,1)S(1)} %get-tuple-element.19.own_ref), channel_id=1, source_target_pairs={{0,1},{1,0},{2,3},{3,2},{4,5},{5,4},{6,7},{7,6},{8,9},{9,8},{10,11... | collective-permute-start | bytes 1572872 | tf_op jit(solution)/shard_map/ppermute | solution.py:251
  109.2 5.3 %all-to-all-done.3.in_ref = bf16[4,136,256]{2,1,0:T(8,128)(2,1)S(1)} async-done(((bf16[4,136,256]{2,1,0:T(8,128)(2,1)}), bf16[4,136,256]{2,1,0:T(8,128)(2,1)S(1)}, u32[]{:S(2)}, u32[]{:S(2)}) %all-to-all-start.3) | async-done | bytes 278560 | tf_op jit(solution)/shard_map/all_to_all | solution.py:237
  114.5 0.9 shard_map.71
  115.4 3.5 %all-to-all-start.4 = ((bf16[8,128,256]{2,1,0:T(8,128)(2,1)}), bf16[8,128,256]{2,1,0:T(8,128)(2,1)S(1)}, u32[]{:S(2)}, u32[]{:S(2)}) async-start(bf16[8,128,256]{2,1,0:T(8,128)(2,1)} %shard_map.71), calls=%async_computation.4 | async-start | bytes 1048576 | tf_op jit(solution)/shard_map/all_to_all | solution.py:237
  118.9 1.0 shard_map.67.o_ref
  119.9 9.2 %all-to-all-done.4.in_ref = bf16[8,128,256]{2,1,0:T(8,128)(2,1)S(1)} async-done(((bf16[8,128,256]{2,1,0:T(8,128)(2,1)}), bf16[8,128,256]{2,1,0:T(8,128)(2,1)S(1)}, u32[]{:S(2)}, u32[]{:S(2)}) %all-to-all-start.4) | async-done | bytes 524320 | tf_op jit(solution)/shard_map/all_to_all | solution.py:237
  129.2 0.4 shard_map.72
  129.6 19.9 %all_to_all.32.in_ref = bf16[8,64,512]{2,1,0:T(8,128)(2,1)S(1)} all-to-all(bf16[8,64,512]{2,1,0:T(8,128)(2,1)S(1)} %shard_map.72), channel_id=1, replica_groups=mesh['z'=12,'y'=8,'x'=4,'c'=2] {'y'}, dimensions={0} | all-to-all | bytes 1048576 | tf_op jit(solution)/shard_map/all_to_all | solution.py:237
  149.5 0.7 shard_map.73
  (13 shorter events, 0.0 us)
Async XLA Ops:
  0.0 0.8 copy-start.4
  0.8 27.2 %copy-start.2 = (bf16[16,4096]{1,0:T(8,128)(2,1)S(1)}, bf16[16,4096]{1,0:T(8,128)(2,1)}, u32[]{:S(2)}) copy-start(bf16[16,4096]{1,0:T(8,128)(2,1)} %k_ref.1) | copy-start | bytes 393220
  0.8 27.3 %copy-start.3 = (bf16[16,4096]{1,0:T(8,128)(2,1)S(1)}, bf16[16,4096]{1,0:T(8,128)(2,1)}, u32[]{:S(2)}) copy-start(bf16[16,4096]{1,0:T(8,128)(2,1)} %v_ref.1) | copy-start | bytes 393220
  1.6 26.5 %copy-start = (bf16[64,4096]{1,0:T(8,128)(2,1)S(1)}, bf16[64,4096]{1,0:T(8,128)(2,1)}, u32[]{:S(2)}) copy-start(bf16[64,4096]{1,0:T(8,128)(2,1)} %q_ref.1) | copy-start | bytes 1572868
  1.6 26.5 %copy-start.1 = (bf16[64,4096]{1,0:T(8,128)(2,1)S(1)}, bf16[64,4096]{1,0:T(8,128)(2,1)}, u32[]{:S(2)}) copy-start(bf16[64,4096]{1,0:T(8,128)(2,1)} %o_ref.1) | copy-start | bytes 1572868
  26.1 25.7 %collective-permute-start.3 = (bf16[512,512]{1,0:T(8,128)(2,1)S(1)}, bf16[512,512]{1,0:T(8,128)(2,1)S(1)}, u32[]{:S(2)}, u32[]{:S(2)}) collective-permute-start(bf16[512,512]{1,0:T(8,128)(2,1)S(1)} %bitcast.6), channel_id=1, source_target_pairs={{0,1},{1,0},{2,3},{3,2},{4,5},{5,4},{6,7},{7,6},{8,9},{9,8},{10,11... | collective-permute-start | bytes 1572872 | tf_op jit(solution)/shard_map/ppermute | solution.py:251
  29.0 13.2 %collective-permute-start = (bf16[160,1024]{1,0:T(8,128)(2,1)S(1)}, bf16[160,1024]{1,0:T(8,128)(2,1)S(1)}, u32[]{:S(2)}, u32[]{:S(2)}) collective-permute-start(bf16[160,1024]{1,0:T(8,128)(2,1)S(1)} %get-tuple-element.16), channel_id=1, source_target_pairs={{0,2},{2,4},{4,6},{6,0},{1,3},{3,5},{5,7},{7,1},{8,10},{10,12},{12... | collective-permute-start | bytes 983048 | tf_op jit(solution)/shard_map/ppermute | solution.py:247
  32.4 17.8 %collective-permute-start.1 = (bf16[160,1024]{1,0:T(8,128)(2,1)S(1)}, bf16[160,1024]{1,0:T(8,128)(2,1)S(1)}, u32[]{:S(2)}, u32[]{:S(2)}) collective-permute-start(bf16[160,1024]{1,0:T(8,128)(2,1)S(1)} %get-tuple-element.17), channel_id=1, source_target_pairs={{0,4},{2,6},{4,0},{6,2},{1,5},{3,7},{5,1},{7,3},{8,12},{10,14},{12... | collective-permute-start | bytes 983048 | tf_op jit(solution)/shard_map/ppermute | solution.py:247
  37.1 14.7 %collective-permute-start.2 = (bf16[160,1024]{1,0:T(8,128)(2,1)S(1)}, bf16[160,1024]{1,0:T(8,128)(2,1)S(1)}, u32[]{:S(2)}, u32[]{:S(2)}) collective-permute-start(bf16[160,1024]{1,0:T(8,128)(2,1)S(1)} %get-tuple-element.18), channel_id=1, source_target_pairs={{0,6},{2,0},{4,2},{6,4},{1,7},{3,1},{5,3},{7,5},{8,14},{10,8},{12,... | collective-permute-start | bytes 983048 | tf_op jit(solution)/shard_map/ppermute | solution.py:247
  65.9 14.9 %copy-start.5 = (s32[6144]{0:T(1024)S(1)}, s32[6144]{0:T(1024)}, u32[]{:S(2)}) copy-start(s32[6144]{0:T(1024)} %param.11) | copy-start | bytes 73732
  65.9 33.4 %all-to-all-start.2 = ((bf16[12,128,128]{2,1,0:T(8,128)(2,1)}), bf16[12,128,128]{2,1,0:T(8,128)(2,1)S(1)}, u32[]{:S(2)}, u32[]{:S(2)}) async-start(bf16[12,128,128]{2,1,0:T(8,128)(2,1)} %get-tuple-element.24), calls=%async_computation.2 | async-start | bytes 786432 | tf_op jit(solution)/shard_map/all_to_all | solution.py:237
  103.7 10.8 %all-to-all-start.3 = ((bf16[4,136,256]{2,1,0:T(8,128)(2,1)}), bf16[4,136,256]{2,1,0:T(8,128)(2,1)S(1)}, u32[]{:S(2)}, u32[]{:S(2)}) async-start(bf16[4,136,256]{2,1,0:T(8,128)(2,1)} %shard_map.70), calls=%async_computation.3 | async-start | bytes 557056 | tf_op jit(solution)/shard_map/all_to_all | solution.py:237
  107.2 11.8 %collective-permute-start.4 = (bf16[4,64,1024]{2,1,0:T(8,128)(2,1)S(1)}, bf16[4,64,1024]{2,1,0:T(8,128)(2,1)S(1)}, u32[]{:S(2)}, u32[]{:S(2)}) collective-permute-start(bf16[4,64,1024]{2,1,0:T(8,128)(2,1)S(1)} %get-tuple-element.19.own_ref), channel_id=1, source_target_pairs={{0,1},{1,0},{2,3},{3,2},{4,5},{5,4},{6,7},{7,6},{8,9},{9,8},{10,11... | collective-permute-start | bytes 1572872 | tf_op jit(solution)/shard_map/ppermute | solution.py:251
  115.4 13.7 %all-to-all-start.4 = ((bf16[8,128,256]{2,1,0:T(8,128)(2,1)}), bf16[8,128,256]{2,1,0:T(8,128)(2,1)S(1)}, u32[]{:S(2)}, u32[]{:S(2)}) async-start(bf16[8,128,256]{2,1,0:T(8,128)(2,1)} %shard_map.71), calls=%async_computation.4 | async-start | bytes 1048576 | tf_op jit(solution)/shard_map/all_to_all | solution.py:237

commit v6 on v4

--- a/solution.py
+++ b/solution.py
@@ -133,24 +133,24 @@
     l_ref[...] = jnp.zeros((8, 1024), F32)
     o_ref[...] = jnp.zeros((128, 1024), F32)
     heads = [slice(h * 256, (h + 1) * 256) for h in range(4)]
-    pairs = (z - first + 2) >> 1
+    groups = (z - first + 4) >> 2
 
     def tile(which, i):
         rows = slice(which * 64, which * 64 + 64)
         columns = []
-        for j in (first + 2 * i, jnp.minimum(first + 2 * i + 1, 11)):
+        for j in [jnp.minimum(first + 4 * i + g, 11) for g in range(4)]:
             columns.append(jnp.concatenate([kv_ref[0, j, rows, :], kv_ref[1, j, rows, :]], axis=0))
         return jnp.concatenate(columns, axis=1)
 
     def score(i, unused):
-        j = first + 2 * i
-        key = tile(0, i).astype(F32).T.astype(BF16)
+        j = first + 4 * i
+        key = tile(0, i).T
 
         def note(s, lanes):
             s_ref[i, :, lanes] = s
-            m_ref[:, lanes] = jnp.maximum(m_ref[:, lanes], jnp.max(s.reshape(32, 8, 256), axis=0))
-
-        inside = (j * 512 >= latest) & (j + 1 < z)
+            m_ref[:, lanes] = jnp.maximum(m_ref[:, lanes], jnp.max(s.reshape(64, 8, 256), axis=0))
+
+        inside = (j * 512 >= latest) & (j + 3 < z)
 
         @pl.when(inside)
         def _():
@@ -159,9 +159,9 @@
 
         @pl.when(jnp.logical_not(inside))
         def _():
-            row = lax.broadcasted_iota(jnp.int32, (256, 256), 0)
+            row = lax.broadcasted_iota(jnp.int32, (512, 256), 0)
             place = j * 512 + (row >> 7) * 512 + x * 128 + (row & 127)
-            query = z * 512 + c * 256 + lax.broadcasted_iota(jnp.int32, (256, 256), 1)
+            query = z * 512 + c * 256 + lax.broadcasted_iota(jnp.int32, (512, 256), 1)
             allowed = (place >= start_ref[...]) & (place <= query)
             for lanes in heads:
                 s = jnp.dot(key, qs_ref[:, lanes], preferred_element_type=F32) * factor
@@ -169,18 +169,18 @@
 
         return unused
 
-    lax.fori_loop(0, pairs, score, 0)
+    lax.fori_loop(0, groups, score, 0)
     top = jnp.max(m_ref[...], axis=0, keepdims=True)
 
     def mix(i, unused):
         val = tile(1, i)
         for lanes in heads:
             p = jnp.exp2(s_ref[i, :, lanes] - top[:, lanes])
-            l_ref[:, lanes] += jnp.sum(p.reshape(32, 8, 256), axis=0)
+            l_ref[:, lanes] += jnp.sum(p.reshape(64, 8, 256), axis=0)
             o_ref[:, lanes] += jnp.dot(val, p.astype(BF16), preferred_element_type=F32)
         return unused
 
-    lax.fori_loop(0, pairs, mix, 0)
+    lax.fori_loop(0, groups, mix, 0)
     total = jnp.sum(l_ref[...], axis=0, keepdims=True)
     stats = [v.astype(F32) for v in split3(top) + split3(total)]
     stats = jnp.concatenate(stats + [jnp.zeros((2, 1024), F32)], axis=0)
@@ -294,7 +294,7 @@
         limit=16,
         scratch=[
             pltpu.VMEM((128, 1024), BF16),
-            pltpu.VMEM((6, 256, 1024), F32),
+            pltpu.VMEM((3, 512, 1024), F32),
             pltpu.VMEM((8, 1024), F32),
             pltpu.VMEM((8, 1024), F32),
             pltpu.VMEM((128, 1024), F32),

time: 148 us -> 148 us (level)
  no operation moved by 1% of the time
where the time goes in v6:
time: 148 us
  blocking collectives  78.5 us (53%)
  starting transfers between devices  40.8 us (28%)
  waiting for transfers between devices  16.9 us (11%)
  Pallas kernels  10.2 us (7%)
    all_to_all x4, blocking collectives, trade(): return lax.all_to_all(block, axis, split_axis=0, concat_axis=0, tiled=True)  62.1 us
    all_to_all x2, starting transfers between devices, trade(): return lax.all_to_all(block, axis, split_axis=0, concat_axis=0, tiled=True)  18 us
    all_gather x2, blocking collectives, gather(): return lax.all_gather(block, axis, axis=0, tiled=False)  16.5 us
    ppermute x2, starting transfers between devices, partner(): return lax.ppermute(block, 'c', [(0, 1), (1, 0)])  12.6 us
    ppermute x3, waiting for transfers between devices, send(): return lax.ppermute(block, 'x', [(i, (i + step) % 4) for i in range(4)])  11.4 us
    ppermute x3, starting transfers between devices, send(): return lax.ppermute(block, 'x', [(i, (i + step) % 4) for i in range(4)])  10.2 us
    pallas_call x7, Pallas kernels, call(): pl.pallas_call(body, out_shape=many, in_specs=specs, out_specs=[pl.BlockS...  7.35 us
    all_to_all x2, waiting for transfers between devices, trade(): return lax.all_to_all(block, axis, split_axis=0, concat_axis=0, tiled=True)  5.49 us
  transfers between devices with their start and end apart: 7, of which 4 were waited for; matrix products, arithmetic and copies ran while one was open for 0% of the time, Pallas kernels for 4%

profile of v6, /device:TPU:1, one launch (start us, length us, event | category | flops | bytes accessed | tf_op | source)
XLA Modules:
  0.0 147.6 jit_solution(14009794441452181112)
XLA Ops:
  0.0 0.8 copy-done.4
  0.8 0.7 shard_map.65
  1.6 0.0 copy-start
  1.6 0.0 copy-start.1
  1.6 19.8 %all_to_all.30 = bf16[8,64,512]{2,1,0:T(8,128)(2,1)S(1)} all-to-all(bf16[8,64,512]{2,1,0:T(8,128)(2,1)S(1)} %shard_map.65), channel_id=1, replica_groups=mesh['z'=12,'y'=8,'x'=4,'c'=2] {'y'}, dimensions={0} | all-to-all | bytes 1048576 | tf_op jit(solution)/shard_map/all_to_all | solution.py:229
  21.4 8.4 %collective-permute-start.3 = (bf16[512,512]{1,0:T(8,128)(2,1)S(1)}, bf16[512,512]{1,0:T(8,128)(2,1)S(1)}, u32[]{:S(2)}, u32[]{:S(2)}) collective-permute-start(bf16[512,512]{1,0:T(8,128)(2,1)S(1)} %bitcast.6), channel_id=1, source_target_pairs={{0,1},{1,0},{2,3},{3,2},{4,5},{5,4},{6,7},{7,6},{8,9},{9,8},{10,11... | collective-permute-start | bytes 1572872 | tf_op jit(solution)/shard_map/ppermute | solution.py:243
  29.9 0.9 shard_map.64
  30.8 2.8 %collective-permute-start = (bf16[160,1024]{1,0:T(8,128)(2,1)S(1)}, bf16[160,1024]{1,0:T(8,128)(2,1)S(1)}, u32[]{:S(2)}, u32[]{:S(2)}) collective-permute-start(bf16[160,1024]{1,0:T(8,128)(2,1)S(1)} %get-tuple-element.16), channel_id=1, source_target_pairs={{0,2},{2,4},{4,6},{6,0},{1,3},{3,5},{5,7},{7,1},{8,10},{10,12},{12... | collective-permute-start | bytes 983048 | tf_op jit(solution)/shard_map/ppermute | solution.py:239
  33.6 4.4 %collective-permute-start.1 = (bf16[160,1024]{1,0:T(8,128)(2,1)S(1)}, bf16[160,1024]{1,0:T(8,128)(2,1)S(1)}, u32[]{:S(2)}, u32[]{:S(2)}) collective-permute-start(bf16[160,1024]{1,0:T(8,128)(2,1)S(1)} %get-tuple-element.17), channel_id=1, source_target_pairs={{0,4},{2,6},{4,0},{6,2},{1,5},{3,7},{5,1},{7,3},{8,12},{10,14},{12... | collective-permute-start | bytes 983048 | tf_op jit(solution)/shard_map/ppermute | solution.py:239
  38.0 3.1 %collective-permute-start.2 = (bf16[160,1024]{1,0:T(8,128)(2,1)S(1)}, bf16[160,1024]{1,0:T(8,128)(2,1)S(1)}, u32[]{:S(2)}, u32[]{:S(2)}) collective-permute-start(bf16[160,1024]{1,0:T(8,128)(2,1)S(1)} %get-tuple-element.18), channel_id=1, source_target_pairs={{0,6},{2,0},{4,2},{6,4},{1,7},{3,1},{5,3},{7,5},{8,14},{10,8},{12,... | collective-permute-start | bytes 983048 | tf_op jit(solution)/shard_map/ppermute | solution.py:239
  41.1 2.1 %collective-permute-done.w1 = bf16[160,1024]{1,0:T(8,128)(2,1)S(1)} collective-permute-done((bf16[160,1024]{1,0:T(8,128)(2,1)S(1)}, bf16[160,1024]{1,0:T(8,128)(2,1)S(1)}, u32[]{:S(2)}, u32[]{:S(2)}) %collective-permute-start) | collective-permute-done | bytes 327712 | tf_op jit(solution)/shard_map/ppermute | solution.py:239
  43.2 7.7 %collective-permute-done.1.w2 = bf16[160,1024]{1,0:T(8,128)(2,1)S(1)} collective-permute-done((bf16[160,1024]{1,0:T(8,128)(2,1)S(1)}, bf16[160,1024]{1,0:T(8,128)(2,1)S(1)}, u32[]{:S(2)}, u32[]{:S(2)}) %collective-permute-start.1) | collective-permute-done | bytes 327712 | tf_op jit(solution)/shard_map/ppermute | solution.py:239
  50.9 1.6 %collective-permute-done.2.w3 = bf16[160,1024]{1,0:T(8,128)(2,1)S(1)} collective-permute-done((bf16[160,1024]{1,0:T(8,128)(2,1)S(1)}, bf16[160,1024]{1,0:T(8,128)(2,1)S(1)}, u32[]{:S(2)}, u32[]{:S(2)}) %collective-permute-start.2) | collective-permute-done | bytes 327712 | tf_op jit(solution)/shard_map/ppermute | solution.py:239
  52.4 0.0 collective-permute-done.3.other_ref
  52.4 1.3 shard_map.66
  53.7 11.2 %all_to_all.31.in_ref = bf16[4,384,128]{2,1,0:T(8,128)(2,1)S(1)} all-to-all(bf16[4,384,128]{2,1,0:T(8,128)(2,1)S(1)} %get-tuple-element.22), channel_id=1, replica_groups=mesh['z'=12,'y'=8,'x'=4,'c'=2] {'x'}, dimensions={0} | all-to-all | bytes 786432 | tf_op jit(solution)/shard_map/all_to_all | solution.py:229
  65.0 0.8 shard_map.68
  65.8 14.6 %all-to-all-start.2 = ((bf16[12,128,128]{2,1,0:T(8,128)(2,1)}), bf16[12,128,128]{2,1,0:T(8,128)(2,1)S(1)}, u32[]{:S(2)}, u32[]{:S(2)}) async-start(bf16[12,128,128]{2,1,0:T(8,128)(2,1)} %get-tuple-element.24), calls=%async_computation.2 | async-start | bytes 786432 | tf_op jit(solution)/shard_map/all_to_all | solution.py:229
  80.4 2.1 %shard_map.67 = (s32[1,256]{1,0:T(1,128)S(1)}, s32[2]{0:T(128)S(1)}) custom-call(s32[4]{0:T(128)S(1)} %compare_select_fusion.1.meta_ref, s32[24,256]{1,0:T(8,128)S(1)} %reshape.7.seg_ref), custom_call_target="tpu_custom_call" | custom-call | tf_op jit(solution)/shard_map/pallas_call | solution.py:250
  82.5 4.2 %collective-permute-start.4 = (bf16[4,64,1024]{2,1,0:T(8,128)(2,1)S(1)}, bf16[4,64,1024]{2,1,0:T(8,128)(2,1)S(1)}, u32[]{:S(2)}, u32[]{:S(2)}) collective-permute-start(bf16[4,64,1024]{2,1,0:T(8,128)(2,1)S(1)} %get-tuple-element.19.own_ref), channel_id=1, source_target_pairs={{0,1},{1,0},{2,3},{3,2},{4,5},{5,4},{6,7},{7,6},{8,9},{9,8},{10,11... | collective-permute-start | bytes 1572872 | tf_op jit(solution)/shard_map/ppermute | solution.py:243
  86.7 13.0 %all-gather = bf16[2048,128]{1,0:T(8,128)(2,1)S(1)} all-gather(bf16[256,128]{1,0:T(8,128)(2,1)S(1)} %get-tuple-element.23), channel_id=2, replica_groups=mesh['z'=12,'y'=8,'x'=4,'c'=2] {'x','c'}, dimensions={0}, use_global_device_ids=true | all-gather | bytes 589824 | tf_op jit(solution)/shard_map/all_gather | solution.py:233
  99.7 0.0 all-to-all-done.2
  99.7 3.5 %all-gather.1 = bf16[24,128,128]{2,1,0:T(8,128)(2,1)S(1)} all-gather(bf16[12,128,128]{2,1,0:T(8,128)(2,1)S(1)} %all-to-all-done.2), channel_id=3, replica_groups=mesh['z'=12,'y'=8,'x'=4,'c'=2] {'c'}, dimensions={0}, use_global_device_ids=true | all-gather | bytes 1179648 | tf_op jit(solution)/shard_map/all_gather | solution.py:233
  103.2 1.8 %shard_map.69 = bf16[4,136,256]{2,1,0:T(8,128)(2,1)S(1)} custom-call(s32[4]{0:T(128)S(1)} %compare_select_fusion.1.meta_ref, s32[2]{0:T(128)S(1)} %get-tuple-element.20.first_ref, s32[1,256]{1,0:T(1,128)S(1)} %get-tuple-element.21.start_ref, bf16[8,256,128]{2,1,0:T(8,128)(2,1)S(1)} %bitcast.8, bf16[2,12,128,128]{3,2,1,0:T(8,128)(2,1)S(1)} %bitcast.5), custom_call_target="tpu_custom_call" | custom-call | tf_op jit(solution)/shard_map/pallas_call | solution.py:25
  105.0 8.9 %all_to_all.32.in_ref = bf16[4,136,256]{2,1,0:T(8,128)(2,1)S(1)} all-to-all(bf16[4,136,256]{2,1,0:T(8,128)(2,1)S(1)} %shard_map.69), channel_id=1, replica_groups=mesh['z'=12,'y'=8,'x'=4,'c'=2] {'x'}, dimensions={0} | all-to-all | bytes 557056 | tf_op jit(solution)/shard_map/all_to_all | solution.py:229
  113.9 0.8 shard_map.70
  114.7 3.4 %all-to-all-start.4 = ((bf16[4,128,256]{2,1,0:T(8,128)(2,1)}), bf16[4,128,256]{2,1,0:T(8,128)(2,1)S(1)}, u32[]{:S(2)}, u32[]{:S(2)}) async-start(bf16[4,128,256]{2,1,0:T(8,128)(2,1)} %shard_map.70), calls=%async_computation.4 | async-start | bytes 524288 | tf_op jit(solution)/shard_map/all_to_all | solution.py:229
  118.1 0.0 collective-permute-done.4.other_ref
  118.1 5.5 %all-to-all-done.4.a_ref = bf16[4,128,256]{2,1,0:T(8,128)(2,1)S(1)} async-done(((bf16[4,128,256]{2,1,0:T(8,128)(2,1)}), bf16[4,128,256]{2,1,0:T(8,128)(2,1)S(1)}, u32[]{:S(2)}, u32[]{:S(2)}) %all-to-all-start.4) | async-done | bytes 262176 | tf_op jit(solution)/shard_map/all_to_all | solution.py:229
  123.6 1.1 shard_map.71
  124.7 22.1 %all_to_all.33.in_ref = bf16[16,64,256]{2,1,0:T(8,128)(2,1)S(1)} all-to-all(bf16[16,64,256]{2,1,0:T(8,128)(2,1)S(1)} %shard_map.71), channel_id=1, replica_groups=mesh['z'=12,'y'=8,'x'=4,'c'=2] {'y','c'}, dimensions={0} | all-to-all | bytes 1048576 | tf_op jit(solution)/shard_map/all_to_all | solution.py:229
  146.9 0.7 shard_map.72
  (11 shorter events, 0.0 us)
Async XLA Ops:
  0.0 0.8 copy-start.4
  0.8 29.0 %copy-start.2 = (bf16[16,4096]{1,0:T(8,128)(2,1)S(1)}, bf16[16,4096]{1,0:T(8,128)(2,1)}, u32[]{:S(2)}) copy-start(bf16[16,4096]{1,0:T(8,128)(2,1)} %k_ref.1) | copy-start | bytes 393220
  0.8 29.0 %copy-start.3 = (bf16[16,4096]{1,0:T(8,128)(2,1)S(1)}, bf16[16,4096]{1,0:T(8,128)(2,1)}, u32[]{:S(2)}) copy-start(bf16[16,4096]{1,0:T(8,128)(2,1)} %v_ref.1) | copy-start | bytes 393220
  1.6 28.3 %copy-start = (bf16[64,4096]{1,0:T(8,128)(2,1)S(1)}, bf16[64,4096]{1,0:T(8,128)(2,1)}, u32[]{:S(2)}) copy-start(bf16[64,4096]{1,0:T(8,128)(2,1)} %q_ref.1) | copy-start | bytes 1572868
  1.6 28.3 %copy-start.1 = (bf16[64,4096]{1,0:T(8,128)(2,1)S(1)}, bf16[64,4096]{1,0:T(8,128)(2,1)}, u32[]{:S(2)}) copy-start(bf16[64,4096]{1,0:T(8,128)(2,1)} %o_ref.1) | copy-start | bytes 1572868
  21.4 31.0 %collective-permute-start.3 = (bf16[512,512]{1,0:T(8,128)(2,1)S(1)}, bf16[512,512]{1,0:T(8,128)(2,1)S(1)}, u32[]{:S(2)}, u32[]{:S(2)}) collective-permute-start(bf16[512,512]{1,0:T(8,128)(2,1)S(1)} %bitcast.6), channel_id=1, source_target_pairs={{0,1},{1,0},{2,3},{3,2},{4,5},{5,4},{6,7},{7,6},{8,9},{9,8},{10,11... | collective-permute-start | bytes 1572872 | tf_op jit(solution)/shard_map/ppermute | solution.py:243
  30.8 12.4 %collective-permute-start = (bf16[160,1024]{1,0:T(8,128)(2,1)S(1)}, bf16[160,1024]{1,0:T(8,128)(2,1)S(1)}, u32[]{:S(2)}, u32[]{:S(2)}) collective-permute-start(bf16[160,1024]{1,0:T(8,128)(2,1)S(1)} %get-tuple-element.16), channel_id=1, source_target_pairs={{0,2},{2,4},{4,6},{6,0},{1,3},{3,5},{5,7},{7,1},{8,10},{10,12},{12... | collective-permute-start | bytes 983048 | tf_op jit(solution)/shard_map/ppermute | solution.py:239
  33.6 17.2 %collective-permute-start.1 = (bf16[160,1024]{1,0:T(8,128)(2,1)S(1)}, bf16[160,1024]{1,0:T(8,128)(2,1)S(1)}, u32[]{:S(2)}, u32[]{:S(2)}) collective-permute-start(bf16[160,1024]{1,0:T(8,128)(2,1)S(1)} %get-tuple-element.17), channel_id=1, source_target_pairs={{0,4},{2,6},{4,0},{6,2},{1,5},{3,7},{5,1},{7,3},{8,12},{10,14},{12... | collective-permute-start | bytes 983048 | tf_op jit(solution)/shard_map/ppermute | solution.py:239
  38.0 14.4 %collective-permute-start.2 = (bf16[160,1024]{1,0:T(8,128)(2,1)S(1)}, bf16[160,1024]{1,0:T(8,128)(2,1)S(1)}, u32[]{:S(2)}, u32[]{:S(2)}) collective-permute-start(bf16[160,1024]{1,0:T(8,128)(2,1)S(1)} %get-tuple-element.18), channel_id=1, source_target_pairs={{0,6},{2,0},{4,2},{6,4},{1,7},{3,1},{5,3},{7,5},{8,14},{10,8},{12,... | collective-permute-start | bytes 983048 | tf_op jit(solution)/shard_map/ppermute | solution.py:239
  65.8 14.6 %copy-start.5 = (s32[6144]{0:T(1024)S(1)}, s32[6144]{0:T(1024)}, u32[]{:S(2)}) copy-start(s32[6144]{0:T(1024)} %param.11) | copy-start | bytes 73732
  65.8 33.9 %all-to-all-start.2 = ((bf16[12,128,128]{2,1,0:T(8,128)(2,1)}), bf16[12,128,128]{2,1,0:T(8,128)(2,1)S(1)}, u32[]{:S(2)}, u32[]{:S(2)}) async-start(bf16[12,128,128]{2,1,0:T(8,128)(2,1)} %get-tuple-element.24), calls=%async_computation.2 | async-start | bytes 786432 | tf_op jit(solution)/shard_map/all_to_all | solution.py:229
  82.5 35.6 %collective-permute-start.4 = (bf16[4,64,1024]{2,1,0:T(8,128)(2,1)S(1)}, bf16[4,64,1024]{2,1,0:T(8,128)(2,1)S(1)}, u32[]{:S(2)}, u32[]{:S(2)}) collective-permute-start(bf16[4,64,1024]{2,1,0:T(8,128)(2,1)S(1)} %get-tuple-element.19.own_ref), channel_id=1, source_target_pairs={{0,1},{1,0},{2,3},{3,2},{4,5},{5,4},{6,7},{7,6},{8,9},{9,8},{10,11... | collective-permute-start | bytes 1572872 | tf_op jit(solution)/shard_map/ppermute | solution.py:243
  114.7 8.9 %all-to-all-start.4 = ((bf16[4,128,256]{2,1,0:T(8,128)(2,1)}), bf16[4,128,256]{2,1,0:T(8,128)(2,1)S(1)}, u32[]{:S(2)}, u32[]{:S(2)}) async-start(bf16[4,128,256]{2,1,0:T(8,128)(2,1)} %shard_map.70), calls=%async_computation.4 | async-start | bytes 524288 | tf_op jit(solution)/shard_map/all_to_all | solution.py:229

commit v7 on v6

--- a/solution.py
+++ b/solution.py
@@ -39,10 +39,9 @@
 
 def find_starts(meta_ref, seg_ref, start_ref, first_ref):
     at = meta_ref[0] * 2 + meta_ref[2]
-    window = seg_ref[pl.ds(at, 1), :]
+    window = jnp.concatenate([seg_ref[pl.ds(at * 2, 1), :], seg_ref[pl.ds(at * 2 + 1, 1), :]], axis=1)
     lane = lax.broadcasted_iota(jnp.int32, (1, 256), 1)
-    head = jnp.min(window)
-    begin = jnp.sum((seg_ref[...] < head).astype(jnp.int32))
+    begin = jnp.sum((seg_ref[...] < window[:, 0:1]).astype(jnp.int32))
     changed = (lane > 0) & (window != pltpu.roll(window, 1, 1))
     starts = jnp.where(changed, at * 256 + lane, begin)
     for bit in range(8):
@@ -254,15 +253,15 @@
         out_specs=[pl.BlockSpec(memory_space=s) for s in (pltpu.VMEM, pltpu.SMEM)],
         scratch_shapes=[],
         compiler_params=pltpu.CompilerParams(vmem_limit_bytes=4 << 20),
-    )(meta, segments.reshape(24, 256))
+    )(meta, segments.reshape(48, 128))
     copies = pl.pallas_call(
         spread_tokens,
         out_shape=shape(8, 64, 512),
-        in_specs=[pl.BlockSpec(memory_space=pl.ANY)],
-        out_specs=pl.BlockSpec(memory_space=pl.ANY),
+        in_specs=[pl.BlockSpec(memory_space=pltpu.HBM)],
+        out_specs=pl.BlockSpec(memory_space=pltpu.HBM),
         scratch_shapes=[pltpu.SemaphoreType.DMA((8,))],
         compiler_params=pltpu.CompilerParams(vmem_limit_bytes=4 << 20),
-    )(tokens.T)
+    )(pltpu.with_memory_space_constraint(tokens.T, pltpu.HBM))
     own = trade(copies, "y").reshape(512, 512)
     packed = call(
         pack_weights, [shape(160, 1024)] * 4,

time: 148 us -> 148 us (level)
  no operation moved by 1% of the time
where the time goes in v7:
time: 148 us; the launch traced here: 147 us
  blocking collectives  78.7 us (53%)
  starting transfers between devices  40.9 us (28%)
  waiting for transfers between devices  16.9 us (11%)
  Pallas kernels  10.6 us (7%)
    all_to_all x4, blocking collectives, trade(): return lax.all_to_all(block, axis, split_axis=0, concat_axis=0, tiled=True)  62.1 us
    all_to_all x2, starting transfers between devices, trade(): return lax.all_to_all(block, axis, split_axis=0, concat_axis=0, tiled=True)  18 us
    all_gather x2, blocking collectives, gather(): return lax.all_gather(block, axis, axis=0, tiled=False)  16.6 us
    ppermute x2, starting transfers between devices, partner(): return lax.ppermute(block, 'c', [(0, 1), (1, 0)])  12.6 us
    ppermute x3, waiting for transfers between devices, send(): return lax.ppermute(block, 'x', [(i, (i + step) % 4) for i in range(4)])  11.4 us
    ppermute x3, starting transfers between devices, send(): return lax.ppermute(block, 'x', [(i, (i + step) % 4) for i in range(4)])  10.2 us
    pallas_call x7, Pallas kernels, call(): pl.pallas_call(body, out_shape=many, in_specs=specs, out_specs=[pl.BlockS...  7.34 us
    all_to_all x2, waiting for transfers between devices, trade(): return lax.all_to_all(block, axis, split_axis=0, concat_axis=0, tiled=True)  5.49 us
  transfers between devices with their start and end apart: 7, of which 4 were waited for; matrix products, arithmetic and copies ran while one was open for 0% of the time, Pallas kernels for 4%

profile of v7, /device:TPU:1, one launch (start us, length us, event | category | flops | bytes accessed | tf_op | source)
XLA Modules:
  0.0 147.3 jit_solution(14838562620618229543)
XLA Ops:
  0.0 1.3 shard_map.65
  1.3 0.0 copy-start
  1.3 0.0 copy-start.1
  1.3 19.8 %all_to_all.30 = bf16[8,64,512]{2,1,0:T(8,128)(2,1)S(1)} all-to-all(bf16[8,64,512]{2,1,0:T(8,128)(2,1)S(1)} %shard_map.65), channel_id=1, replica_groups=mesh['z'=12,'y'=8,'x'=4,'c'=2] {'y'}, dimensions={0} | all-to-all | bytes 1048576 | tf_op jit(solution)/shard_map/all_to_all | solution.py:228
  21.1 8.4 %collective-permute-start.3 = (bf16[512,512]{1,0:T(8,128)(2,1)S(1)}, bf16[512,512]{1,0:T(8,128)(2,1)S(1)}, u32[]{:S(2)}, u32[]{:S(2)}) collective-permute-start(bf16[512,512]{1,0:T(8,128)(2,1)S(1)} %bitcast.7), channel_id=1, source_target_pairs={{0,1},{1,0},{2,3},{3,2},{4,5},{5,4},{6,7},{7,6},{8,9},{9,8},{10,11... | collective-permute-start | bytes 1572872 | tf_op jit(solution)/shard_map/ppermute | solution.py:242
  29.6 0.0 copy-done.2
  29.6 0.9 shard_map.64
  30.5 2.8 %collective-permute-start = (bf16[160,1024]{1,0:T(8,128)(2,1)S(1)}, bf16[160,1024]{1,0:T(8,128)(2,1)S(1)}, u32[]{:S(2)}, u32[]{:S(2)}) collective-permute-start(bf16[160,1024]{1,0:T(8,128)(2,1)S(1)} %get-tuple-element.16), channel_id=1, source_target_pairs={{0,2},{2,4},{4,6},{6,0},{1,3},{3,5},{5,7},{7,1},{8,10},{10,12},{12... | collective-permute-start | bytes 983048 | tf_op jit(solution)/shard_map/ppermute | solution.py:238
  33.3 4.4 %collective-permute-start.1 = (bf16[160,1024]{1,0:T(8,128)(2,1)S(1)}, bf16[160,1024]{1,0:T(8,128)(2,1)S(1)}, u32[]{:S(2)}, u32[]{:S(2)}) collective-permute-start(bf16[160,1024]{1,0:T(8,128)(2,1)S(1)} %get-tuple-element.17), channel_id=1, source_target_pairs={{0,4},{2,6},{4,0},{6,2},{1,5},{3,7},{5,1},{7,3},{8,12},{10,14},{12... | collective-permute-start | bytes 983048 | tf_op jit(solution)/shard_map/ppermute | solution.py:238
  37.7 3.1 %collective-permute-start.2 = (bf16[160,1024]{1,0:T(8,128)(2,1)S(1)}, bf16[160,1024]{1,0:T(8,128)(2,1)S(1)}, u32[]{:S(2)}, u32[]{:S(2)}) collective-permute-start(bf16[160,1024]{1,0:T(8,128)(2,1)S(1)} %get-tuple-element.18), channel_id=1, source_target_pairs={{0,6},{2,0},{4,2},{6,4},{1,7},{3,1},{5,3},{7,5},{8,14},{10,8},{12,... | collective-permute-start | bytes 983048 | tf_op jit(solution)/shard_map/ppermute | solution.py:238
  40.8 2.1 %collective-permute-done.w1 = bf16[160,1024]{1,0:T(8,128)(2,1)S(1)} collective-permute-done((bf16[160,1024]{1,0:T(8,128)(2,1)S(1)}, bf16[160,1024]{1,0:T(8,128)(2,1)S(1)}, u32[]{:S(2)}, u32[]{:S(2)}) %collective-permute-start) | collective-permute-done | bytes 327712 | tf_op jit(solution)/shard_map/ppermute | solution.py:238
  42.9 7.7 %collective-permute-done.1.w2 = bf16[160,1024]{1,0:T(8,128)(2,1)S(1)} collective-permute-done((bf16[160,1024]{1,0:T(8,128)(2,1)S(1)}, bf16[160,1024]{1,0:T(8,128)(2,1)S(1)}, u32[]{:S(2)}, u32[]{:S(2)}) %collective-permute-start.1) | collective-permute-done | bytes 327712 | tf_op jit(solution)/shard_map/ppermute | solution.py:238
  50.6 1.6 %collective-permute-done.2.w3 = bf16[160,1024]{1,0:T(8,128)(2,1)S(1)} collective-permute-done((bf16[160,1024]{1,0:T(8,128)(2,1)S(1)}, bf16[160,1024]{1,0:T(8,128)(2,1)S(1)}, u32[]{:S(2)}, u32[]{:S(2)}) %collective-permute-start.2) | collective-permute-done | bytes 327712 | tf_op jit(solution)/shard_map/ppermute | solution.py:238
  52.1 0.0 collective-permute-done.3.other_ref
  52.1 1.3 shard_map.66
  53.4 11.2 %all_to_all.31.in_ref = bf16[4,384,128]{2,1,0:T(8,128)(2,1)S(1)} all-to-all(bf16[4,384,128]{2,1,0:T(8,128)(2,1)S(1)} %get-tuple-element.22), channel_id=1, replica_groups=mesh['z'=12,'y'=8,'x'=4,'c'=2] {'x'}, dimensions={0} | all-to-all | bytes 786432 | tf_op jit(solution)/shard_map/all_to_all | solution.py:228
  64.7 0.8 shard_map.68
  65.5 14.6 %all-to-all-start.2 = ((bf16[12,128,128]{2,1,0:T(8,128)(2,1)}), bf16[12,128,128]{2,1,0:T(8,128)(2,1)S(1)}, u32[]{:S(2)}, u32[]{:S(2)}) async-start(bf16[12,128,128]{2,1,0:T(8,128)(2,1)} %get-tuple-element.24), calls=%async_computation.2 | async-start | bytes 786432 | tf_op jit(solution)/shard_map/all_to_all | solution.py:228
  80.1 2.0 %shard_map.67 = (s32[1,256]{1,0:T(1,128)S(1)}, s32[2]{0:T(128)S(1)}) custom-call(s32[4]{0:T(128)S(1)} %compare_select_fusion.1.meta_ref, s32[48,128]{1,0:T(8,128)S(1)} %bitcast.10), custom_call_target="tpu_custom_call" | custom-call | tf_op jit(solution)/shard_map/pallas_call | solution.py:249
  82.1 4.2 %collective-permute-start.4 = (bf16[4,64,1024]{2,1,0:T(8,128)(2,1)S(1)}, bf16[4,64,1024]{2,1,0:T(8,128)(2,1)S(1)}, u32[]{:S(2)}, u32[]{:S(2)}) collective-permute-start(bf16[4,64,1024]{2,1,0:T(8,128)(2,1)S(1)} %get-tuple-element.19.own_ref), channel_id=1, source_target_pairs={{0,1},{1,0},{2,3},{3,2},{4,5},{5,4},{6,7},{7,6},{8,9},{9,8},{10,11... | collective-permute-start | bytes 1572872 | tf_op jit(solution)/shard_map/ppermute | solution.py:242
  86.3 13.0 %all-gather = bf16[2048,128]{1,0:T(8,128)(2,1)S(1)} all-gather(bf16[256,128]{1,0:T(8,128)(2,1)S(1)} %get-tuple-element.23), channel_id=2, replica_groups=mesh['z'=12,'y'=8,'x'=4,'c'=2] {'x','c'}, dimensions={0}, use_global_device_ids=true | all-gather | bytes 589824 | tf_op jit(solution)/shard_map/all_gather | solution.py:232
  99.2 0.0 all-to-all-done.2
  99.2 3.7 %all-gather.1 = bf16[24,128,128]{2,1,0:T(8,128)(2,1)S(1)} all-gather(bf16[12,128,128]{2,1,0:T(8,128)(2,1)S(1)} %all-to-all-done.2), channel_id=3, replica_groups=mesh['z'=12,'y'=8,'x'=4,'c'=2] {'c'}, dimensions={0}, use_global_device_ids=true | all-gather | bytes 1179648 | tf_op jit(solution)/shard_map/all_gather | solution.py:232
  102.9 1.8 %shard_map.69 = bf16[4,136,256]{2,1,0:T(8,128)(2,1)S(1)} custom-call(s32[4]{0:T(128)S(1)} %compare_select_fusion.1.meta_ref, s32[2]{0:T(128)S(1)} %get-tuple-element.20.first_ref, s32[1,256]{1,0:T(1,128)S(1)} %get-tuple-element.21.start_ref, bf16[8,256,128]{2,1,0:T(8,128)(2,1)S(1)} %bitcast.9, bf16[2,12,128,128]{3,2,1,0:T(8,128)(2,1)S(1)} %bitcast.6), custom_call_target="tpu_custom_call" | custom-call | tf_op jit(solution)/shard_map/pallas_call | solution.py:25
  104.7 8.9 %all_to_all.32.in_ref = bf16[4,136,256]{2,1,0:T(8,128)(2,1)S(1)} all-to-all(bf16[4,136,256]{2,1,0:T(8,128)(2,1)S(1)} %shard_map.69), channel_id=1, replica_groups=mesh['z'=12,'y'=8,'x'=4,'c'=2] {'x'}, dimensions={0} | all-to-all | bytes 557056 | tf_op jit(solution)/shard_map/all_to_all | solution.py:228
  113.6 0.8 shard_map.70
  114.4 3.4 %all-to-all-start.4 = ((bf16[4,128,256]{2,1,0:T(8,128)(2,1)}), bf16[4,128,256]{2,1,0:T(8,128)(2,1)S(1)}, u32[]{:S(2)}, u32[]{:S(2)}) async-start(bf16[4,128,256]{2,1,0:T(8,128)(2,1)} %shard_map.70), calls=%async_computation.4 | async-start | bytes 524288 | tf_op jit(solution)/shard_map/all_to_all | solution.py:228
  117.8 0.0 collective-permute-done.4.other_ref
  117.8 5.5 %all-to-all-done.4.a_ref = bf16[4,128,256]{2,1,0:T(8,128)(2,1)S(1)} async-done(((bf16[4,128,256]{2,1,0:T(8,128)(2,1)}), bf16[4,128,256]{2,1,0:T(8,128)(2,1)S(1)}, u32[]{:S(2)}, u32[]{:S(2)}) %all-to-all-start.4) | async-done | bytes 262176 | tf_op jit(solution)/shard_map/all_to_all | solution.py:228
  123.3 1.1 shard_map.71
  124.4 22.1 %all_to_all.33.in_ref = bf16[16,64,256]{2,1,0:T(8,128)(2,1)S(1)} all-to-all(bf16[16,64,256]{2,1,0:T(8,128)(2,1)S(1)} %shard_map.71), channel_id=1, replica_groups=mesh['z'=12,'y'=8,'x'=4,'c'=2] {'y','c'}, dimensions={0} | all-to-all | bytes 1048576 | tf_op jit(solution)/shard_map/all_to_all | solution.py:228
  146.6 0.7 shard_map.72
  (8 shorter events, 0.0 us)
Async XLA Ops:
  0.0 29.6 %copy-start.2 = (bf16[16,4096]{1,0:T(8,128)(2,1)S(1)}, bf16[16,4096]{1,0:T(8,128)(2,1)}, u32[]{:S(2)}) copy-start(bf16[16,4096]{1,0:T(8,128)(2,1)} %k_ref.1) | copy-start | bytes 393220
  0.0 29.6 %copy-start.3 = (bf16[16,4096]{1,0:T(8,128)(2,1)S(1)}, bf16[16,4096]{1,0:T(8,128)(2,1)}, u32[]{:S(2)}) copy-start(bf16[16,4096]{1,0:T(8,128)(2,1)} %v_ref.1) | copy-start | bytes 393220
  1.3 28.3 %copy-start = (bf16[64,4096]{1,0:T(8,128)(2,1)S(1)}, bf16[64,4096]{1,0:T(8,128)(2,1)}, u32[]{:S(2)}) copy-start(bf16[64,4096]{1,0:T(8,128)(2,1)} %q_ref.1) | copy-start | bytes 1572868
  1.3 28.3 %copy-start.1 = (bf16[64,4096]{1,0:T(8,128)(2,1)S(1)}, bf16[64,4096]{1,0:T(8,128)(2,1)}, u32[]{:S(2)}) copy-start(bf16[64,4096]{1,0:T(8,128)(2,1)} %o_ref.1) | copy-start | bytes 1572868
  21.1 31.0 %collective-permute-start.3 = (bf16[512,512]{1,0:T(8,128)(2,1)S(1)}, bf16[512,512]{1,0:T(8,128)(2,1)S(1)}, u32[]{:S(2)}, u32[]{:S(2)}) collective-permute-start(bf16[512,512]{1,0:T(8,128)(2,1)S(1)} %bitcast.7), channel_id=1, source_target_pairs={{0,1},{1,0},{2,3},{3,2},{4,5},{5,4},{6,7},{7,6},{8,9},{9,8},{10,11... | collective-permute-start | bytes 1572872 | tf_op jit(solution)/shard_map/ppermute | solution.py:242
  30.5 12.4 %collective-permute-start = (bf16[160,1024]{1,0:T(8,128)(2,1)S(1)}, bf16[160,1024]{1,0:T(8,128)(2,1)S(1)}, u32[]{:S(2)}, u32[]{:S(2)}) collective-permute-start(bf16[160,1024]{1,0:T(8,128)(2,1)S(1)} %get-tuple-element.16), channel_id=1, source_target_pairs={{0,2},{2,4},{4,6},{6,0},{1,3},{3,5},{5,7},{7,1},{8,10},{10,12},{12... | collective-permute-start | bytes 983048 | tf_op jit(solution)/shard_map/ppermute | solution.py:238
  33.3 17.2 %collective-permute-start.1 = (bf16[160,1024]{1,0:T(8,128)(2,1)S(1)}, bf16[160,1024]{1,0:T(8,128)(2,1)S(1)}, u32[]{:S(2)}, u32[]{:S(2)}) collective-permute-start(bf16[160,1024]{1,0:T(8,128)(2,1)S(1)} %get-tuple-element.17), channel_id=1, source_target_pairs={{0,4},{2,6},{4,0},{6,2},{1,5},{3,7},{5,1},{7,3},{8,12},{10,14},{12... | collective-permute-start | bytes 983048 | tf_op jit(solution)/shard_map/ppermute | solution.py:238
  37.7 14.4 %collective-permute-start.2 = (bf16[160,1024]{1,0:T(8,128)(2,1)S(1)}, bf16[160,1024]{1,0:T(8,128)(2,1)S(1)}, u32[]{:S(2)}, u32[]{:S(2)}) collective-permute-start(bf16[160,1024]{1,0:T(8,128)(2,1)S(1)} %get-tuple-element.18), channel_id=1, source_target_pairs={{0,6},{2,0},{4,2},{6,4},{1,7},{3,1},{5,3},{7,5},{8,14},{10,8},{12,... | collective-permute-start | bytes 983048 | tf_op jit(solution)/shard_map/ppermute | solution.py:238
  65.5 14.6 %copy-start.4 = (s32[6144]{0:T(1024)S(1)}, s32[6144]{0:T(1024)}, u32[]{:S(2)}) copy-start(s32[6144]{0:T(1024)} %param.11) | copy-start | bytes 73732
  65.5 33.8 %all-to-all-start.2 = ((bf16[12,128,128]{2,1,0:T(8,128)(2,1)}), bf16[12,128,128]{2,1,0:T(8,128)(2,1)S(1)}, u32[]{:S(2)}, u32[]{:S(2)}) async-start(bf16[12,128,128]{2,1,0:T(8,128)(2,1)} %get-tuple-element.24), calls=%async_computation.2 | async-start | bytes 786432 | tf_op jit(solution)/shard_map/all_to_all | solution.py:228
  82.1 35.7 %collective-permute-start.4 = (bf16[4,64,1024]{2,1,0:T(8,128)(2,1)S(1)}, bf16[4,64,1024]{2,1,0:T(8,128)(2,1)S(1)}, u32[]{:S(2)}, u32[]{:S(2)}) collective-permute-start(bf16[4,64,1024]{2,1,0:T(8,128)(2,1)S(1)} %get-tuple-element.19.own_ref), channel_id=1, source_target_pairs={{0,1},{1,0},{2,3},{3,2},{4,5},{5,4},{6,7},{7,6},{8,9},{9,8},{10,11... | collective-permute-start | bytes 1572872 | tf_op jit(solution)/shard_map/ppermute | solution.py:242
  114.4 8.9 %all-to-all-start.4 = ((bf16[4,128,256]{2,1,0:T(8,128)(2,1)}), bf16[4,128,256]{2,1,0:T(8,128)(2,1)S(1)}, u32[]{:S(2)}, u32[]{:S(2)}) async-start(bf16[4,128,256]{2,1,0:T(8,128)(2,1)} %shard_map.70), calls=%async_computation.4 | async-start | bytes 524288 | tf_op jit(solution)/shard_map/all_to_all | solution.py:228

commit v8 on v7

--- a/solution.py
+++ b/solution.py
@@ -101,8 +101,11 @@
         kv_ref[j] = total[256:384]
 
 
-def spread_tokens(in_ref, out_ref, sems):
-    copies = [pltpu.make_async_copy(in_ref, out_ref.at[y], sems.at[y]) for y in range(8)]
+def spread_tokens(in_ref, out_ref, held_ref, sems):
+    load = pltpu.make_async_copy(in_ref, held_ref, sems.at[8])
+    load.start()
+    load.wait()
+    copies = [pltpu.make_async_copy(held_ref, out_ref.at[y], sems.at[y]) for y in range(8)]
     for copy in copies:
         copy.start()
     for copy in copies:
@@ -259,7 +262,7 @@
         out_shape=shape(8, 64, 512),
         in_specs=[pl.BlockSpec(memory_space=pltpu.HBM)],
         out_specs=pl.BlockSpec(memory_space=pltpu.HBM),
-        scratch_shapes=[pltpu.SemaphoreType.DMA((8,))],
+        scratch_shapes=[pltpu.VMEM((64, 512), BF16), pltpu.SemaphoreType.DMA((9,))],
         compiler_params=pltpu.CompilerParams(vmem_limit_bytes=4 << 20),
     )(pltpu.with_memory_space_constraint(tokens.T, pltpu.HBM))
     own = trade(copies, "y").reshape(512, 512)

time: 148 us -> 148 us (level)
  no operation moved by 1% of the time
where the time goes in v8:
time: 148 us
  blocking collectives  78.7 us (53%)
  starting transfers between devices  40.9 us (28%)
  waiting for transfers between devices  16.9 us (11%)
  Pallas kernels  10.9 us (7%)
    all_to_all x4, blocking collectives, trade(): return lax.all_to_all(block, axis, split_axis=0, concat_axis=0, tiled=True)  62.1 us
    all_to_all x2, starting transfers between devices, trade(): return lax.all_to_all(block, axis, split_axis=0, concat_axis=0, tiled=True)  18 us
    all_gather x2, blocking collectives, gather(): return lax.all_gather(block, axis, axis=0, tiled=False)  16.6 us
    ppermute x2, starting transfers between devices, partner(): return lax.ppermute(block, 'c', [(0, 1), (1, 0)])  12.6 us
    ppermute x3, waiting for transfers between devices, send(): return lax.ppermute(block, 'x', [(i, (i + step) % 4) for i in range(4)])  11.4 us
    ppermute x3, starting transfers between devices, send(): return lax.ppermute(block, 'x', [(i, (i + step) % 4) for i in range(4)])  10.2 us
    pallas_call x7, Pallas kernels, call(): pl.pallas_call(body, out_shape=many, in_specs=specs, out_specs=[pl.BlockS...  7.34 us
    all_to_all x2, waiting for transfers between devices, trade(): return lax.all_to_all(block, axis, split_axis=0, concat_axis=0, tiled=True)  5.49 us
  transfers between devices with their start and end apart: 7, of which 4 were waited for; matrix products, arithmetic and copies ran while one was open for 0% of the time, Pallas kernels for 4%

profile of v8, /device:TPU:1, one launch (start us, length us, event | category | flops | bytes accessed | tf_op | source)
XLA Modules:
  0.0 147.6 jit_solution(5256058238201372489)
XLA Ops:
  0.0 1.6 %shard_map.65 = bf16[8,64,512]{2,1,0:T(8,128)(2,1)S(1)} custom-call(bf16[64,512]{1,0:T(8,128)(2,1)} %bitcast.11), custom_call_target="tpu_custom_call" | custom-call | tf_op jit(solution)/shard_map/pallas_call | solution.py:260
  1.6 0.0 copy-start
  1.6 0.0 copy-start.1
  1.6 19.8 %all_to_all.30 = bf16[8,64,512]{2,1,0:T(8,128)(2,1)S(1)} all-to-all(bf16[8,64,512]{2,1,0:T(8,128)(2,1)S(1)} %shard_map.65), channel_id=1, replica_groups=mesh['z'=12,'y'=8,'x'=4,'c'=2] {'y'}, dimensions={0} | all-to-all | bytes 1048576 | tf_op jit(solution)/shard_map/all_to_all | solution.py:231
  21.4 8.4 %collective-permute-start.3 = (bf16[512,512]{1,0:T(8,128)(2,1)S(1)}, bf16[512,512]{1,0:T(8,128)(2,1)S(1)}, u32[]{:S(2)}, u32[]{:S(2)}) collective-permute-start(bf16[512,512]{1,0:T(8,128)(2,1)S(1)} %bitcast.7), channel_id=1, source_target_pairs={{0,1},{1,0},{2,3},{3,2},{4,5},{5,4},{6,7},{7,6},{8,9},{9,8},{10,11... | collective-permute-start | bytes 1572872 | tf_op jit(solution)/shard_map/ppermute | solution.py:245
  29.9 0.9 shard_map.64
  30.8 2.8 %collective-permute-start = (bf16[160,1024]{1,0:T(8,128)(2,1)S(1)}, bf16[160,1024]{1,0:T(8,128)(2,1)S(1)}, u32[]{:S(2)}, u32[]{:S(2)}) collective-permute-start(bf16[160,1024]{1,0:T(8,128)(2,1)S(1)} %get-tuple-element.16), channel_id=1, source_target_pairs={{0,2},{2,4},{4,6},{6,0},{1,3},{3,5},{5,7},{7,1},{8,10},{10,12},{12... | collective-permute-start | bytes 983048 | tf_op jit(solution)/shard_map/ppermute | solution.py:241
  33.7 4.4 %collective-permute-start.1 = (bf16[160,1024]{1,0:T(8,128)(2,1)S(1)}, bf16[160,1024]{1,0:T(8,128)(2,1)S(1)}, u32[]{:S(2)}, u32[]{:S(2)}) collective-permute-start(bf16[160,1024]{1,0:T(8,128)(2,1)S(1)} %get-tuple-element.17), channel_id=1, source_target_pairs={{0,4},{2,6},{4,0},{6,2},{1,5},{3,7},{5,1},{7,3},{8,12},{10,14},{12... | collective-permute-start | bytes 983048 | tf_op jit(solution)/shard_map/ppermute | solution.py:241
  38.0 3.1 %collective-permute-start.2 = (bf16[160,1024]{1,0:T(8,128)(2,1)S(1)}, bf16[160,1024]{1,0:T(8,128)(2,1)S(1)}, u32[]{:S(2)}, u32[]{:S(2)}) collective-permute-start(bf16[160,1024]{1,0:T(8,128)(2,1)S(1)} %get-tuple-element.18), channel_id=1, source_target_pairs={{0,6},{2,0},{4,2},{6,4},{1,7},{3,1},{5,3},{7,5},{8,14},{10,8},{12,... | collective-permute-start | bytes 983048 | tf_op jit(solution)/shard_map/ppermute | solution.py:241
  41.1 2.1 %collective-permute-done.w1 = bf16[160,1024]{1,0:T(8,128)(2,1)S(1)} collective-permute-done((bf16[160,1024]{1,0:T(8,128)(2,1)S(1)}, bf16[160,1024]{1,0:T(8,128)(2,1)S(1)}, u32[]{:S(2)}, u32[]{:S(2)}) %collective-permute-start) | collective-permute-done | bytes 327712 | tf_op jit(solution)/shard_map/ppermute | solution.py:241
  43.2 7.7 %collective-permute-done.1.w2 = bf16[160,1024]{1,0:T(8,128)(2,1)S(1)} collective-permute-done((bf16[160,1024]{1,0:T(8,128)(2,1)S(1)}, bf16[160,1024]{1,0:T(8,128)(2,1)S(1)}, u32[]{:S(2)}, u32[]{:S(2)}) %collective-permute-start.1) | collective-permute-done | bytes 327712 | tf_op jit(solution)/shard_map/ppermute | solution.py:241
  50.9 1.6 %collective-permute-done.2.w3 = bf16[160,1024]{1,0:T(8,128)(2,1)S(1)} collective-permute-done((bf16[160,1024]{1,0:T(8,128)(2,1)S(1)}, bf16[160,1024]{1,0:T(8,128)(2,1)S(1)}, u32[]{:S(2)}, u32[]{:S(2)}) %collective-permute-start.2) | collective-permute-done | bytes 327712 | tf_op jit(solution)/shard_map/ppermute | solution.py:241
  52.5 0.0 collective-permute-done.3.other_ref
  52.5 1.3 shard_map.66
  53.8 11.2 %all_to_all.31.in_ref = bf16[4,384,128]{2,1,0:T(8,128)(2,1)S(1)} all-to-all(bf16[4,384,128]{2,1,0:T(8,128)(2,1)S(1)} %get-tuple-element.22), channel_id=1, replica_groups=mesh['z'=12,'y'=8,'x'=4,'c'=2] {'x'}, dimensions={0} | all-to-all | bytes 786432 | tf_op jit(solution)/shard_map/all_to_all | solution.py:231
  65.0 0.8 shard_map.68
  65.8 14.6 %all-to-all-start.2 = ((bf16[12,128,128]{2,1,0:T(8,128)(2,1)}), bf16[12,128,128]{2,1,0:T(8,128)(2,1)S(1)}, u32[]{:S(2)}, u32[]{:S(2)}) async-start(bf16[12,128,128]{2,1,0:T(8,128)(2,1)} %get-tuple-element.24), calls=%async_computation.2 | async-start | bytes 786432 | tf_op jit(solution)/shard_map/all_to_all | solution.py:231
  80.4 0.0 copy-done.4
  80.4 2.0 %shard_map.67 = (s32[1,256]{1,0:T(1,128)S(1)}, s32[2]{0:T(128)S(1)}) custom-call(s32[4]{0:T(128)S(1)} %compare_select_fusion.1.meta_ref, s32[48,128]{1,0:T(8,128)S(1)} %bitcast.10), custom_call_target="tpu_custom_call" | custom-call | tf_op jit(solution)/shard_map/pallas_call | solution.py:252
  82.4 4.2 %collective-permute-start.4 = (bf16[4,64,1024]{2,1,0:T(8,128)(2,1)S(1)}, bf16[4,64,1024]{2,1,0:T(8,128)(2,1)S(1)}, u32[]{:S(2)}, u32[]{:S(2)}) collective-permute-start(bf16[4,64,1024]{2,1,0:T(8,128)(2,1)S(1)} %get-tuple-element.19.own_ref), channel_id=1, source_target_pairs={{0,1},{1,0},{2,3},{3,2},{4,5},{5,4},{6,7},{7,6},{8,9},{9,8},{10,11... | collective-permute-start | bytes 1572872 | tf_op jit(solution)/shard_map/ppermute | solution.py:245
  86.6 13.0 %all-gather = bf16[2048,128]{1,0:T(8,128)(2,1)S(1)} all-gather(bf16[256,128]{1,0:T(8,128)(2,1)S(1)} %get-tuple-element.23), channel_id=2, replica_groups=mesh['z'=12,'y'=8,'x'=4,'c'=2] {'x','c'}, dimensions={0}, use_global_device_ids=true | all-gather | bytes 589824 | tf_op jit(solution)/shard_map/all_gather | solution.py:235
  99.6 0.0 all-to-all-done.2
  99.6 3.7 %all-gather.1 = bf16[24,128,128]{2,1,0:T(8,128)(2,1)S(1)} all-gather(bf16[12,128,128]{2,1,0:T(8,128)(2,1)S(1)} %all-to-all-done.2), channel_id=3, replica_groups=mesh['z'=12,'y'=8,'x'=4,'c'=2] {'c'}, dimensions={0}, use_global_device_ids=true | all-gather | bytes 1179648 | tf_op jit(solution)/shard_map/all_gather | solution.py:235
  103.2 1.8 %shard_map.69 = bf16[4,136,256]{2,1,0:T(8,128)(2,1)S(1)} custom-call(s32[4]{0:T(128)S(1)} %compare_select_fusion.1.meta_ref, s32[2]{0:T(128)S(1)} %get-tuple-element.20.first_ref, s32[1,256]{1,0:T(1,128)S(1)} %get-tuple-element.21.start_ref, bf16[8,256,128]{2,1,0:T(8,128)(2,1)S(1)} %bitcast.9, bf16[2,12,128,128]{3,2,1,0:T(8,128)(2,1)S(1)} %bitcast.6), custom_call_target="tpu_custom_call" | custom-call | tf_op jit(solution)/shard_map/pallas_call | solution.py:25
  105.0 8.9 %all_to_all.32.in_ref = bf16[4,136,256]{2,1,0:T(8,128)(2,1)S(1)} all-to-all(bf16[4,136,256]{2,1,0:T(8,128)(2,1)S(1)} %shard_map.69), channel_id=1, replica_groups=mesh['z'=12,'y'=8,'x'=4,'c'=2] {'x'}, dimensions={0} | all-to-all | bytes 557056 | tf_op jit(solution)/shard_map/all_to_all | solution.py:231
  113.9 0.8 shard_map.70
  114.7 3.4 %all-to-all-start.4 = ((bf16[4,128,256]{2,1,0:T(8,128)(2,1)}), bf16[4,128,256]{2,1,0:T(8,128)(2,1)S(1)}, u32[]{:S(2)}, u32[]{:S(2)}) async-start(bf16[4,128,256]{2,1,0:T(8,128)(2,1)} %shard_map.70), calls=%async_computation.4 | async-start | bytes 524288 | tf_op jit(solution)/shard_map/all_to_all | solution.py:231
  118.1 0.0 collective-permute-done.4.other_ref
  118.1 5.5 %all-to-all-done.4.a_ref = bf16[4,128,256]{2,1,0:T(8,128)(2,1)S(1)} async-done(((bf16[4,128,256]{2,1,0:T(8,128)(2,1)}), bf16[4,128,256]{2,1,0:T(8,128)(2,1)S(1)}, u32[]{:S(2)}, u32[]{:S(2)}) %all-to-all-start.4) | async-done | bytes 262176 | tf_op jit(solution)/shard_map/all_to_all | solution.py:231
  123.6 1.1 shard_map.71
  124.7 22.1 %all_to_all.33.in_ref = bf16[16,64,256]{2,1,0:T(8,128)(2,1)S(1)} all-to-all(bf16[16,64,256]{2,1,0:T(8,128)(2,1)S(1)} %shard_map.71), channel_id=1, replica_groups=mesh['z'=12,'y'=8,'x'=4,'c'=2] {'y','c'}, dimensions={0} | all-to-all | bytes 1048576 | tf_op jit(solution)/shard_map/all_to_all | solution.py:231
  146.9 0.7 shard_map.72
  (8 shorter events, 0.0 us)
Async XLA Ops:
  0.0 29.9 %copy-start.2 = (bf16[16,4096]{1,0:T(8,128)(2,1)S(1)}, bf16[16,4096]{1,0:T(8,128)(2,1)}, u32[]{:S(2)}) copy-start(bf16[16,4096]{1,0:T(8,128)(2,1)} %k_ref.1) | copy-start | bytes 393220
  0.0 29.9 %copy-start.3 = (bf16[16,4096]{1,0:T(8,128)(2,1)S(1)}, bf16[16,4096]{1,0:T(8,128)(2,1)}, u32[]{:S(2)}) copy-start(bf16[16,4096]{1,0:T(8,128)(2,1)} %v_ref.1) | copy-start | bytes 393220
  1.6 28.3 %copy-start = (bf16[64,4096]{1,0:T(8,128)(2,1)S(1)}, bf16[64,4096]{1,0:T(8,128)(2,1)}, u32[]{:S(2)}) copy-start(bf16[64,4096]{1,0:T(8,128)(2,1)} %q_ref.1) | copy-start | bytes 1572868
  1.6 28.3 %copy-start.1 = (bf16[64,4096]{1,0:T(8,128)(2,1)S(1)}, bf16[64,4096]{1,0:T(8,128)(2,1)}, u32[]{:S(2)}) copy-start(bf16[64,4096]{1,0:T(8,128)(2,1)} %o_ref.1) | copy-start | bytes 1572868
  21.4 31.0 %collective-permute-start.3 = (bf16[512,512]{1,0:T(8,128)(2,1)S(1)}, bf16[512,512]{1,0:T(8,128)(2,1)S(1)}, u32[]{:S(2)}, u32[]{:S(2)}) collective-permute-start(bf16[512,512]{1,0:T(8,128)(2,1)S(1)} %bitcast.7), channel_id=1, source_target_pairs={{0,1},{1,0},{2,3},{3,2},{4,5},{5,4},{6,7},{7,6},{8,9},{9,8},{10,11... | collective-permute-start | bytes 1572872 | tf_op jit(solution)/shard_map/ppermute | solution.py:245
  30.8 12.4 %collective-permute-start = (bf16[160,1024]{1,0:T(8,128)(2,1)S(1)}, bf16[160,1024]{1,0:T(8,128)(2,1)S(1)}, u32[]{:S(2)}, u32[]{:S(2)}) collective-permute-start(bf16[160,1024]{1,0:T(8,128)(2,1)S(1)} %get-tuple-element.16), channel_id=1, source_target_pairs={{0,2},{2,4},{4,6},{6,0},{1,3},{3,5},{5,7},{7,1},{8,10},{10,12},{12... | collective-permute-start | bytes 983048 | tf_op jit(solution)/shard_map/ppermute | solution.py:241
  33.7 17.2 %collective-permute-start.1 = (bf16[160,1024]{1,0:T(8,128)(2,1)S(1)}, bf16[160,1024]{1,0:T(8,128)(2,1)S(1)}, u32[]{:S(2)}, u32[]{:S(2)}) collective-permute-start(bf16[160,1024]{1,0:T(8,128)(2,1)S(1)} %get-tuple-element.17), channel_id=1, source_target_pairs={{0,4},{2,6},{4,0},{6,2},{1,5},{3,7},{5,1},{7,3},{8,12},{10,14},{12... | collective-permute-start | bytes 983048 | tf_op jit(solution)/shard_map/ppermute | solution.py:241
  38.0 14.4 %collective-permute-start.2 = (bf16[160,1024]{1,0:T(8,128)(2,1)S(1)}, bf16[160,1024]{1,0:T(8,128)(2,1)S(1)}, u32[]{:S(2)}, u32[]{:S(2)}) collective-permute-start(bf16[160,1024]{1,0:T(8,128)(2,1)S(1)} %get-tuple-element.18), channel_id=1, source_target_pairs={{0,6},{2,0},{4,2},{6,4},{1,7},{3,1},{5,3},{7,5},{8,14},{10,8},{12,... | collective-permute-start | bytes 983048 | tf_op jit(solution)/shard_map/ppermute | solution.py:241
  65.8 14.6 %copy-start.4 = (s32[6144]{0:T(1024)S(1)}, s32[6144]{0:T(1024)}, u32[]{:S(2)}) copy-start(s32[6144]{0:T(1024)} %param.11) | copy-start | bytes 73732
  65.8 33.8 %all-to-all-start.2 = ((bf16[12,128,128]{2,1,0:T(8,128)(2,1)}), bf16[12,128,128]{2,1,0:T(8,128)(2,1)S(1)}, u32[]{:S(2)}, u32[]{:S(2)}) async-start(bf16[12,128,128]{2,1,0:T(8,128)(2,1)} %get-tuple-element.24), calls=%async_computation.2 | async-start | bytes 786432 | tf_op jit(solution)/shard_map/all_to_all | solution.py:231
  82.4 35.8 %collective-permute-start.4 = (bf16[4,64,1024]{2,1,0:T(8,128)(2,1)S(1)}, bf16[4,64,1024]{2,1,0:T(8,128)(2,1)S(1)}, u32[]{:S(2)}, u32[]{:S(2)}) collective-permute-start(bf16[4,64,1024]{2,1,0:T(8,128)(2,1)S(1)} %get-tuple-element.19.own_ref), channel_id=1, source_target_pairs={{0,1},{1,0},{2,3},{3,2},{4,5},{5,4},{6,7},{7,6},{8,9},{9,8},{10,11... | collective-permute-start | bytes 1572872 | tf_op jit(solution)/shard_map/ppermute | solution.py:245
  114.7 8.9 %all-to-all-start.4 = ((bf16[4,128,256]{2,1,0:T(8,128)(2,1)}), bf16[4,128,256]{2,1,0:T(8,128)(2,1)S(1)}, u32[]{:S(2)}, u32[]{:S(2)}) async-start(bf16[4,128,256]{2,1,0:T(8,128)(2,1)} %shard_map.70), calls=%async_computation.4 | async-start | bytes 524288 | tf_op jit(solution)/shard_map/all_to_all | solution.py:231
